TPU v7x, 1024 devices: a whole 8x8x8 slice. The times are simulated.
1024 devices in a mesh: bulk: 128 (over x, y, z_hi), owner: 8 (over z_lo, core).
Axes of the slice: x: 8, y: 8, z: 8 (z_hi: 2, z_lo: 4; z = z_hi * 4 + z_lo), core: 2. Of those that a mesh axis runs over, the one named last changes fastest.
Arguments:
- slab_cols: float32 [4096, 8192], P('bulk', 'owner'), may hold values from -6 to 6
- pivots: int32 [8192], replicated, may hold values from 0 to 8191, each once
- lower_panels: bfloat16 [8192, 2048], P('bulk', 'owner'), may hold values from -0.125 to 0.125
- upper_rows: bfloat16 [4096, 2048], P('bulk', 'owner'), may hold values from -6 to 6
Outputs:
- updated: float32 [4096, 8192], P('bulk', 'owner')
All inputs are finite; a program needn't handle non-finite values.
Results may differ from a plain program's by a relative error of at most 0.0003.
Values may be sent and summed in bfloat16 or wider, within the bound.
No kernel may reach another device: no remote copies, remote signals or barrier semaphores. Data moves between devices by JAX's collectives and lax.ppermute only.
A program may use at most 32 MiB of HBM per device.

v0:
```python
import jax
import jax.numpy as jnp
from jax import lax
from jax.sharding import PartitionSpec as P


def pivoted(slab_cols, pivots, owner_index, row_block):
    gathered_slab = lax.all_gather(slab_cols, "owner", axis=1, tiled=True)
    local_pivots = lax.dynamic_slice_in_dim(pivots, owner_index * row_block, row_block)
    return jnp.take(gathered_slab, local_pivots, axis=1)


def shards(slab_cols, pivots, lower_panels, upper_rows):
    owners = lax.axis_size("owner")
    row_block = pivots.shape[0] // owners
    owner_index = lax.axis_index("owner")
    update = lax.dot_general(
        upper_rows,
        lax.all_gather(lower_panels, "bulk", axis=0, tiled=True),
        (((1,), (1,)), ((), ())),
        preferred_element_type=jnp.float32,
    )
    partial_value = -update
    summed = lax.psum_scatter(partial_value, "owner", scatter_dimension=1, tiled=True)
    result = pivoted(slab_cols, pivots, owner_index, row_block) + summed
    return result


def solution(mesh):
    in_specs = (P("bulk", "owner"), P(), P("bulk", "owner"), P("bulk", "owner"))
    out_specs = P("bulk", "owner")
    return jax.shard_map(shards, mesh=mesh, in_specs=in_specs, out_specs=out_specs, check_vma=False)
```

profile of v0, /device:TPU:4, one launch (start us, length us, event | category | flops | bytes accessed | tf_op | source)
XLA Modules:
  0.0 303.3 jit_solution(6144171006849584691)
XLA Ops:
  6.5 0.0 copy-start
  6.5 0.0 all-gather.5.cloned.1.call-start
  6.5 0.7 all-gather.5.cloned.1.call-update
  7.3 0.0 all-gather.3.cloned.1.call-start
  7.3 1.9 copy.5
  9.2 0.0 all-gather.3.cloned.1.call-update
  9.2 0.0 reduce-scatter.2.cloned.1.call-start
  9.3 184.2 %all-gather.5.cloned.1.call-done = bf16[8192,256]{1,0:T(8,128)(2,1)} async-done(((bf16[64,256]{1,0:T(8,128)(2,1)}), bf16[8192,256]{1,0:T(8,128)(2,1)}) %all-gather.5.cloned.1.call-update) | async-done | bytes 4194320 | tf_op jit(solution)/shard_map/all_gather | solution.py:19
  193.4 0.0 copy-done
  193.4 4.6 %convolution_negate_fusion = f32[32,8192]{1,0:T(8,128)} fusion(bf16[32,256]{1,0:T(8,128)(2,1)S(1)} %copy-done, bf16[8192,256]{1,0:T(8,128)(2,1)} %all-gather.5.cloned.1.call-done), kind=kOutput, calls=%fused_computation.1 | convolution fusion | flops 134479872 | bytes 5259264 | tf_op jit(solution)/shard_map/dot_general | solution.py:17
  198.0 0.0 reduce-scatter.2.cloned.1.call-update
  198.0 0.7 compare_and_fusion
  198.7 0.7 fusion
  199.4 49.0 %all-gather.3.cloned.1.call-done = f32[32,8192]{0,1:T(8,128)} async-done(((f32[32,1024]{0,1:T(8,128)}), f32[32,8192]{0,1:T(8,128)}) %all-gather.3.cloned.1.call-update) | async-done | bytes 1048592 | tf_op jit(solution)/shard_map/all_gather | solution.py:8
  248.4 5.0 %gather_fusion = f32[1024,32]{1,0:T(8,128)S(1)} fusion(f32[32,8192]{0,1:T(8,128)} %all-gather.3.cloned.1.call-done, s32[1024]{0:T(1024)S(1)} %fusion), kind=kCustom, calls=%fused_computation | custom fusion | bytes 266240 | tf_op jit(solution)/shard_map/jit(_take)/gather | solution.py:10
  253.4 0.2 copy.6
  253.6 41.6 %reduce-scatter.2.cloned.1.call-done = f32[32,1024]{1,0:T(8,128)} async-done(((f32[32,8192]{1,0:T(8,128)}), f32[32,1024]{1,0:T(8,128)}) %reduce-scatter.2.cloned.1.call-update) | async-done | bytes 131088 | tf_op jit(solution)/shard_map/reduce_scatter | solution.py:24
  295.2 1.6 bitcast_add_fusion
Async XLA Ops:
  6.5 186.9 %copy-start = (bf16[32,256]{1,0:T(8,128)(2,1)S(1)}, bf16[32,256]{1,0:T(8,128)(2,1)}, u32[]{:S(2)}) copy-start(bf16[32,256]{1,0:T(8,128)(2,1)} %param.7) | copy-start | bytes 49156
  6.5 186.9 %all-gather.5.cloned.1.call-start = ((), (), s32[]{:S(2)}) async-start(), calls=%async_computation.2 | async-start | bytes 4227072 | tf_op jit(solution)/shard_map/all_gather | solution.py:19
  7.3 241.2 %all-gather.3.cloned.1.call-start = ((), (), s32[]{:S(2)}) async-start(), calls=%async_computation.1 | async-start | bytes 4718592 | tf_op jit(solution)/shard_map/all_gather | solution.py:8
  9.2 285.9 %reduce-scatter.2.cloned.1.call-start = ((), (), s32[]{:S(2)}) async-start(), calls=%async_computation.3 | async-start | bytes 1179648 | tf_op jit(solution)/shard_map/reduce_scatter | solution.py:24
Sparse Core Ops, SparseCore 0:
  13.1 180.2 all-gather.4
  196.1 52.2 all-gather.2
  251.8 43.3 reduce-scatter.1
where the time goes:
time: 304 us; the launch traced here: 303 us
  waiting for transfers between devices  275 us (90%)
  between operations  13.1 us (4%)
  local copies, waits for them, and re-layouts  7.06 us (2%)
  matrix products  4.57 us (2%)
    all_gather x1, waiting for transfers between devices, shards(): lax.all_gather(lower_panels, 'bulk', axis=0, tiled=True)  184 us
    all_gather x1, waiting for transfers between devices, pivoted(): gathered_slab = lax.all_gather(slab_cols, 'owner', axis=1, tiled=True)  49 us
    reduce_scatter x1, waiting for transfers between devices, shards(): lax.psum_scatter(partial_value, 'owner', scatter_dimension=1, tiled=True)  41.6 us
  transfers between devices with their start and end apart: 3, of which 3 were waited for; matrix products, arithmetic and copies ran while one was open for 4% of the time, Pallas kernels for 0%

commit v1 on v0

v1 whole, which is shorter than its diff:
```python
import jax
import jax.numpy as jnp
from jax import lax
from jax.sharding import Mesh, PartitionSpec as P

BULK = ("x", "yh", "yl", "zh")
OWNER = ("zl", "c")
AXES = {"x": 8, "yh": 4, "yl": 2, "zh": 2, "zl": 4, "c": 2}


def gather(block, axes):
    members = lax.axis_size(axes)
    copies = jnp.broadcast_to(block[None], (members,) + block.shape)
    return lax.all_to_all(copies, axes, 0, 0, tiled=True)


def shards(slab_cols, pivots, lower_panels, upper_rows):
    owner_index = lax.axis_index(OWNER)
    row_block = slab_cols.shape[1]
    columns, inner = upper_rows.shape

    slab = lax.all_gather(slab_cols, OWNER, axis=1, tiled=True)

    upper = gather(upper_rows, ("yh", "zh")).reshape(-1, inner)
    lower = gather(lower_panels, ("x", "yl"))

    core = lax.axis_index("c")
    lower = lower.reshape(4, 2, -1, inner)

    def partial_value(parity):
        rows = lax.dynamic_index_in_dim(lower, parity, axis=1, keepdims=False)
        dots = [
            lax.dot_general(upper, rows[z], (((1,), (1,)), ((), ())), preferred_element_type=jnp.float32)
            for z in range(4)
        ]
        return jnp.stack(dots)

    kept = lax.ppermute(partial_value(1 - core), "c", [(0, 1), (1, 0)]) + partial_value(core)

    pieces = kept.reshape(32, columns, -1)
    pieces = lax.all_to_all(pieces, ("zl", "yh", "zh"), 0, 0, tiled=True)
    pieces = pieces.reshape(4, 4, 2, columns, 2, -1).sum(0)
    update = pieces.transpose(2, 0, 3, 1, 4).reshape(columns, row_block)

    local_pivots = lax.dynamic_slice_in_dim(pivots, owner_index * row_block, row_block)
    return jnp.take(slab, local_pivots, axis=1, mode="clip") - update


def solution(mesh):
    fine = Mesh(mesh.devices.reshape(tuple(AXES.values())), tuple(AXES))
    spec = P(BULK, OWNER)
    return jax.shard_map(
        shards, mesh=fine, in_specs=(spec, P(), spec, spec), out_specs=spec, check_vma=False
    )
```

time: 304 us -> 137 us (0.45)
  the two profiles are of different devices: /device:TPU:4 before, /device:TPU:16 now
where the time goes in v1:
time: 137 us; the launch traced here: 136 us
  waiting for transfers between devices  57.5 us (42%)
  blocking collectives  31.4 us (23%)
  starting transfers between devices  18.7 us (14%)
  between operations  13.6 us (10%)
  local copies, waits for them, and re-layouts  11.9 us (9%)
  other arithmetic  1.63 us (1%)
  matrix products  1.54 us (1%)
    all_gather x1, waiting for transfers between devices, shards(): slab = lax.all_gather(slab_cols, OWNER, axis=1, tiled=True)  44.1 us
    all_to_all x1, blocking collectives, gather(): return lax.all_to_all(copies, axes, 0, 0, tiled=True)  31.4 us
    all_to_all x1, waiting for transfers between devices, gather(): return lax.all_to_all(copies, axes, 0, 0, tiled=True)  12.3 us
    all_to_all x1, starting transfers between devices, shards(): pieces = lax.all_to_all(pieces, ('zl', 'yh', 'zh'), 0, 0, tiled=True)  8.54 us
    all_to_all x1, starting transfers between devices, gather(): return lax.all_to_all(copies, axes, 0, 0, tiled=True)  8.23 us
    gather x1, local copies, waits for them, and re-layouts, shards(): return jnp.take(slab, local_pivots, axis=1, mode='clip') - update  4.99 us
  transfers between devices with their start and end apart: 4, of which 3 were waited for; matrix products, arithmetic and copies ran while one was open for 8% of the time, Pallas kernels for 0%

profile of v1, /device:TPU:16, one launch (start us, length us, event | category | flops | bytes accessed | tf_op | source)
XLA Modules:
  0.0 136.2 jit_solution(11430091525504248915)
XLA Ops:
  6.5 0.7 broadcast_in_dim.18
  7.3 31.4 %all_to_all.15 = bf16[8,32,256]{2,1,0:T(8,128)(2,1)S(1)} all-to-all(bf16[8,32,256]{2,1,0:T(8,128)(2,1)S(1)} %broadcast_in_dim.18), channel_id=1, replica_groups=mesh['x'=8,'yh'=4,'yl'=2,'zh'=2,'zl'=4,'c'=2] {'yh','zh'}, dimensions={0} | all-to-all | bytes 262144 | tf_op jit(solution)/shard_map/all_to_all | solution.py:14
  38.6 1.6 %broadcast_in_dim.8 = bf16[16,64,256]{2,1,0:T(8,128)(2,1)} broadcast(bf16[64,256]{1,0:T(8,128)(2,1)} %param.6), dimensions={1,2} | broadcast | bytes 557056 | tf_op jit(solution)/shard_map/broadcast_in_dim | solution.py:13
  40.2 8.2 %all-to-all-start = ((bf16[16,64,256]{2,1,0:T(8,128)(2,1)}), bf16[16,64,256]{2,1,0:T(8,128)(2,1)S(1)}, u32[]{:S(2)}, u32[]{:S(2)}) async-start(bf16[16,64,256]{2,1,0:T(8,128)(2,1)} %broadcast_in_dim.8), calls=%async_computation | async-start | bytes 1048576 | tf_op jit(solution)/shard_map/all_to_all | solution.py:14
  48.5 1.9 %copy.10 = f32[32,1024]{0,1:T(8,128)} copy(f32[32,1024]{1,0:T(8,128)} %param.4) | data formatting | bytes 262144 | tf_op args[0]
  50.5 12.3 %all-to-all-done = bf16[16,64,256]{2,1,0:T(8,128)(2,1)S(1)} async-done(((bf16[16,64,256]{2,1,0:T(8,128)(2,1)}), bf16[16,64,256]{2,1,0:T(8,128)(2,1)S(1)}, u32[]{:S(2)}, u32[]{:S(2)}) %all-to-all-start) | async-done | bytes 524320 | tf_op jit(solution)/shard_map/all_to_all | solution.py:14
  63.0 0.2 convolution_bitcast_fusion.5
  63.2 0.2 convolution_bitcast_fusion.6
  63.4 0.2 convolution_bitcast_fusion.4
  63.6 1.9 %collective-permute-start = (f32[4,256,128]{1,2,0:T(8,128)S(1)}, f32[4,256,128]{1,2,0:T(8,128)S(1)}, u32[]{:S(2)}, u32[]{:S(2)}) collective-permute-start(f32[4,256,128]{1,2,0:T(8,128)S(1)} %pad_maximum_fusion), channel_id=1, source_target_pairs={{0,1},{1,0},{2,3},{3,2},{4,5},{5,4},{6,7},{7,6},{8,9},{9,8},{10,11... | collective-permute-start | bytes 1572872 | tf_op jit(solution)/shard_map/ppermute | solution.py:38
  65.6 0.2 convolution_bitcast_fusion.1
  65.8 0.2 convolution_bitcast_fusion.2
  66.0 0.2 convolution_bitcast_fusion.3
  66.2 0.2 convolution_bitcast_fusion
  66.4 1.1 collective-permute-done
  67.5 1.0 copy.11
  68.5 8.5 %all-to-all-start.2 = ((f32[32,32,128]{2,1,0:T(8,128)}), f32[32,32,128]{2,1,0:T(8,128)S(1)}, u32[]{:S(2)}, u32[]{:S(2)}) async-start(f32[32,32,128]{2,1,0:T(8,128)} %bitcast.27), calls=%async_computation.2 | async-start | bytes 1048576 | tf_op jit(solution)/shard_map/all_to_all | solution.py:41
  77.1 0.7 dynamic-slice_clamp_fusion
  77.8 44.1 %all-gather.2.cloned.1.call-done = f32[32,8192]{0,1:T(8,128)} async-done(((f32[32,1024]{0,1:T(8,128)}), f32[32,8192]{0,1:T(8,128)}) %all-gather.2.cloned.1.call-update) | async-done | bytes 1048592 | tf_op jit(solution)/shard_map/all_gather | solution.py:22
  121.9 5.0 %gather_fusion = f32[1024,32]{1,0:T(8,128)S(1)} fusion(f32[32,8192]{0,1:T(8,128)} %all-gather.2.cloned.1.call-done, s32[1024]{0:T(1024)S(1)} %dynamic-slice_clamp_fusion), kind=kCustom, calls=%fused_computation | custom fusion | bytes 266240 | tf_op jit(solution)/shard_map/jit(_take)/gather | solution.py:46
  126.9 0.6 reshape.36
  127.5 0.8 reduce_sum.9
  128.3 0.2 copy.12
  128.5 0.8 copy.13
  (7 shorter events, 0.4 us)
Async XLA Ops:
  40.2 22.6 %all-to-all-start = ((bf16[16,64,256]{2,1,0:T(8,128)(2,1)}), bf16[16,64,256]{2,1,0:T(8,128)(2,1)S(1)}, u32[]{:S(2)}, u32[]{:S(2)}) async-start(bf16[16,64,256]{2,1,0:T(8,128)(2,1)} %broadcast_in_dim.8), calls=%async_computation | async-start | bytes 1048576 | tf_op jit(solution)/shard_map/all_to_all | solution.py:14
  48.5 73.4 %all-gather.2.cloned.1.call-start = ((), (), s32[]{:S(2)}) async-start(), calls=%async_computation.3 | async-start | bytes 4718592 | tf_op jit(solution)/shard_map/all_gather | solution.py:22
  63.6 3.8 %collective-permute-start = (f32[4,256,128]{1,2,0:T(8,128)S(1)}, f32[4,256,128]{1,2,0:T(8,128)S(1)}, u32[]{:S(2)}, u32[]{:S(2)}) collective-permute-start(f32[4,256,128]{1,2,0:T(8,128)S(1)} %pad_maximum_fusion), channel_id=1, source_target_pairs={{0,1},{1,0},{2,3},{3,2},{4,5},{5,4},{6,7},{7,6},{8,9},{9,8},{10,11... | collective-permute-start | bytes 1572872 | tf_op jit(solution)/shard_map/ppermute | solution.py:38
  68.5 58.3 %all-to-all-start.2 = ((f32[32,32,128]{2,1,0:T(8,128)}), f32[32,32,128]{2,1,0:T(8,128)S(1)}, u32[]{:S(2)}, u32[]{:S(2)}) async-start(f32[32,32,128]{2,1,0:T(8,128)} %bitcast.27), calls=%async_computation.2 | async-start | bytes 1048576 | tf_op jit(solution)/shard_map/all_to_all | solution.py:41
Sparse Core Ops, SparseCore 0:
  51.9 69.8 all-gather.1

commit v2 on v1

v2 whole, which is shorter than its diff:
```python
import jax
import jax.numpy as jnp
from jax import lax
from jax.experimental import pallas as pl
from jax.experimental.pallas import tpu as pltpu
from jax.sharding import Mesh, PartitionSpec as P


BULK = ("x", "yh", "yl", "zh")
OWNER = ("zl", "c")
AXES = {"x": 8, "yh": 4, "yl": 2, "zh": 2, "zl": 4, "c": 2}
SWAP = [(0, 1), (1, 0)]
VMEM = pl.BlockSpec(memory_space=pltpu.VMEM)
SMEM = pl.BlockSpec(memory_space=pltpu.SMEM)


def gather(block, axes):
    members = lax.axis_size(axes)
    copies = jnp.broadcast_to(block[None], (members,) + block.shape)
    return lax.all_to_all(copies, axes, 0, 0, tiled=True)


def product(parity_ref, upper_ref, lower_ref, out_ref):
    upper = upper_ref[...]
    for z in range(4):
        out_ref[z] = lax.dot_general(
            upper, lower_ref[2 * z + parity_ref[0]], (((1,), (1,)), ((), ())), preferred_element_type=jnp.float32
        )


def permute(place_ref, pivots_ref, own_ref, other_ref, out_ref):
    owner, core = place_ref[0], place_ref[1]

    def block(b, _):
        index = pivots_ref[pl.ds(owner * 8 + b, 1), :]
        side = ((index >> 10) & 1) ^ core
        key = jnp.broadcast_to(side * 32 + (index >> 11) * 8 + ((index >> 7) & 7), (32, 128))
        lane = jnp.broadcast_to(index & 127, (32, 128))
        found = jnp.zeros((32, 128), jnp.float32)
        for k in range(64):
            ref = own_ref if k < 32 else other_ref
            source = ref[(k % 32) // 8, :, (k % 8) * 128 : (k % 8 + 1) * 128]
            found = jnp.where(key == k, jnp.take_along_axis(source, lane, axis=1, mode="promise_in_bounds"), found)
        out_ref[:, pl.ds(pl.multiple_of(b * 128, 128), 128)] = found
        return 0

    lax.fori_loop(0, 8, block, 0)


def finish(pieces_ref, permuted_ref, out_ref):
    low = lax.broadcasted_iota(jnp.int32, (32, 128), 1) < 64
    for yh in range(4):
        first, second = (sum(pieces_ref[zl * 8 + yh * 2 + zh] for zl in range(4)) for zh in range(2))
        blocks = (
            jnp.where(low, first, pltpu.roll(second, 64, 1)),
            jnp.where(low, pltpu.roll(first, 64, 1), second),
        )
        for yl in range(2):
            at = slice((yh * 2 + yl) * 128, (yh * 2 + yl + 1) * 128)
            out_ref[:, at] = permuted_ref[:, at] - blocks[yl]


def shards(slab_cols, pivots, lower_panels, upper_rows):
    core = lax.axis_index("c")
    columns, row_block = slab_cols.shape
    inner = upper_rows.shape[1]

    upper = gather(upper_rows, ("yh", "zh")).reshape(-1, inner)
    lower = gather(lower_panels, ("x", "yl")).reshape(8, -1, inner)

    own = lax.all_gather(slab_cols, "zl", axis=0)
    other = lax.ppermute(own, "c", SWAP)

    def partial_value(parity):
        return pl.pallas_call(
            product,
            out_shape=jax.ShapeDtypeStruct((4, upper.shape[0], lower.shape[1]), jnp.float32),
            in_specs=[SMEM, VMEM, VMEM],
            out_specs=VMEM,
            name="product",
        )(parity.reshape(1), upper, lower)

    kept = lax.ppermute(partial_value(1 - core), "c", SWAP) + partial_value(core)

    pieces = lax.all_to_all(kept.reshape(32, columns, -1), ("zl", "yh", "zh"), 0, 0, tiled=True)

    permuted = pl.pallas_call(
        permute,
        out_shape=jax.ShapeDtypeStruct((columns, row_block), jnp.float32),
        in_specs=[SMEM, VMEM, VMEM, VMEM],
        out_specs=VMEM,
        name="permute",
    )(jnp.stack([lax.axis_index(OWNER), core]), pivots.reshape(-1, 128), own, other)
    return pl.pallas_call(
        finish,
        out_shape=jax.ShapeDtypeStruct((columns, row_block), jnp.float32),
        in_specs=[VMEM, VMEM],
        out_specs=VMEM,
        name="finish",
    )(pieces, permuted)


def solution(mesh):
    fine = Mesh(mesh.devices.reshape(tuple(AXES.values())), tuple(AXES))
    spec = P(BULK, OWNER)

    return jax.shard_map(shards, mesh=fine, in_specs=(spec, P(), spec, spec), out_specs=spec, check_vma=False)
```

time: 137 us -> 114 us (0.83)
  the two profiles are of different devices: /device:TPU:16 before, /device:TPU:1 now
where the time goes in v2:
time: 114 us
  blocking collectives  56 us (49%)
  starting transfers between devices  24.9 us (22%)
  waiting for transfers between devices  15.3 us (13%)
  Pallas kernels  10.9 us (10%)
  local copies, waits for them, and re-layouts  3.93 us (3%)
  other arithmetic  2.57 us (2%)
    all_to_all x1, blocking collectives, gather(): return lax.all_to_all(copies, axes, 0, 0, tiled=True)  31.7 us
    all_gather x1, blocking collectives, shards(): own = lax.all_gather(slab_cols, 'zl', axis=0)  24.2 us
    all_to_all x1, waiting for transfers between devices, gather(): return lax.all_to_all(copies, axes, 0, 0, tiled=True)  14.5 us
    all_to_all x1, starting transfers between devices, shards(): lax.all_to_all(kept.reshape(32, columns, -1), ('zl', 'yh', 'zh'), 0, 0, t...  8.4 us
    all_to_all x1, starting transfers between devices, gather(): return lax.all_to_all(copies, axes, 0, 0, tiled=True)  6.92 us
    ppermute x1, starting transfers between devices, shards(): lax.ppermute(partial_value(1 - core), 'c', SWAP) + partial_value(core)  6.01 us
    pallas_call x1, Pallas kernels, shards(): pl.pallas_call(permute, out_shape=jax.ShapeDtypeStruct((columns, row_bloc...  4.65 us
    pallas_call x2, Pallas kernels, partial_value(): pl.pallas_call(product, out_shape=jax.ShapeDtypeStruct((4, upper.shape[0]...  4.42 us
  transfers between devices with their start and end apart: 4, of which 2 were waited for; matrix products, arithmetic and copies ran while one was open for 1% of the time, Pallas kernels for 6%

profile of v2, /device:TPU:1, one launch (start us, length us, event | category | flops | bytes accessed | tf_op | source)
XLA Modules:
  0.0 113.7 jit_solution(5048340986554743626)
XLA Ops:
  0.0 0.7 broadcast_in_dim.4
  0.7 0.0 copy-start.5
  0.7 31.7 %all_to_all.15 = bf16[8,32,256]{2,1,0:T(8,128)(2,1)} all-to-all(bf16[8,32,256]{2,1,0:T(8,128)(2,1)S(1)} %broadcast_in_dim.4), channel_id=1, replica_groups=mesh['x'=8,'yh'=4,'yl'=2,'zh'=2,'zl'=4,'c'=2] {'yh','zh'}, dimensions={0} | all-to-all | bytes 262144 | tf_op jit(solution)/shard_map/all_to_all | solution.py:20
  32.5 0.0 copy-done.5
  32.5 0.8 broadcast_in_dim.5
  33.3 6.9 %all-to-all-start.1 = ((bf16[16,64,256]{2,1,0:T(8,128)(2,1)}), bf16[16,64,256]{2,1,0:T(8,128)(2,1)S(1)}, u32[]{:S(2)}, u32[]{:S(2)}) async-start(bf16[16,64,256]{2,1,0:T(8,128)(2,1)} %broadcast_in_dim.5), calls=%async_computation.1 | async-start | bytes 1048576 | tf_op jit(solution)/shard_map/all_to_all | solution.py:20
  40.3 14.5 %all-to-all-done.1 = bf16[16,64,256]{2,1,0:T(8,128)(2,1)S(1)} async-done(((bf16[16,64,256]{2,1,0:T(8,128)(2,1)}), bf16[16,64,256]{2,1,0:T(8,128)(2,1)S(1)}, u32[]{:S(2)}, u32[]{:S(2)}) %all-to-all-start.1) | async-done | bytes 524320 | tf_op jit(solution)/shard_map/all_to_all | solution.py:20
  54.7 0.8 copy-done
  55.5 2.2 %product.2 = f32[4,256,128]{2,1,0:T(8,128)} custom-call(s32[1]{0:T(128)} %bitcast.parity_ref, bf16[256,256]{1,0:T(8,128)(2,1)} %bitcast.12, bf16[8,128,256]{2,1,0:T(8,128)(2,1)} %bitcast.8), custom_call_target="tpu_custom_call" | custom-call | tf_op jit(solution)/shard_map/product/pallas_call | solution.py:75
  57.7 6.0 %collective-permute-start = (f32[4,256,128]{2,1,0:T(8,128)}, f32[4,256,128]{2,1,0:T(8,128)S(1)}, u32[]{:S(2)}, u32[]{:S(2)}) collective-permute-start(f32[4,256,128]{2,1,0:T(8,128)} %product.2), channel_id=1, source_target_pairs={{0,1},{1,0},{2,3},{3,2},{4,5},{5,4},{6,7},{7,6},{8,9},{9,8},{10,11... | collective-permute-start | bytes 1572872 | tf_op jit(solution)/shard_map/ppermute | solution.py:83
  63.7 2.2 %product.3 = f32[4,256,128]{2,1,0:T(8,128)} custom-call(s32[1]{0:T(128)} %bitcast.3.parity_ref, bf16[256,256]{1,0:T(8,128)(2,1)} %bitcast.13, bf16[8,128,256]{2,1,0:T(8,128)(2,1)} %bitcast.9), custom_call_target="tpu_custom_call" | custom-call | tf_op jit(solution)/shard_map/product/pallas_call | solution.py:75
  66.0 0.0 collective-permute-done
  66.0 1.9 %add.6 = f32[4,256,128]{2,1,0:T(8,128)} add(f32[4,256,128]{2,1,0:T(8,128)S(1)} %collective-permute-done, f32[4,256,128]{2,1,0:T(8,128)} %product.3) | non-fusion elementwise | flops 131072 | bytes 1572864 | tf_op jit(solution)/shard_map/add | solution.py:83
  67.9 8.4 %all-to-all-start.2 = ((f32[32,32,128]{2,1,0:T(8,128)}), f32[32,32,128]{2,1,0:T(8,128)S(1)}, u32[]{:S(2)}, u32[]{:S(2)}) async-start(f32[32,32,128]{2,1,0:T(8,128)} %bitcast.4), calls=%async_computation.2 | async-start | bytes 1048576 | tf_op jit(solution)/shard_map/all_to_all | solution.py:85
  76.3 24.2 %all-gather = f32[128,1024]{1,0:T(8,128)S(1)} all-gather(f32[32,1024]{1,0:T(8,128)S(1)} %copy-done.4), channel_id=2, replica_groups=mesh['x'=8,'yh'=4,'yl'=2,'zh'=2,'zl'=4,'c'=2] {'zl'}, dimensions={0}, use_global_device_ids=true | all-gather | bytes 655360 | tf_op jit(solution)/shard_map/all_gather | solution.py:71
  100.5 3.6 %collective-permute-start.1 = (f32[4,32,1024]{2,1,0:T(8,128)S(1)}, f32[4,32,1024]{2,1,0:T(8,128)S(1)}, u32[]{:S(2)}, u32[]{:S(2)}) collective-permute-start(f32[4,32,1024]{2,1,0:T(8,128)S(1)} %bitcast.10), channel_id=1, source_target_pairs={{0,1},{1,0},{2,3},{3,2},{4,5},{5,4},{6,7},{7,6},{8,9},{9,8},{10,11... | collective-permute-start | bytes 1572872 | tf_op jit(solution)/shard_map/ppermute | solution.py:72
  104.1 0.7 pad_add_fusion.place_ref
  104.8 0.9 collective-permute-done.1.other_ref
  105.7 0.0 copy-done.1
  105.7 0.8 copy-done.3
  106.4 4.7 %permute.1.permuted_ref = f32[32,1024]{1,0:T(8,128)} custom-call(s32[2]{0:T(128)} %pad_add_fusion.place_ref, s32[64,128]{1,0:T(8,128)} %bitcast.14, f32[4,32,1024]{2,1,0:T(8,128)} %bitcast.11, f32[4,32,1024]{2,1,0:T(8,128)} %copy-done.3), custom_call_target="tpu_custom_call" | custom-call | tf_op jit(solution)/shard_map/permute/pallas_call | solution.py:87
  111.1 0.0 all-to-all-done.2.pieces_ref
  111.1 0.8 copy-done.2
  111.9 1.8 %finish.1 = f32[32,1024]{1,0:T(8,128)} custom-call(f32[32,32,128]{2,1,0:T(8,128)} %copy-done.2, f32[32,1024]{1,0:T(8,128)} %permute.1.permuted_ref), custom_call_target="tpu_custom_call" | custom-call | tf_op jit(solution)/shard_map/finish/pallas_call | solution.py:94
  (6 shorter events, 0.0 us)
Async XLA Ops:
  0.7 31.8 %copy-start.5 = (bf16[64,256]{1,0:T(8,128)(2,1)S(1)}, bf16[64,256]{1,0:T(8,128)(2,1)}, u32[]{:S(2)}) copy-start(bf16[64,256]{1,0:T(8,128)(2,1)} %param.6) | copy-start | bytes 98308
  33.3 21.4 %all-to-all-start.1 = ((bf16[16,64,256]{2,1,0:T(8,128)(2,1)}), bf16[16,64,256]{2,1,0:T(8,128)(2,1)S(1)}, u32[]{:S(2)}, u32[]{:S(2)}) async-start(bf16[16,64,256]{2,1,0:T(8,128)(2,1)} %broadcast_in_dim.5), calls=%async_computation.1 | async-start | bytes 1048576 | tf_op jit(solution)/shard_map/all_to_all | solution.py:20
  54.7 0.8 copy-start
  57.7 8.2 %collective-permute-start = (f32[4,256,128]{2,1,0:T(8,128)}, f32[4,256,128]{2,1,0:T(8,128)S(1)}, u32[]{:S(2)}, u32[]{:S(2)}) collective-permute-start(f32[4,256,128]{2,1,0:T(8,128)} %product.2), channel_id=1, source_target_pairs={{0,1},{1,0},{2,3},{3,2},{4,5},{5,4},{6,7},{7,6},{8,9},{9,8},{10,11... | collective-permute-start | bytes 1572872 | tf_op jit(solution)/shard_map/ppermute | solution.py:83
  67.9 8.4 %copy-start.4 = (f32[32,1024]{1,0:T(8,128)S(1)}, f32[32,1024]{1,0:T(8,128)}, u32[]{:S(2)}) copy-start(f32[32,1024]{1,0:T(8,128)} %param.4) | copy-start | bytes 393220
  67.9 43.2 %all-to-all-start.2 = ((f32[32,32,128]{2,1,0:T(8,128)}), f32[32,32,128]{2,1,0:T(8,128)S(1)}, u32[]{:S(2)}, u32[]{:S(2)}) async-start(f32[32,32,128]{2,1,0:T(8,128)} %bitcast.4), calls=%async_computation.2 | async-start | bytes 1048576 | tf_op jit(solution)/shard_map/all_to_all | solution.py:85
  100.5 5.1 %copy-start.1 = (f32[128,1024]{1,0:T(8,128)}, f32[128,1024]{1,0:T(8,128)S(1)}, u32[]{:S(2)}) copy-start(f32[128,1024]{1,0:T(8,128)S(1)} %all-gather) | copy-start | bytes 1572868
  100.5 5.1 %collective-permute-start.1 = (f32[4,32,1024]{2,1,0:T(8,128)S(1)}, f32[4,32,1024]{2,1,0:T(8,128)S(1)}, u32[]{:S(2)}, u32[]{:S(2)}) collective-permute-start(f32[4,32,1024]{2,1,0:T(8,128)S(1)} %bitcast.10), channel_id=1, source_target_pairs={{0,1},{1,0},{2,3},{3,2},{4,5},{5,4},{6,7},{7,6},{8,9},{9,8},{10,11... | collective-permute-start | bytes 1572872 | tf_op jit(solution)/shard_map/ppermute | solution.py:72
  105.7 0.8 copy-start.3
  111.1 0.8 copy-start.2

commit v3 on v2

--- a/solution.py
+++ b/solution.py
@@ -14,6 +14,16 @@
 SMEM = pl.BlockSpec(memory_space=pltpu.SMEM)
 
 
+def kernel(body, scalars, arrays, out, vmem_out=True):
+    arrays = [pltpu.with_memory_space_constraint(a, pltpu.VMEM) for a in arrays]
+    return pl.pallas_call(
+        body,
+        out_shape=pltpu.VMEM(out, jnp.float32) if vmem_out else jax.ShapeDtypeStruct(out, jnp.float32),
+        in_specs=[SMEM] * len(scalars) + [VMEM] * len(arrays),
+        out_specs=VMEM,
+    )(*scalars, *arrays)
+
+
 def gather(block, axes):
     members = lax.axis_size(axes)
     copies = jnp.broadcast_to(block[None], (members,) + block.shape)
@@ -26,6 +36,10 @@
         out_ref[z] = lax.dot_general(
             upper, lower_ref[2 * z + parity_ref[0]], (((1,), (1,)), ((), ())), preferred_element_type=jnp.float32
         )
+
+
+def add(left_ref, right_ref, out_ref):
+    out_ref[...] = left_ref[...] + right_ref[...]
 
 
 def permute(place_ref, pivots_ref, own_ref, other_ref, out_ref):
@@ -72,32 +86,18 @@
     other = lax.ppermute(own, "c", SWAP)
 
     def partial_value(parity):
-        return pl.pallas_call(
-            product,
-            out_shape=jax.ShapeDtypeStruct((4, upper.shape[0], lower.shape[1]), jnp.float32),
-            in_specs=[SMEM, VMEM, VMEM],
-            out_specs=VMEM,
-            name="product",
-        )(parity.reshape(1), upper, lower)
+        out = (4, upper.shape[0], lower.shape[1])
+        return kernel(product, [parity.reshape(1)], [upper, lower], out)
 
-    kept = lax.ppermute(partial_value(1 - core), "c", SWAP) + partial_value(core)
+    received = lax.ppermute(partial_value(1 - core), "c", SWAP)
+    kept = partial_value(core)
+    kept = kernel(add, [], [received, kept], kept.shape)
 
     pieces = lax.all_to_all(kept.reshape(32, columns, -1), ("zl", "yh", "zh"), 0, 0, tiled=True)
 
-    permuted = pl.pallas_call(
-        permute,
-        out_shape=jax.ShapeDtypeStruct((columns, row_block), jnp.float32),
-        in_specs=[SMEM, VMEM, VMEM, VMEM],
-        out_specs=VMEM,
-        name="permute",
-    )(jnp.stack([lax.axis_index(OWNER), core]), pivots.reshape(-1, 128), own, other)
-    return pl.pallas_call(
-        finish,
-        out_shape=jax.ShapeDtypeStruct((columns, row_block), jnp.float32),
-        in_specs=[VMEM, VMEM],
-        out_specs=VMEM,
-        name="finish",
-    )(pieces, permuted)
+    place = jnp.stack([lax.axis_index(OWNER), core])
+    permuted = kernel(permute, [place], [pivots.reshape(-1, 128), own, other], (columns, row_block))
+    return kernel(finish, [], [pieces, permuted], (columns, row_block), vmem_out=False)
 
 
 def solution(mesh):

time: 114 us -> 106 us (0.930)
  Pallas kernels: 10.9 us -> 5.63 us
  local copies, waits for them, and re-layouts: 3.93 us -> 1.6 us
  other arithmetic: 2.57 us -> 0.61 us
  waiting for transfers between devices: 15.3 us -> 16.6 us
    pallas_call x4 -> x5, Pallas kernels: 10.9 us -> 5.63 us  [kernel(): pl.pallas_call(body, out_shape=pltpu.VMEM(out, jnp.float32) if vmem_out e...]
    unnamed x12 -> x6, local copies, waits for them, and re-layouts: 2.37 us -> 0.02 us
    add x1 -> x0, other arithmetic: 1.91 us -> none  [shards(): lax.ppermute(partial_value(1 - core), 'c', SWAP) + partial_value(core)]
    ppermute x1, waiting for transfers between devices: 0.01 us -> 1.22 us  [shards(): received = lax.ppermute(partial_value(1 - core), 'c', SWAP)]
  transfers between devices with their start and end apart: 4 -> 4, of which waited for: 2 -> 3; matrix products, arithmetic and copies ran while one was open for 1% -> 1% of each run, Pallas kernels for 6% -> 4%
where the time goes in v3:
time: 106 us; the launch traced here: 105 us
  blocking collectives  55.2 us (52%)
  starting transfers between devices  25.6 us (24%)
  waiting for transfers between devices  16.6 us (16%)
  Pallas kernels  5.63 us (5%)
  local copies, waits for them, and re-layouts  1.6 us (2%)
    all_to_all x1, blocking collectives, gather(): return lax.all_to_all(copies, axes, 0, 0, tiled=True)  31.6 us
    all_gather x1, blocking collectives, shards(): own = lax.all_gather(slab_cols, 'zl', axis=0)  23.6 us
    all_to_all x1, waiting for transfers between devices, gather(): return lax.all_to_all(copies, axes, 0, 0, tiled=True)  14.5 us
    all_to_all x1, starting transfers between devices, shards(): lax.all_to_all(kept.reshape(32, columns, -1), ('zl', 'yh', 'zh'), 0, 0, t...  8.4 us
    all_to_all x1, starting transfers between devices, gather(): return lax.all_to_all(copies, axes, 0, 0, tiled=True)  6.92 us
    ppermute x1, starting transfers between devices, shards(): received = lax.ppermute(partial_value(1 - core), 'c', SWAP)  6.02 us
    pallas_call x5, Pallas kernels, kernel(): pl.pallas_call(body, out_shape=pltpu.VMEM(out, jnp.float32) if vmem_out e...  5.63 us
    ppermute x1, starting transfers between devices, shards(): other = lax.ppermute(own, 'c', SWAP)  4.3 us
  transfers between devices with their start and end apart: 4, of which 3 were waited for; matrix products, arithmetic and copies ran while one was open for 1% of the time, Pallas kernels for 4%

profile of v3, /device:TPU:1, one launch (start us, length us, event | category | flops | bytes accessed | tf_op | source)
XLA Modules:
  0.0 105.4 jit_solution(17740581317388617815)
XLA Ops:
  0.0 0.7 broadcast_in_dim.4
  0.7 0.0 copy-start.2
  0.7 31.6 %all_to_all.15 = bf16[8,32,256]{2,1,0:T(8,128)(2,1)S(1)} all-to-all(bf16[8,32,256]{2,1,0:T(8,128)(2,1)S(1)} %broadcast_in_dim.4), channel_id=1, replica_groups=mesh['x'=8,'yh'=4,'yl'=2,'zh'=2,'zl'=4,'c'=2] {'yh','zh'}, dimensions={0} | all-to-all | bytes 262144 | tf_op jit(solution)/shard_map/all_to_all | solution.py:30
  32.4 0.0 copy-done.2
  32.4 0.9 broadcast_in_dim.5
  33.2 6.9 %all-to-all-start.1 = ((bf16[16,64,256]{2,1,0:T(8,128)(2,1)}), bf16[16,64,256]{2,1,0:T(8,128)(2,1)S(1)}, u32[]{:S(2)}, u32[]{:S(2)}) async-start(bf16[16,64,256]{2,1,0:T(8,128)(2,1)} %broadcast_in_dim.5), calls=%async_computation.1 | async-start | bytes 1048576 | tf_op jit(solution)/shard_map/all_to_all | solution.py:30
  40.2 14.5 %all-to-all-done.1 = bf16[16,64,256]{2,1,0:T(8,128)(2,1)S(1)} async-done(((bf16[16,64,256]{2,1,0:T(8,128)(2,1)}), bf16[16,64,256]{2,1,0:T(8,128)(2,1)S(1)}, u32[]{:S(2)}, u32[]{:S(2)}) %all-to-all-start.1) | async-done | bytes 524320 | tf_op jit(solution)/shard_map/all_to_all | solution.py:30
  54.6 0.3 shard_map.46
  54.9 6.0 %collective-permute-start = (f32[4,256,128]{2,1,0:T(8,128)S(1)}, f32[4,256,128]{2,1,0:T(8,128)S(1)}, u32[]{:S(2)}, u32[]{:S(2)}) collective-permute-start(f32[4,256,128]{2,1,0:T(8,128)S(1)} %shard_map.46), channel_id=1, source_target_pairs={{0,1},{1,0},{2,3},{3,2},{4,5},{5,4},{6,7},{7,6},{8,9},{9,8},{10,11... | collective-permute-start | bytes 1572872 | tf_op jit(solution)/shard_map/ppermute | solution.py:92
  61.0 0.3 shard_map.47.right_ref
  61.3 1.2 %collective-permute-done.left_ref = f32[4,256,128]{2,1,0:T(8,128)S(1)} collective-permute-done((f32[4,256,128]{2,1,0:T(8,128)S(1)}, f32[4,256,128]{2,1,0:T(8,128)S(1)}, u32[]{:S(2)}, u32[]{:S(2)}) %collective-permute-start) | collective-permute-done | bytes 524320 | tf_op jit(solution)/shard_map/ppermute | solution.py:92
  62.5 0.9 shard_map.48
  63.3 0.0 copy-start.1
  63.3 8.4 %all-to-all-start.2 = ((f32[32,32,128]{2,1,0:T(8,128)}), f32[32,32,128]{2,1,0:T(8,128)S(1)}, u32[]{:S(2)}, u32[]{:S(2)}) async-start(f32[32,32,128]{2,1,0:T(8,128)} %bitcast.4), calls=%async_computation.2 | async-start | bytes 1048576 | tf_op jit(solution)/shard_map/all_to_all | solution.py:96
  71.7 0.0 copy-done.1
  71.8 0.0 copy-start
  71.8 23.6 %all-gather = f32[128,1024]{1,0:T(8,128)S(1)} all-gather(f32[32,1024]{1,0:T(8,128)S(1)} %copy-done.1), channel_id=2, replica_groups=mesh['x'=8,'yh'=4,'yl'=2,'zh'=2,'zl'=4,'c'=2] {'zl'}, dimensions={0}, use_global_device_ids=true | all-gather | bytes 655360 | tf_op jit(solution)/shard_map/all_gather | solution.py:85
  95.3 4.3 %collective-permute-start.1 = (f32[4,32,1024]{2,1,0:T(8,128)S(1)}, f32[4,32,1024]{2,1,0:T(8,128)S(1)}, u32[]{:S(2)}, u32[]{:S(2)}) collective-permute-start(f32[4,32,1024]{2,1,0:T(8,128)S(1)} %bitcast.10), channel_id=1, source_target_pairs={{0,1},{1,0},{2,3},{3,2},{4,5},{5,4},{6,7},{7,6},{8,9},{9,8},{10,11... | collective-permute-start | bytes 1572872 | tf_op jit(solution)/shard_map/ppermute | solution.py:86
  99.7 0.6 pad_add_fusion.place_ref
  100.3 0.9 collective-permute-done.1.other_ref
  101.2 0.0 copy-done
  101.2 3.4 %shard_map.49.permuted_ref = f32[32,1024]{1,0:T(8,128)S(1)} custom-call(s32[2]{0:T(128)} %pad_add_fusion.place_ref, s32[64,128]{1,0:T(8,128)S(1)} %bitcast.14, f32[4,32,1024]{2,1,0:T(8,128)S(1)} %bitcast.11, f32[4,32,1024]{2,1,0:T(8,128)S(1)} %collective-permute-done.1.other_ref), custom_call_target="tpu_custom_call" | custom-call | tf_op jit(solution)/shard_map/pallas_call | solution.py:19
  104.6 0.0 all-to-all-done.2.pieces_ref
  104.6 0.8 shard_map.50
Async XLA Ops:
  0.7 31.6 %copy-start.2 = (bf16[64,256]{1,0:T(8,128)(2,1)S(1)}, bf16[64,256]{1,0:T(8,128)(2,1)}, u32[]{:S(2)}) copy-start(bf16[64,256]{1,0:T(8,128)(2,1)} %param.6) | copy-start | bytes 98308
  33.2 21.4 %all-to-all-start.1 = ((bf16[16,64,256]{2,1,0:T(8,128)(2,1)}), bf16[16,64,256]{2,1,0:T(8,128)(2,1)S(1)}, u32[]{:S(2)}, u32[]{:S(2)}) async-start(bf16[16,64,256]{2,1,0:T(8,128)(2,1)} %broadcast_in_dim.5), calls=%async_computation.1 | async-start | bytes 1048576 | tf_op jit(solution)/shard_map/all_to_all | solution.py:30
  54.9 7.5 %collective-permute-start = (f32[4,256,128]{2,1,0:T(8,128)S(1)}, f32[4,256,128]{2,1,0:T(8,128)S(1)}, u32[]{:S(2)}, u32[]{:S(2)}) collective-permute-start(f32[4,256,128]{2,1,0:T(8,128)S(1)} %shard_map.46), channel_id=1, source_target_pairs={{0,1},{1,0},{2,3},{3,2},{4,5},{5,4},{6,7},{7,6},{8,9},{9,8},{10,11... | collective-permute-start | bytes 1572872 | tf_op jit(solution)/shard_map/ppermute | solution.py:92
  63.3 8.4 %copy-start.1 = (f32[32,1024]{1,0:T(8,128)S(1)}, f32[32,1024]{1,0:T(8,128)}, u32[]{:S(2)}) copy-start(f32[32,1024]{1,0:T(8,128)} %param.4) | copy-start | bytes 393220
  63.3 41.3 %all-to-all-start.2 = ((f32[32,32,128]{2,1,0:T(8,128)}), f32[32,32,128]{2,1,0:T(8,128)S(1)}, u32[]{:S(2)}, u32[]{:S(2)}) async-start(f32[32,32,128]{2,1,0:T(8,128)} %bitcast.4), calls=%async_computation.2 | async-start | bytes 1048576 | tf_op jit(solution)/shard_map/all_to_all | solution.py:96
  71.8 29.4 %copy-start = (s32[8192]{0:T(1024)S(1)}, s32[8192]{0:T(1024)}, u32[]{:S(2)}) copy-start(s32[8192]{0:T(1024)} %param.5) | copy-start | bytes 98308
  95.3 5.8 %collective-permute-start.1 = (f32[4,32,1024]{2,1,0:T(8,128)S(1)}, f32[4,32,1024]{2,1,0:T(8,128)S(1)}, u32[]{:S(2)}, u32[]{:S(2)}) collective-permute-start(f32[4,32,1024]{2,1,0:T(8,128)S(1)} %bitcast.10), channel_id=1, source_target_pairs={{0,1},{1,0},{2,3},{3,2},{4,5},{5,4},{6,7},{7,6},{8,9},{9,8},{10,11... | collective-permute-start | bytes 1572872 | tf_op jit(solution)/shard_map/ppermute | solution.py:86

commit v4 on v3

--- a/solution.py
+++ b/solution.py
@@ -7,8 +7,8 @@
 
 
 BULK = ("x", "yh", "yl", "zh")
-OWNER = ("zl", "c")
-AXES = {"x": 8, "yh": 4, "yl": 2, "zh": 2, "zl": 4, "c": 2}
+OWNER = ("z1", "z0", "c")
+AXES = {"x": 8, "yh": 4, "yl": 2, "zh": 2, "z1": 2, "z0": 2, "c": 2}
 SWAP = [(0, 1), (1, 0)]
 VMEM = pl.BlockSpec(memory_space=pltpu.VMEM)
 SMEM = pl.BlockSpec(memory_space=pltpu.SMEM)
@@ -24,18 +24,21 @@
     )(*scalars, *arrays)
 
 
-def gather(block, axes):
-    members = lax.axis_size(axes)
-    copies = jnp.broadcast_to(block[None], (members,) + block.shape)
-    return lax.all_to_all(copies, axes, 0, 0, tiled=True)
-
-
 def product(parity_ref, upper_ref, lower_ref, out_ref):
-    upper = upper_ref[...]
     for z in range(4):
-        out_ref[z] = lax.dot_general(
-            upper, lower_ref[2 * z + parity_ref[0]], (((1,), (1,)), ((), ())), preferred_element_type=jnp.float32
-        )
+        halves = []
+        for half in range(2):
+            dots = [
+                lax.dot_general(
+                    upper_ref[:, z0, half * 16 : half * 16 + 16, :].reshape(128, 256),
+                    lower_ref[2 * z + parity_ref[0], z0],
+                    (((1,), (1,)), ((), ())),
+                    preferred_element_type=jnp.float32,
+                )
+                for z0 in range(2)
+            ]
+            halves.append(dots[0] + dots[1])
+        out_ref[z] = jnp.concatenate(halves, axis=1).reshape(8, 16, 128)
 
 
 def add(left_ref, right_ref, out_ref):
@@ -62,16 +65,19 @@
 
 
 def finish(pieces_ref, permuted_ref, out_ref):
-    low = lax.broadcasted_iota(jnp.int32, (32, 128), 1) < 64
+    quarter = lax.broadcasted_iota(jnp.int32, (16, 128), 1) // 32
     for yh in range(4):
-        first, second = (sum(pieces_ref[zl * 8 + yh * 2 + zh] for zl in range(4)) for zh in range(2))
-        blocks = (
-            jnp.where(low, first, pltpu.roll(second, 64, 1)),
-            jnp.where(low, pltpu.roll(first, 64, 1), second),
-        )
+        sums = [pieces_ref[0, q % 2, yh, q // 2] + pieces_ref[1, q % 2, yh, q // 2] for q in range(4)]
         for yl in range(2):
             at = slice((yh * 2 + yl) * 128, (yh * 2 + yl + 1) * 128)
-            out_ref[:, at] = permuted_ref[:, at] - blocks[yl]
+            for half in range(2):
+                rows = slice(half * 16, half * 16 + 16)
+                update = sums[0]
+                for q in range(4):
+                    shift = (q * 32 - half * 64 - yl * 32) % 128
+                    moved = pltpu.roll(sums[q], shift, 1) if shift else sums[q]
+                    update = jnp.where(quarter == q, moved, update)
+                out_ref[rows, at] = permuted_ref[rows, at] - update
 
 
 def shards(slab_cols, pivots, lower_panels, upper_rows):
@@ -79,21 +85,25 @@
     columns, row_block = slab_cols.shape
     inner = upper_rows.shape[1]
 
-    upper = gather(upper_rows, ("yh", "zh")).reshape(-1, inner)
-    lower = gather(lower_panels, ("x", "yl")).reshape(8, -1, inner)
+    upper = jnp.broadcast_to(upper_rows[None], (16, columns, inner))
+    upper = lax.all_to_all(upper, ("yh", "zh", "z0"), 0, 0, tiled=True).reshape(8, 2, columns, inner)
+    lower = jnp.broadcast_to(lower_panels.reshape(1, 2, 1, -1, inner), (8, 2, 2, 32, inner))
+    lower = lax.all_to_all(lower.reshape(32, 32, inner), ("x", "z0", "yl"), 0, 0, tiled=True)
+    lower = lower.reshape(8, 2, 64, inner)
 
-    own = lax.all_gather(slab_cols, "zl", axis=0)
+    own = lax.all_gather(slab_cols, ("z1", "z0"), axis=0)
     other = lax.ppermute(own, "c", SWAP)
 
     def partial_value(parity):
-        out = (4, upper.shape[0], lower.shape[1])
+        out = (4, 8, 16, 128)
         return kernel(product, [parity.reshape(1)], [upper, lower], out)
 
     received = lax.ppermute(partial_value(1 - core), "c", SWAP)
     kept = partial_value(core)
     kept = kernel(add, [], [received, kept], kept.shape)
 
-    pieces = lax.all_to_all(kept.reshape(32, columns, -1), ("zl", "yh", "zh"), 0, 0, tiled=True)
+    pieces = lax.all_to_all(kept.reshape(32, 16, 128), ("z1", "z0", "yh", "zh"), 0, 0, tiled=True)
+    pieces = pieces.reshape(2, 2, 4, 2, 16, 128)
 
     place = jnp.stack([lax.axis_index(OWNER), core])
     permuted = kernel(permute, [place], [pivots.reshape(-1, 128), own, other], (columns, row_block))

time: 106 us -> 107 us (level)
  the two profiles are of different devices: /device:TPU:1 before, /device:TPU:128 now
where the time goes in v4:
time: 107 us
  blocking collectives  50.5 us (47%)
  waiting for transfers between devices  26.5 us (25%)
  starting transfers between devices  21.3 us (20%)
  Pallas kernels  5.94 us (6%)
  local copies, waits for them, and re-layouts  1.61 us (2%)
    all_to_all x1, blocking collectives, shards(): lax.all_to_all(upper, ('yh', 'zh', 'z0'), 0, 0, tiled=True)  33.1 us
    all_gather x1, blocking collectives, shards(): own = lax.all_gather(slab_cols, ('z1', 'z0'), axis=0)  17.3 us
    all_to_all x1, waiting for transfers between devices, shards(): lax.all_to_all(lower.reshape(32, 32, inner), ('x', 'z0', 'yl'), 0, 0, til...  14.9 us
    all_to_all x1, waiting for transfers between devices, shards(): lax.all_to_all(kept.reshape(32, 16, 128), ('z1', 'z0', 'yh', 'zh'), 0, 0,...  11.7 us
    all_to_all x1, starting transfers between devices, shards(): lax.all_to_all(kept.reshape(32, 16, 128), ('z1', 'z0', 'yh', 'zh'), 0, 0,...  9.1 us
    all_to_all x1, starting transfers between devices, shards(): lax.all_to_all(lower.reshape(32, 32, inner), ('x', 'z0', 'yl'), 0, 0, til...  8.38 us
    pallas_call x5, Pallas kernels, kernel(): pl.pallas_call(body, out_shape=pltpu.VMEM(out, jnp.float32) if vmem_out e...  5.94 us
  transfers between devices with their start and end apart: 4, of which 2 were waited for; matrix products, arithmetic and copies ran while one was open for 1% of the time, Pallas kernels for 4%

profile of v4, /device:TPU:128, one launch (start us, length us, event | category | flops | bytes accessed | tf_op | source)
XLA Modules:
  0.0 106.6 jit_solution(15505445004565134697)
XLA Ops:
  0.0 0.7 broadcast_in_dim.6
  0.7 0.0 copy-start.2
  0.8 33.1 %all_to_all.15 = bf16[16,32,256]{2,1,0:T(8,128)(2,1)S(1)} all-to-all(bf16[16,32,256]{2,1,0:T(8,128)(2,1)S(1)} %broadcast_in_dim.6), channel_id=1, replica_groups=mesh['x'=8,'yh'=4,'yl'=2,'zh'=2,'z1'=2,'z0'=2,'c'=2] {'yh','zh','z0'}, dimensions={0} | all-to-all | bytes 524288 | tf_op jit(solution)/shard_map/all_to_all | solution.py:89
  33.9 0.0 copy-done.2
  33.9 0.9 broadcast_in_dim.15
  34.8 8.4 %all-to-all-start.1 = ((bf16[32,32,256]{2,1,0:T(8,128)(2,1)}), bf16[32,32,256]{2,1,0:T(8,128)(2,1)S(1)}, u32[]{:S(2)}, u32[]{:S(2)}) async-start(bf16[32,32,256]{2,1,0:T(8,128)(2,1)} %bitcast.3), calls=%async_computation.1 | async-start | bytes 1048576 | tf_op jit(solution)/shard_map/all_to_all | solution.py:91
  43.2 14.9 %all-to-all-done.1 = bf16[32,32,256]{2,1,0:T(8,128)(2,1)S(1)} async-done(((bf16[32,32,256]{2,1,0:T(8,128)(2,1)}), bf16[32,32,256]{2,1,0:T(8,128)(2,1)S(1)}, u32[]{:S(2)}, u32[]{:S(2)}) %all-to-all-start.1) | async-done | bytes 524320 | tf_op jit(solution)/shard_map/all_to_all | solution.py:91
  58.0 0.0 copy-start.1
  58.0 0.5 shard_map.46
  58.5 1.9 %collective-permute-start = (f32[4,8,16,128]{3,2,1,0:T(8,128)S(1)}, f32[4,8,16,128]{3,2,1,0:T(8,128)S(1)}, u32[]{:S(2)}, u32[]{:S(2)}) collective-permute-start(f32[4,8,16,128]{3,2,1,0:T(8,128)S(1)} %shard_map.46), channel_id=1, source_target_pairs={{0,1},{1,0},{2,3},{3,2},{4,5},{5,4},{6,7},{7,6},{8,9},{9,8},{10,11... | collective-permute-start | bytes 786440 | tf_op jit(solution)/shard_map/ppermute | solution.py:101
  60.4 0.0 copy-done.1
  60.4 17.3 %all-gather = f32[128,1024]{1,0:T(8,128)S(1)} all-gather(f32[32,1024]{1,0:T(8,128)S(1)} %copy-done.1), channel_id=2, replica_groups=mesh['x'=8,'yh'=4,'yl'=2,'zh'=2,'z1'=2,'z0'=2,'c'=2] {'z1','z0'}, dimensions={0}, use_global_device_ids=true | all-gather | bytes 655360 | tf_op jit(solution)/shard_map/all_gather | solution.py:94
  77.8 1.9 %collective-permute-start.1 = (f32[4,32,1024]{2,1,0:T(8,128)S(1)}, f32[4,32,1024]{2,1,0:T(8,128)S(1)}, u32[]{:S(2)}, u32[]{:S(2)}) collective-permute-start(f32[4,32,1024]{2,1,0:T(8,128)S(1)} %bitcast.15), channel_id=1, source_target_pairs={{0,1},{1,0},{2,3},{3,2},{4,5},{5,4},{6,7},{7,6},{8,9},{9,8},{10,11... | collective-permute-start | bytes 1572872 | tf_op jit(solution)/shard_map/ppermute | solution.py:95
  79.7 0.5 shard_map.47.right_ref
  80.2 0.0 collective-permute-done.left_ref
  80.2 0.7 shard_map.48
  80.9 0.0 copy-start
  80.9 9.1 %all-to-all-start.2 = ((f32[32,16,128]{2,1,0:T(8,128)}), f32[32,16,128]{2,1,0:T(8,128)S(1)}, u32[]{:S(2)}, u32[]{:S(2)}) async-start(f32[32,16,128]{2,1,0:T(8,128)} %bitcast.6), calls=%async_computation.2 | async-start | bytes 524288 | tf_op jit(solution)/shard_map/all_to_all | solution.py:105
  90.0 0.7 pad_add_fusion.place_ref
  90.7 0.0 collective-permute-done.1.other_ref
  90.7 0.0 copy-done
  90.7 3.4 %shard_map.49.permuted_ref = f32[32,1024]{1,0:T(8,128)S(1)} custom-call(s32[2]{0:T(128)} %pad_add_fusion.place_ref, s32[64,128]{1,0:T(8,128)S(1)} %bitcast.18, f32[4,32,1024]{2,1,0:T(8,128)S(1)} %bitcast.16, f32[4,32,1024]{2,1,0:T(8,128)S(1)} %collective-permute-done.1.other_ref), custom_call_target="tpu_custom_call" | custom-call | tf_op jit(solution)/shard_map/pallas_call | solution.py:19
  94.1 11.7 %all-to-all-done.2 = f32[32,16,128]{2,1,0:T(8,128)S(1)} async-done(((f32[32,16,128]{2,1,0:T(8,128)}), f32[32,16,128]{2,1,0:T(8,128)S(1)}, u32[]{:S(2)}, u32[]{:S(2)}) %all-to-all-start.2) | async-done | bytes 262176 | tf_op jit(solution)/shard_map/all_to_all | solution.py:105
  105.8 0.8 shard_map.50
Async XLA Ops:
  0.7 33.2 %copy-start.2 = (bf16[64,256]{1,0:T(8,128)(2,1)S(1)}, bf16[64,256]{1,0:T(8,128)(2,1)}, u32[]{:S(2)}) copy-start(bf16[64,256]{1,0:T(8,128)(2,1)} %param.6) | copy-start | bytes 98308
  34.8 23.2 %all-to-all-start.1 = ((bf16[32,32,256]{2,1,0:T(8,128)(2,1)}), bf16[32,32,256]{2,1,0:T(8,128)(2,1)S(1)}, u32[]{:S(2)}, u32[]{:S(2)}) async-start(bf16[32,32,256]{2,1,0:T(8,128)(2,1)} %bitcast.3), calls=%async_computation.1 | async-start | bytes 1048576 | tf_op jit(solution)/shard_map/all_to_all | solution.py:91
  58.0 2.4 %copy-start.1 = (f32[32,1024]{1,0:T(8,128)S(1)}, f32[32,1024]{1,0:T(8,128)}, u32[]{:S(2)}) copy-start(f32[32,1024]{1,0:T(8,128)} %param.4) | copy-start | bytes 393220
  58.5 21.7 %collective-permute-start = (f32[4,8,16,128]{3,2,1,0:T(8,128)S(1)}, f32[4,8,16,128]{3,2,1,0:T(8,128)S(1)}, u32[]{:S(2)}, u32[]{:S(2)}) collective-permute-start(f32[4,8,16,128]{3,2,1,0:T(8,128)S(1)} %shard_map.46), channel_id=1, source_target_pairs={{0,1},{1,0},{2,3},{3,2},{4,5},{5,4},{6,7},{7,6},{8,9},{9,8},{10,11... | collective-permute-start | bytes 786440 | tf_op jit(solution)/shard_map/ppermute | solution.py:101
  77.8 12.9 %collective-permute-start.1 = (f32[4,32,1024]{2,1,0:T(8,128)S(1)}, f32[4,32,1024]{2,1,0:T(8,128)S(1)}, u32[]{:S(2)}, u32[]{:S(2)}) collective-permute-start(f32[4,32,1024]{2,1,0:T(8,128)S(1)} %bitcast.15), channel_id=1, source_target_pairs={{0,1},{1,0},{2,3},{3,2},{4,5},{5,4},{6,7},{7,6},{8,9},{9,8},{10,11... | collective-permute-start | bytes 1572872 | tf_op jit(solution)/shard_map/ppermute | solution.py:95
  80.9 9.8 %copy-start = (s32[8192]{0:T(1024)S(1)}, s32[8192]{0:T(1024)}, u32[]{:S(2)}) copy-start(s32[8192]{0:T(1024)} %param.5) | copy-start | bytes 98308
  80.9 24.9 %all-to-all-start.2 = ((f32[32,16,128]{2,1,0:T(8,128)}), f32[32,16,128]{2,1,0:T(8,128)S(1)}, u32[]{:S(2)}, u32[]{:S(2)}) async-start(f32[32,16,128]{2,1,0:T(8,128)} %bitcast.6), calls=%async_computation.2 | async-start | bytes 524288 | tf_op jit(solution)/shard_map/all_to_all | solution.py:105

commit v5 on v3

v5 whole, which is shorter than its diff:
```python
import jax
import jax.numpy as jnp
from jax import lax
from jax.experimental import pallas as pl
from jax.experimental.pallas import tpu as pltpu
from jax.sharding import Mesh, PartitionSpec as P


BULK = ("x", "y", "zh")
OWNER = ("zl", "c")
AXES = {"x": 8, "y": 8, "zh": 2, "zl": 4, "c": 2}
SWAP = [(0, 1), (1, 0)]
VMEM = pl.BlockSpec(memory_space=pltpu.VMEM)
SMEM = pl.BlockSpec(memory_space=pltpu.SMEM)


def kernel(body, scalars, arrays, out, dtype=jnp.float32, vmem_out=True):
    arrays = [pltpu.with_memory_space_constraint(a, pltpu.VMEM) for a in arrays]
    return pl.pallas_call(
        body,
        out_shape=pltpu.VMEM(out, dtype) if vmem_out else jax.ShapeDtypeStruct(out, dtype),
        in_specs=[SMEM] * len(scalars) + [VMEM] * len(arrays),
        out_specs=VMEM,
    )(*scalars, *arrays)


def copies(own_ref, other_ref, out_ref):
    for x in range(8):
        out_ref[x, 0] = own_ref[...]
        out_ref[x, 1] = other_ref[...]


def product(place_ref, upper_ref, lower_ref, out_ref):
    parity, zh = place_ref[0], place_ref[1]
    for z in range(4):
        owner = 2 * z + parity
        rows = jnp.concatenate([lower_ref[owner, zh], lower_ref[owner, 1 - zh]], axis=0)
        out_ref[z] = lax.dot_general(
            upper_ref[...], rows, (((1,), (1,)), ((), ())), preferred_element_type=jnp.float32
        )


def add(left_ref, right_ref, out_ref):
    out_ref[...] = left_ref[...] + right_ref[...]


def permute(place_ref, pivots_ref, own_ref, other_ref, out_ref):
    owner, core = place_ref[0], place_ref[1]

    def block(b, _):
        index = pivots_ref[pl.ds(owner * 8 + b, 1), :]
        side = ((index >> 10) & 1) ^ core
        key = jnp.broadcast_to(side * 32 + (index >> 11) * 8 + ((index >> 7) & 7), (32, 128))
        lane = jnp.broadcast_to(index & 127, (32, 128))
        found = jnp.zeros((32, 128), jnp.float32)
        for k in range(64):
            ref = own_ref if k < 32 else other_ref
            source = ref[(k % 32) // 8, :, (k % 8) * 128 : (k % 8 + 1) * 128]
            found = jnp.where(key == k, jnp.take_along_axis(source, lane, axis=1, mode="promise_in_bounds"), found)
        out_ref[:, pl.ds(pl.multiple_of(b * 128, 128), 128)] = found
        return 0

    lax.fori_loop(0, 8, block, 0)


def finish(pieces_ref, permuted_ref, out_ref):
    for y in range(8):
        at = slice(y * 128, (y + 1) * 128)
        out_ref[:, at] = permuted_ref[:, at] - sum(pieces_ref[zl * 8 + y] for zl in range(4))


def shards(slab_cols, pivots, lower_panels, upper_rows):
    core = lax.axis_index("c")
    columns, row_block = slab_cols.shape
    inner = upper_rows.shape[1]

    upper = jnp.broadcast_to(upper_rows[None], (8, columns, inner))
    upper = lax.all_to_all(upper, "y", 0, 0, tiled=True).reshape(-1, inner)
    paired = lax.ppermute(lower_panels, "zh", SWAP)
    lower = kernel(copies, [], [lower_panels, paired], (8, 2, 64, inner), dtype=jnp.bfloat16)
    lower = lax.all_to_all(lower.reshape(8, 128, inner), "x", 0, 0, tiled=True).reshape(8, 2, 64, inner)

    own = lax.all_gather(slab_cols, "zl", axis=0)
    other = lax.ppermute(own, "c", SWAP)

    def partial_value(parity):
        place = jnp.stack([parity, lax.axis_index("zh")])
        return kernel(product, [place], [upper, lower], (4, 256, 128))

    received = lax.ppermute(partial_value(1 - core), "c", SWAP)
    kept = kernel(add, [], [received, partial_value(core)], (4, 256, 128))

    pieces = lax.all_to_all(kept.reshape(32, columns, -1), ("zl", "y"), 0, 0, tiled=True)

    place = jnp.stack([lax.axis_index(OWNER), core])
    permuted = kernel(permute, [place], [pivots.reshape(-1, 128), own, other], (columns, row_block))
    return kernel(finish, [], [pieces, permuted], (columns, row_block), vmem_out=False)


def solution(mesh):
    fine = Mesh(mesh.devices.reshape(tuple(AXES.values())), tuple(AXES))
    spec = P(BULK, OWNER)

    return jax.shard_map(shards, mesh=fine, in_specs=(spec, P(), spec, spec), out_specs=spec, check_vma=False)
```

time: 106 us -> 103 us (0.972)
  blocking collectives: 55.2 us -> 23.1 us
  starting transfers between devices: 25.6 us -> 50.5 us
  Pallas kernels: 5.63 us -> 7.69 us
  other arithmetic: 0.61 us -> 1.84 us
    all_to_all x1 -> x0, blocking collectives: 31.6 us -> none  [gather(): return lax.all_to_all(copies, axes, 0, 0, tiled=True)]
    ppermute x0 -> x1, starting transfers between devices: none -> 14.3 us  [shards(): paired = lax.ppermute(lower_panels, 'zh', SWAP)]
    all_to_all x2 -> x3, starting transfers between devices: 15.3 us -> 27.3 us  [the longest x1 12.6 us: shards(): lax.all_to_all(kept.reshape(32, columns, -1), ('zl', 'y'), 0, 0, tiled=True)]
    pallas_call x5 -> x6, Pallas kernels: 5.63 us -> 7.69 us  [kernel(): pl.pallas_call(body, out_shape=pltpu.VMEM(out, dtype) if vmem_out else ja...]
    ppermute x1, starting transfers between devices: 6.02 us -> 4.65 us  [shards(): received = lax.ppermute(partial_value(1 - core), 'c', SWAP)]
    ppermute x0 -> x1, waiting for transfers between devices: none -> 1.29 us  [shards(): paired = lax.ppermute(lower_panels, 'zh', SWAP)]
    another operation x0 -> x2, other arithmetic: none -> 1.24 us  [partial_value(): place = jnp.stack([parity, lax.axis_index('zh')])]
    ppermute x1, waiting for transfers between devices: 1.22 us -> 0.01 us  [shards(): received = lax.ppermute(partial_value(1 - core), 'c', SWAP)]
  transfers between devices with their start and end apart: 4 -> 6, of which waited for: 3 -> 3; matrix products, arithmetic and copies ran while one was open for 1% -> 2% of each run, Pallas kernels for 4% -> 5%
where the time goes in v5:
time: 103 us; the launch traced here: 102 us
  starting transfers between devices  50.5 us (49%)
  blocking collectives  23.1 us (22%)
  waiting for transfers between devices  17.3 us (17%)
  Pallas kernels  7.69 us (7%)
  other arithmetic  1.84 us (2%)
  local copies, waits for them, and re-layouts  1.39 us (1%)
    all_gather x1, blocking collectives, shards(): own = lax.all_gather(slab_cols, 'zl', axis=0)  23.1 us
    all_to_all x1, waiting for transfers between devices, shards(): lax.all_to_all(lower.reshape(8, 128, inner), 'x', 0, 0, tiled=True)  15.1 us
    ppermute x1, starting transfers between devices, shards(): paired = lax.ppermute(lower_panels, 'zh', SWAP)  14.3 us
    all_to_all x1, starting transfers between devices, shards(): lax.all_to_all(kept.reshape(32, columns, -1), ('zl', 'y'), 0, 0, tiled=True)  12.6 us
    all_to_all x1, starting transfers between devices, shards(): upper = lax.all_to_all(upper, 'y', 0, 0, tiled=True).reshape(-1, inner)  8.23 us
    pallas_call x6, Pallas kernels, kernel(): pl.pallas_call(body, out_shape=pltpu.VMEM(out, dtype) if vmem_out else ja...  7.69 us
    all_to_all x1, starting transfers between devices, shards(): lax.all_to_all(lower.reshape(8, 128, inner), 'x', 0, 0, tiled=True)  6.48 us
    ppermute x1, starting transfers between devices, shards(): received = lax.ppermute(partial_value(1 - core), 'c', SWAP)  4.65 us
  transfers between devices with their start and end apart: 6, of which 3 were waited for; matrix products, arithmetic and copies ran while one was open for 2% of the time, Pallas kernels for 5%

profile of v5, /device:TPU:1, one launch (start us, length us, event | category | flops | bytes accessed | tf_op | source)
XLA Modules:
  0.0 102.0 jit_solution(2516807713804047310)
XLA Ops:
  0.0 1.4 %broadcast_in_dim.2 = bf16[8,32,256]{2,1,0:T(8,128)(2,1)} broadcast(bf16[32,256]{1,0:T(8,128)(2,1)} %param.7), dimensions={1,2} | broadcast | bytes 147456 | tf_op jit(solution)/shard_map/broadcast_in_dim | solution.py:77
  1.4 8.2 %all-to-all-start = ((bf16[8,32,256]{2,1,0:T(8,128)(2,1)}), bf16[8,32,256]{2,1,0:T(8,128)(2,1)S(1)}, u32[]{:S(2)}, u32[]{:S(2)}) async-start(bf16[8,32,256]{2,1,0:T(8,128)(2,1)} %broadcast_in_dim.2), calls=%async_computation | async-start | bytes 262144 | tf_op jit(solution)/shard_map/all_to_all | solution.py:78
  9.6 14.3 %collective-permute-start = (bf16[64,256]{1,0:T(8,128)(2,1)S(1)}, bf16[64,256]{1,0:T(8,128)(2,1)S(1)}, u32[]{:S(2)}, u32[]{:S(2)}) collective-permute-start(bf16[64,256]{1,0:T(8,128)(2,1)S(1)} %copy-done), channel_id=1, source_target_pairs={{0,8},{8,0},{1,9},{9,1},{2,10},{10,2},{3,11},{11,3},{4,12},{12,4},... | collective-permute-start | bytes 98312 | tf_op jit(solution)/shard_map/ppermute | solution.py:79
  23.9 1.3 %collective-permute-done.other_ref = bf16[64,256]{1,0:T(8,128)(2,1)S(1)} collective-permute-done((bf16[64,256]{1,0:T(8,128)(2,1)S(1)}, bf16[64,256]{1,0:T(8,128)(2,1)S(1)}, u32[]{:S(2)}, u32[]{:S(2)}) %collective-permute-start) | collective-permute-done | bytes 32800 | tf_op jit(solution)/shard_map/ppermute | solution.py:79
  25.2 0.8 shard_map.46
  26.0 0.0 all-to-all-done
  26.0 6.5 %all-to-all-start.1 = ((bf16[8,128,256]{2,1,0:T(8,128)(2,1)}), bf16[8,128,256]{2,1,0:T(8,128)(2,1)S(1)}, u32[]{:S(2)}, u32[]{:S(2)}) async-start(bf16[8,128,256]{2,1,0:T(8,128)(2,1)} %bitcast.3), calls=%async_computation.1 | async-start | bytes 1048576 | tf_op jit(solution)/shard_map/all_to_all | solution.py:81
  32.5 0.6 pad_add_fusion.place_ref
  33.1 15.1 %all-to-all-done.1 = bf16[8,128,256]{2,1,0:T(8,128)(2,1)S(1)} async-done(((bf16[8,128,256]{2,1,0:T(8,128)(2,1)}), bf16[8,128,256]{2,1,0:T(8,128)(2,1)S(1)}, u32[]{:S(2)}, u32[]{:S(2)}) %all-to-all-start.1) | async-done | bytes 524320 | tf_op jit(solution)/shard_map/all_to_all | solution.py:81
  48.2 1.0 shard_map.47
  49.2 4.6 %collective-permute-start.1 = (f32[4,256,128]{2,1,0:T(8,128)S(1)}, f32[4,256,128]{2,1,0:T(8,128)S(1)}, u32[]{:S(2)}, u32[]{:S(2)}) collective-permute-start(f32[4,256,128]{2,1,0:T(8,128)S(1)} %shard_map.47), channel_id=1, source_target_pairs={{0,1},{1,0},{2,3},{3,2},{4,5},{5,4},{6,7},{7,6},{8,9},{9,8},{10,11... | collective-permute-start | bytes 1572872 | tf_op jit(solution)/shard_map/ppermute | solution.py:90
  53.8 0.7 pad_add_fusion.1.place_ref
  54.5 1.0 shard_map.48.right_ref
  55.4 0.0 collective-permute-done.1.left_ref
  55.4 0.8 shard_map.49
  56.3 12.6 %all-to-all-start.2 = ((f32[32,32,128]{2,1,0:T(8,128)}), f32[32,32,128]{2,1,0:T(8,128)S(1)}, u32[]{:S(2)}, u32[]{:S(2)}) async-start(f32[32,32,128]{2,1,0:T(8,128)} %bitcast.6), calls=%async_computation.2 | async-start | bytes 1048576 | tf_op jit(solution)/shard_map/all_to_all | solution.py:93
  68.9 0.0 copy-start.1
  68.9 23.1 %all-gather = f32[128,1024]{1,0:T(8,128)S(1)} all-gather(f32[32,1024]{1,0:T(8,128)S(1)} %copy-done.2), channel_id=2, replica_groups=mesh['x'=8,'y'=8,'zh'=2,'zl'=4,'c'=2] {'zl'}, dimensions={0}, use_global_device_ids=true | all-gather | bytes 655360 | tf_op jit(solution)/shard_map/all_gather | solution.py:83
  92.1 4.2 %collective-permute-start.2 = (f32[4,32,1024]{2,1,0:T(8,128)S(1)}, f32[4,32,1024]{2,1,0:T(8,128)S(1)}, u32[]{:S(2)}, u32[]{:S(2)}) collective-permute-start(f32[4,32,1024]{2,1,0:T(8,128)S(1)} %bitcast.12), channel_id=1, source_target_pairs={{0,1},{1,0},{2,3},{3,2},{4,5},{5,4},{6,7},{7,6},{8,9},{9,8},{10,11... | collective-permute-start | bytes 1572872 | tf_op jit(solution)/shard_map/ppermute | solution.py:84
  96.3 0.6 pad_add_fusion.2.place_ref
  96.9 0.9 collective-permute-done.2.other_ref
  97.8 3.4 %shard_map.50.permuted_ref = f32[32,1024]{1,0:T(8,128)S(1)} custom-call(s32[2]{0:T(128)} %pad_add_fusion.2.place_ref, s32[64,128]{1,0:T(8,128)S(1)} %bitcast.16, f32[4,32,1024]{2,1,0:T(8,128)S(1)} %bitcast.13, f32[4,32,1024]{2,1,0:T(8,128)S(1)} %collective-permute-done.2.other_ref), custom_call_target="tpu_custom_call" | custom-call | tf_op jit(solution)/shard_map/pallas_call | solution.py:19
  101.3 0.0 all-to-all-done.2.pieces_ref
  101.3 0.7 shard_map.51
  (5 shorter events, 0.0 us)
Async XLA Ops:
  1.4 8.2 %copy-start = (bf16[64,256]{1,0:T(8,128)(2,1)S(1)}, bf16[64,256]{1,0:T(8,128)(2,1)}, u32[]{:S(2)}) copy-start(bf16[64,256]{1,0:T(8,128)(2,1)} %own_ref.1) | copy-start | bytes 98308
  1.4 24.6 %all-to-all-start = ((bf16[8,32,256]{2,1,0:T(8,128)(2,1)}), bf16[8,32,256]{2,1,0:T(8,128)(2,1)S(1)}, u32[]{:S(2)}, u32[]{:S(2)}) async-start(bf16[8,32,256]{2,1,0:T(8,128)(2,1)} %broadcast_in_dim.2), calls=%async_computation | async-start | bytes 262144 | tf_op jit(solution)/shard_map/all_to_all | solution.py:78
  9.6 15.6 %collective-permute-start = (bf16[64,256]{1,0:T(8,128)(2,1)S(1)}, bf16[64,256]{1,0:T(8,128)(2,1)S(1)}, u32[]{:S(2)}, u32[]{:S(2)}) collective-permute-start(bf16[64,256]{1,0:T(8,128)(2,1)S(1)} %copy-done), channel_id=1, source_target_pairs={{0,8},{8,0},{1,9},{9,1},{2,10},{10,2},{3,11},{11,3},{4,12},{12,4},... | collective-permute-start | bytes 98312 | tf_op jit(solution)/shard_map/ppermute | solution.py:79
  26.0 22.2 %all-to-all-start.1 = ((bf16[8,128,256]{2,1,0:T(8,128)(2,1)}), bf16[8,128,256]{2,1,0:T(8,128)(2,1)S(1)}, u32[]{:S(2)}, u32[]{:S(2)}) async-start(bf16[8,128,256]{2,1,0:T(8,128)(2,1)} %bitcast.3), calls=%async_computation.1 | async-start | bytes 1048576 | tf_op jit(solution)/shard_map/all_to_all | solution.py:81
  49.2 6.3 %collective-permute-start.1 = (f32[4,256,128]{2,1,0:T(8,128)S(1)}, f32[4,256,128]{2,1,0:T(8,128)S(1)}, u32[]{:S(2)}, u32[]{:S(2)}) collective-permute-start(f32[4,256,128]{2,1,0:T(8,128)S(1)} %shard_map.47), channel_id=1, source_target_pairs={{0,1},{1,0},{2,3},{3,2},{4,5},{5,4},{6,7},{7,6},{8,9},{9,8},{10,11... | collective-permute-start | bytes 1572872 | tf_op jit(solution)/shard_map/ppermute | solution.py:90
  56.3 12.6 %copy-start.2 = (f32[32,1024]{1,0:T(8,128)S(1)}, f32[32,1024]{1,0:T(8,128)}, u32[]{:S(2)}) copy-start(f32[32,1024]{1,0:T(8,128)} %param.4) | copy-start | bytes 393220
  56.3 45.0 %all-to-all-start.2 = ((f32[32,32,128]{2,1,0:T(8,128)}), f32[32,32,128]{2,1,0:T(8,128)S(1)}, u32[]{:S(2)}, u32[]{:S(2)}) async-start(f32[32,32,128]{2,1,0:T(8,128)} %bitcast.6), calls=%async_computation.2 | async-start | bytes 1048576 | tf_op jit(solution)/shard_map/all_to_all | solution.py:93
  68.9 28.9 %copy-start.1 = (s32[8192]{0:T(1024)S(1)}, s32[8192]{0:T(1024)}, u32[]{:S(2)}) copy-start(s32[8192]{0:T(1024)} %param.5) | copy-start | bytes 98308
  92.1 5.7 %collective-permute-start.2 = (f32[4,32,1024]{2,1,0:T(8,128)S(1)}, f32[4,32,1024]{2,1,0:T(8,128)S(1)}, u32[]{:S(2)}, u32[]{:S(2)}) collective-permute-start(f32[4,32,1024]{2,1,0:T(8,128)S(1)} %bitcast.12), channel_id=1, source_target_pairs={{0,1},{1,0},{2,3},{3,2},{4,5},{5,4},{6,7},{7,6},{8,9},{9,8},{10,11... | collective-permute-start | bytes 1572872 | tf_op jit(solution)/shard_map/ppermute | solution.py:84

commit v6 on v5

--- a/solution.py
+++ b/solution.py
@@ -24,19 +24,18 @@
     )(*scalars, *arrays)
 
 
-def copies(own_ref, other_ref, out_ref):
+def copies(zh_ref, own_ref, other_ref, out_ref):
+    zh = zh_ref[0]
     for x in range(8):
-        out_ref[x, 0] = own_ref[...]
-        out_ref[x, 1] = other_ref[...]
+        out_ref[x, zh] = own_ref[...]
+        out_ref[x, 1 - zh] = other_ref[...]
 
 
-def product(place_ref, upper_ref, lower_ref, out_ref):
-    parity, zh = place_ref[0], place_ref[1]
+def product(parity_ref, upper_ref, lower_ref, out_ref):
+    upper = upper_ref[...]
     for z in range(4):
-        owner = 2 * z + parity
-        rows = jnp.concatenate([lower_ref[owner, zh], lower_ref[owner, 1 - zh]], axis=0)
         out_ref[z] = lax.dot_general(
-            upper_ref[...], rows, (((1,), (1,)), ((), ())), preferred_element_type=jnp.float32
+            upper, lower_ref[2 * z + parity_ref[0]], (((1,), (1,)), ((), ())), preferred_element_type=jnp.float32
         )
 
 
@@ -44,8 +43,8 @@
     out_ref[...] = left_ref[...] + right_ref[...]
 
 
-def permute(place_ref, pivots_ref, own_ref, other_ref, out_ref):
-    owner, core = place_ref[0], place_ref[1]
+def permute(owner_ref, core_ref, pivots_ref, own_ref, other_ref, out_ref):
+    owner, core = owner_ref[0], core_ref[0]
 
     def block(b, _):
         index = pivots_ref[pl.ds(owner * 8 + b, 1), :]
@@ -70,30 +69,28 @@
 
 
 def shards(slab_cols, pivots, lower_panels, upper_rows):
-    core = lax.axis_index("c")
+    core, zh, owner = (lax.axis_index(axes).reshape(1) for axes in ("c", "zh", OWNER))
     columns, row_block = slab_cols.shape
     inner = upper_rows.shape[1]
 
     upper = jnp.broadcast_to(upper_rows[None], (8, columns, inner))
     upper = lax.all_to_all(upper, "y", 0, 0, tiled=True).reshape(-1, inner)
     paired = lax.ppermute(lower_panels, "zh", SWAP)
-    lower = kernel(copies, [], [lower_panels, paired], (8, 2, 64, inner), dtype=jnp.bfloat16)
-    lower = lax.all_to_all(lower.reshape(8, 128, inner), "x", 0, 0, tiled=True).reshape(8, 2, 64, inner)
+    lower = kernel(copies, [zh], [lower_panels, paired], (8, 2, 64, inner), dtype=jnp.bfloat16)
+    lower = lax.all_to_all(lower.reshape(8, 128, inner), "x", 0, 0, tiled=True)
 
     own = lax.all_gather(slab_cols, "zl", axis=0)
     other = lax.ppermute(own, "c", SWAP)
 
     def partial_value(parity):
-        place = jnp.stack([parity, lax.axis_index("zh")])
-        return kernel(product, [place], [upper, lower], (4, 256, 128))
+        return kernel(product, [parity], [upper, lower], (4, 256, 128))
 
     received = lax.ppermute(partial_value(1 - core), "c", SWAP)
     kept = kernel(add, [], [received, partial_value(core)], (4, 256, 128))
 
     pieces = lax.all_to_all(kept.reshape(32, columns, -1), ("zl", "y"), 0, 0, tiled=True)
 
-    place = jnp.stack([lax.axis_index(OWNER), core])
-    permuted = kernel(permute, [place], [pivots.reshape(-1, 128), own, other], (columns, row_block))
+    permuted = kernel(permute, [owner, core], [pivots.reshape(-1, 128), own, other], (columns, row_block))
     return kernel(finish, [], [pieces, permuted], (columns, row_block), vmem_out=False)
 
 

time: 103 us -> 101 us (0.981)
  waiting for transfers between devices: 17.3 us -> 19.7 us
  Pallas kernels: 7.69 us -> 5.68 us
  other arithmetic: 1.84 us -> 0 us
    pallas_call x6, Pallas kernels: 7.69 us -> 5.68 us  [kernel(): pl.pallas_call(body, out_shape=pltpu.VMEM(out, dtype) if vmem_out else ja...]
    another operation x3 -> x0, other arithmetic: 1.84 us -> none  [the longest x2 1.24 us: partial_value(): place = jnp.stack([parity, lax.axis_index('zh')])]
    ppermute x1, waiting for transfers between devices: 0.01 us -> 1.22 us  [shards(): received = lax.ppermute(partial_value(1 - core), 'c', SWAP)]
  transfers between devices with their start and end apart: 6 -> 6, of which waited for: 3 -> 4; matrix products, arithmetic and copies ran while one was open for 2% -> 0% of each run, Pallas kernels for 5% -> 4%
where the time goes in v6:
time: 101 us; the launch traced here: 100 us
  starting transfers between devices  50.2 us (50%)
  blocking collectives  23.2 us (23%)
  waiting for transfers between devices  19.7 us (20%)
  Pallas kernels  5.68 us (6%)
  local copies, waits for them, and re-layouts  1.39 us (1%)
    all_gather x1, blocking collectives, shards(): own = lax.all_gather(slab_cols, 'zl', axis=0)  23.2 us
    all_to_all x1, waiting for transfers between devices, shards(): lower = lax.all_to_all(lower.reshape(8, 128, inner), 'x', 0, 0, tiled=True)  15.7 us
    ppermute x1, starting transfers between devices, shards(): paired = lax.ppermute(lower_panels, 'zh', SWAP)  14.3 us
    all_to_all x1, starting transfers between devices, shards(): lax.all_to_all(kept.reshape(32, columns, -1), ('zl', 'y'), 0, 0, tiled=True)  12.6 us
    all_to_all x1, starting transfers between devices, shards(): upper = lax.all_to_all(upper, 'y', 0, 0, tiled=True).reshape(-1, inner)  8.23 us
    all_to_all x1, starting transfers between devices, shards(): lower = lax.all_to_all(lower.reshape(8, 128, inner), 'x', 0, 0, tiled=True)  6.48 us
    pallas_call x6, Pallas kernels, kernel(): pl.pallas_call(body, out_shape=pltpu.VMEM(out, dtype) if vmem_out else ja...  5.68 us
    ppermute x1, starting transfers between devices, shards(): received = lax.ppermute(partial_value(1 - core), 'c', SWAP)  4.65 us
  transfers between devices with their start and end apart: 6, of which 4 were waited for; matrix products, arithmetic and copies ran while one was open for 0% of the time, Pallas kernels for 4%

profile of v6, /device:TPU:1, one launch (start us, length us, event | category | flops | bytes accessed | tf_op | source)
XLA Modules:
  0.0 100.3 jit_solution(9418902366195456491)
XLA Ops:
  0.0 1.4 %broadcast_in_dim.2 = bf16[8,32,256]{2,1,0:T(8,128)(2,1)} broadcast(bf16[32,256]{1,0:T(8,128)(2,1)} %param.7), dimensions={1,2} | broadcast | bytes 147456 | tf_op jit(solution)/shard_map/broadcast_in_dim | solution.py:76
  1.4 8.2 %all-to-all-start = ((bf16[8,32,256]{2,1,0:T(8,128)(2,1)}), bf16[8,32,256]{2,1,0:T(8,128)(2,1)S(1)}, u32[]{:S(2)}, u32[]{:S(2)}) async-start(bf16[8,32,256]{2,1,0:T(8,128)(2,1)} %broadcast_in_dim.2), calls=%async_computation | async-start | bytes 262144 | tf_op jit(solution)/shard_map/all_to_all | solution.py:77
  9.6 0.0 copy-done.1
  9.6 14.3 %collective-permute-start = (bf16[64,256]{1,0:T(8,128)(2,1)S(1)}, bf16[64,256]{1,0:T(8,128)(2,1)S(1)}, u32[]{:S(2)}, u32[]{:S(2)}) collective-permute-start(bf16[64,256]{1,0:T(8,128)(2,1)S(1)} %copy-done.1), channel_id=1, source_target_pairs={{0,8},{8,0},{1,9},{9,1},{2,10},{10,2},{3,11},{11,3},{4,12},{12,4},... | collective-permute-start | bytes 98312 | tf_op jit(solution)/shard_map/ppermute | solution.py:78
  23.9 1.3 %collective-permute-done.other_ref = bf16[64,256]{1,0:T(8,128)(2,1)S(1)} collective-permute-done((bf16[64,256]{1,0:T(8,128)(2,1)S(1)}, bf16[64,256]{1,0:T(8,128)(2,1)S(1)}, u32[]{:S(2)}, u32[]{:S(2)}) %collective-permute-start) | collective-permute-done | bytes 32800 | tf_op jit(solution)/shard_map/ppermute | solution.py:78
  25.2 0.8 shard_map.46
  26.0 0.0 all-to-all-done
  26.0 6.5 %all-to-all-start.1 = ((bf16[8,128,256]{2,1,0:T(8,128)(2,1)}), bf16[8,128,256]{2,1,0:T(8,128)(2,1)S(1)}, u32[]{:S(2)}, u32[]{:S(2)}) async-start(bf16[8,128,256]{2,1,0:T(8,128)(2,1)} %bitcast.3), calls=%async_computation.1 | async-start | bytes 1048576 | tf_op jit(solution)/shard_map/all_to_all | solution.py:80
  32.5 15.7 %all-to-all-done.1.lower_ref = bf16[8,128,256]{2,1,0:T(8,128)(2,1)S(1)} async-done(((bf16[8,128,256]{2,1,0:T(8,128)(2,1)}), bf16[8,128,256]{2,1,0:T(8,128)(2,1)S(1)}, u32[]{:S(2)}, u32[]{:S(2)}) %all-to-all-start.1) | async-done | bytes 524320 | tf_op jit(solution)/shard_map/all_to_all | solution.py:80
  48.2 0.3 shard_map.47
  48.5 4.6 %collective-permute-start.1 = (f32[4,256,128]{2,1,0:T(8,128)S(1)}, f32[4,256,128]{2,1,0:T(8,128)S(1)}, u32[]{:S(2)}, u32[]{:S(2)}) collective-permute-start(f32[4,256,128]{2,1,0:T(8,128)S(1)} %shard_map.47), channel_id=1, source_target_pairs={{0,1},{1,0},{2,3},{3,2},{4,5},{5,4},{6,7},{7,6},{8,9},{9,8},{10,11... | collective-permute-start | bytes 1572872 | tf_op jit(solution)/shard_map/ppermute | solution.py:88
  53.2 0.3 shard_map.48.right_ref
  53.5 1.2 %collective-permute-done.1.left_ref = f32[4,256,128]{2,1,0:T(8,128)S(1)} collective-permute-done((f32[4,256,128]{2,1,0:T(8,128)S(1)}, f32[4,256,128]{2,1,0:T(8,128)S(1)}, u32[]{:S(2)}, u32[]{:S(2)}) %collective-permute-start.1) | collective-permute-done | bytes 524320 | tf_op jit(solution)/shard_map/ppermute | solution.py:88
  54.7 0.8 shard_map.49
  55.5 12.6 %all-to-all-start.2 = ((f32[32,32,128]{2,1,0:T(8,128)}), f32[32,32,128]{2,1,0:T(8,128)S(1)}, u32[]{:S(2)}, u32[]{:S(2)}) async-start(f32[32,32,128]{2,1,0:T(8,128)} %bitcast.4), calls=%async_computation.2 | async-start | bytes 1048576 | tf_op jit(solution)/shard_map/all_to_all | solution.py:91
  68.1 0.0 copy-done.2
  68.2 0.0 copy-start
  68.2 23.2 %all-gather = f32[128,1024]{1,0:T(8,128)S(1)} all-gather(f32[32,1024]{1,0:T(8,128)S(1)} %copy-done.2), channel_id=2, replica_groups=mesh['x'=8,'y'=8,'zh'=2,'zl'=4,'c'=2] {'zl'}, dimensions={0}, use_global_device_ids=true | all-gather | bytes 655360 | tf_op jit(solution)/shard_map/all_gather | solution.py:82
  91.4 4.0 %collective-permute-start.2 = (f32[4,32,1024]{2,1,0:T(8,128)S(1)}, f32[4,32,1024]{2,1,0:T(8,128)S(1)}, u32[]{:S(2)}, u32[]{:S(2)}) collective-permute-start(f32[4,32,1024]{2,1,0:T(8,128)S(1)} %bitcast.8), channel_id=1, source_target_pairs={{0,1},{1,0},{2,3},{3,2},{4,5},{5,4},{6,7},{7,6},{8,9},{9,8},{10,11... | collective-permute-start | bytes 1572872 | tf_op jit(solution)/shard_map/ppermute | solution.py:83
  95.4 1.5 %collective-permute-done.2.other_ref = f32[4,32,1024]{2,1,0:T(8,128)S(1)} collective-permute-done((f32[4,32,1024]{2,1,0:T(8,128)S(1)}, f32[4,32,1024]{2,1,0:T(8,128)S(1)}, u32[]{:S(2)}, u32[]{:S(2)}) %collective-permute-start.2) | collective-permute-done | bytes 524320 | tf_op jit(solution)/shard_map/ppermute | solution.py:83
  96.9 0.0 copy-done
  96.9 2.8 %shard_map.50.permuted_ref = f32[32,1024]{1,0:T(8,128)S(1)} custom-call(s32[1]{0:T(128)} %bitcast.5.owner_ref, s32[1]{0:T(128)} %bitcast.parity_ref.core_ref, s32[64,128]{1,0:T(8,128)S(1)} %bitcast.12, f32[4,32,1024]{2,1,0:T(8,128)S(1)} %bitcast.9, f32[4,32,1024]{2,1,0:T(8,128)S(1)} %collective-permute-done.2.other_ref), custom_call_target="tpu_custom_call" | custom-call | tf_op jit(solution)/shard_map/pallas_call | solution.py:19
  99.6 0.0 all-to-all-done.2.pieces_ref
  99.6 0.7 shard_map.51
  (2 shorter events, 0.0 us)
Async XLA Ops:
  1.4 8.2 %copy-start.1 = (bf16[64,256]{1,0:T(8,128)(2,1)S(1)}, bf16[64,256]{1,0:T(8,128)(2,1)}, u32[]{:S(2)}) copy-start(bf16[64,256]{1,0:T(8,128)(2,1)} %own_ref.1) | copy-start | bytes 98308
  1.4 24.6 %all-to-all-start = ((bf16[8,32,256]{2,1,0:T(8,128)(2,1)}), bf16[8,32,256]{2,1,0:T(8,128)(2,1)S(1)}, u32[]{:S(2)}, u32[]{:S(2)}) async-start(bf16[8,32,256]{2,1,0:T(8,128)(2,1)} %broadcast_in_dim.2), calls=%async_computation | async-start | bytes 262144 | tf_op jit(solution)/shard_map/all_to_all | solution.py:77
  9.6 15.6 %collective-permute-start = (bf16[64,256]{1,0:T(8,128)(2,1)S(1)}, bf16[64,256]{1,0:T(8,128)(2,1)S(1)}, u32[]{:S(2)}, u32[]{:S(2)}) collective-permute-start(bf16[64,256]{1,0:T(8,128)(2,1)S(1)} %copy-done.1), channel_id=1, source_target_pairs={{0,8},{8,0},{1,9},{9,1},{2,10},{10,2},{3,11},{11,3},{4,12},{12,4},... | collective-permute-start | bytes 98312 | tf_op jit(solution)/shard_map/ppermute | solution.py:78
  26.0 22.2 %all-to-all-start.1 = ((bf16[8,128,256]{2,1,0:T(8,128)(2,1)}), bf16[8,128,256]{2,1,0:T(8,128)(2,1)S(1)}, u32[]{:S(2)}, u32[]{:S(2)}) async-start(bf16[8,128,256]{2,1,0:T(8,128)(2,1)} %bitcast.3), calls=%async_computation.1 | async-start | bytes 1048576 | tf_op jit(solution)/shard_map/all_to_all | solution.py:80
  48.5 6.2 %collective-permute-start.1 = (f32[4,256,128]{2,1,0:T(8,128)S(1)}, f32[4,256,128]{2,1,0:T(8,128)S(1)}, u32[]{:S(2)}, u32[]{:S(2)}) collective-permute-start(f32[4,256,128]{2,1,0:T(8,128)S(1)} %shard_map.47), channel_id=1, source_target_pairs={{0,1},{1,0},{2,3},{3,2},{4,5},{5,4},{6,7},{7,6},{8,9},{9,8},{10,11... | collective-permute-start | bytes 1572872 | tf_op jit(solution)/shard_map/ppermute | solution.py:88
  55.5 12.6 %copy-start.2 = (f32[32,1024]{1,0:T(8,128)S(1)}, f32[32,1024]{1,0:T(8,128)}, u32[]{:S(2)}) copy-start(f32[32,1024]{1,0:T(8,128)} %param.4) | copy-start | bytes 393220
  55.5 44.1 %all-to-all-start.2 = ((f32[32,32,128]{2,1,0:T(8,128)}), f32[32,32,128]{2,1,0:T(8,128)S(1)}, u32[]{:S(2)}, u32[]{:S(2)}) async-start(f32[32,32,128]{2,1,0:T(8,128)} %bitcast.4), calls=%async_computation.2 | async-start | bytes 1048576 | tf_op jit(solution)/shard_map/all_to_all | solution.py:91
  68.2 28.7 %copy-start = (s32[8192]{0:T(1024)S(1)}, s32[8192]{0:T(1024)}, u32[]{:S(2)}) copy-start(s32[8192]{0:T(1024)} %param.5) | copy-start | bytes 98308
  91.4 5.5 %collective-permute-start.2 = (f32[4,32,1024]{2,1,0:T(8,128)S(1)}, f32[4,32,1024]{2,1,0:T(8,128)S(1)}, u32[]{:S(2)}, u32[]{:S(2)}) collective-permute-start(f32[4,32,1024]{2,1,0:T(8,128)S(1)} %bitcast.8), channel_id=1, source_target_pairs={{0,1},{1,0},{2,3},{3,2},{4,5},{5,4},{6,7},{7,6},{8,9},{9,8},{10,11... | collective-permute-start | bytes 1572872 | tf_op jit(solution)/shard_map/ppermute | solution.py:83

commit v7 on v6

--- a/solution.py
+++ b/solution.py
@@ -7,8 +7,8 @@
 
 
 BULK = ("x", "y", "zh")
-OWNER = ("zl", "c")
-AXES = {"x": 8, "y": 8, "zh": 2, "zl": 4, "c": 2}
+OWNER = ("z1", "z0", "c")
+AXES = {"x": 8, "y": 8, "zh": 2, "z1": 2, "z0": 2, "c": 2}
 SWAP = [(0, 1), (1, 0)]
 VMEM = pl.BlockSpec(memory_space=pltpu.VMEM)
 SMEM = pl.BlockSpec(memory_space=pltpu.SMEM)
@@ -31,6 +31,19 @@
         out_ref[x, 1 - zh] = other_ref[...]
 
 
+def repeat(block_ref, out_ref):
+    for y in range(8):
+        out_ref[y] = block_ref[...]
+
+
+def line(z0_ref, z1_ref, own_ref, near_ref, far_ref, far_near_ref, out_ref):
+    z0, z1 = z0_ref[0], z1_ref[0]
+    out_ref[2 * z1 + z0] = own_ref[...]
+    out_ref[2 * z1 + 1 - z0] = near_ref[...]
+    out_ref[2 * (1 - z1) + z0] = far_ref[...]
+    out_ref[2 * (1 - z1) + 1 - z0] = far_near_ref[...]
+
+
 def product(parity_ref, upper_ref, lower_ref, out_ref):
     upper = upper_ref[...]
     for z in range(4):
@@ -43,14 +56,17 @@
     out_ref[...] = left_ref[...] + right_ref[...]
 
 
-def permute(owner_ref, core_ref, pivots_ref, own_ref, other_ref, out_ref):
-    owner, core = owner_ref[0], core_ref[0]
+def places(owner_ref, core_ref, pivots_ref, out_ref):
+    index = pivots_ref[pl.ds(pl.multiple_of(owner_ref[0] * 8, 8), 8), :]
+    side = ((index >> 10) & 1) ^ core_ref[0]
+    out_ref[0] = index & 127
+    out_ref[1] = side * 32 + (index >> 11) * 8 + ((index >> 7) & 7)
 
+
+def permute(places_ref, own_ref, other_ref, out_ref):
     def block(b, _):
-        index = pivots_ref[pl.ds(owner * 8 + b, 1), :]
-        side = ((index >> 10) & 1) ^ core
-        key = jnp.broadcast_to(side * 32 + (index >> 11) * 8 + ((index >> 7) & 7), (32, 128))
-        lane = jnp.broadcast_to(index & 127, (32, 128))
+        lane = jnp.broadcast_to(places_ref[0, pl.ds(b, 1), :], (32, 128))
+        key = jnp.broadcast_to(places_ref[1, pl.ds(b, 1), :], (32, 128))
         found = jnp.zeros((32, 128), jnp.float32)
         for k in range(64):
             ref = own_ref if k < 32 else other_ref
@@ -70,16 +86,20 @@
 
 def shards(slab_cols, pivots, lower_panels, upper_rows):
     core, zh, owner = (lax.axis_index(axes).reshape(1) for axes in ("c", "zh", OWNER))
+    z0, z1 = (lax.axis_index(axis).reshape(1) for axis in ("z0", "z1"))
     columns, row_block = slab_cols.shape
     inner = upper_rows.shape[1]
 
-    upper = jnp.broadcast_to(upper_rows[None], (8, columns, inner))
+    upper = kernel(repeat, [], [upper_rows], (8, columns, inner), dtype=jnp.bfloat16)
     upper = lax.all_to_all(upper, "y", 0, 0, tiled=True).reshape(-1, inner)
     paired = lax.ppermute(lower_panels, "zh", SWAP)
     lower = kernel(copies, [zh], [lower_panels, paired], (8, 2, 64, inner), dtype=jnp.bfloat16)
     lower = lax.all_to_all(lower.reshape(8, 128, inner), "x", 0, 0, tiled=True)
 
-    own = lax.all_gather(slab_cols, "zl", axis=0)
+    near = lax.ppermute(slab_cols, "z0", SWAP)
+    far = lax.ppermute(slab_cols, "z1", SWAP)
+    far_near = lax.ppermute(near, "z1", SWAP)
+    own = kernel(line, [z0, z1], [slab_cols, near, far, far_near], (4, columns, row_block))
     other = lax.ppermute(own, "c", SWAP)
 
     def partial_value(parity):
@@ -88,9 +108,10 @@
     received = lax.ppermute(partial_value(1 - core), "c", SWAP)
     kept = kernel(add, [], [received, partial_value(core)], (4, 256, 128))
 
-    pieces = lax.all_to_all(kept.reshape(32, columns, -1), ("zl", "y"), 0, 0, tiled=True)
+    pieces = lax.all_to_all(kept.reshape(32, columns, -1), ("z1", "z0", "y"), 0, 0, tiled=True)
 
-    permuted = kernel(permute, [owner, core], [pivots.reshape(-1, 128), own, other], (columns, row_block))
+    at = kernel(places, [owner, core], [pivots.reshape(-1, 128)], (2, 8, 128), dtype=jnp.int32)
+    permuted = kernel(permute, [], [at, own, other], (columns, row_block))
     return kernel(finish, [], [pieces, permuted], (columns, row_block), vmem_out=False)
 
 

time: 101 us -> 104 us (1.030)
  blocking collectives: 23.2 us -> 0 us
  waiting for transfers between devices: 19.7 us -> 35.9 us
  starting transfers between devices: 50.2 us -> 60 us
    all_gather x1 -> x0, blocking collectives: 23.2 us -> none  [shards(): own = lax.all_gather(slab_cols, 'zl', axis=0)]
    ppermute x0 -> x3, waiting for transfers between devices: none -> 16.2 us  [the longest x1 9.3 us: shards(): far = lax.ppermute(slab_cols, 'z1', SWAP)]
    ppermute x0 -> x3, starting transfers between devices: none -> 10.9 us  [the longest x1 4.03 us: shards(): far = lax.ppermute(slab_cols, 'z1', SWAP)]
    broadcast_in_dim x1 -> x0, local copies, waits for them, and re-layouts: 1.38 us -> none  [shards(): upper = jnp.broadcast_to(upper_rows[None], (8, columns, inner))]
    ppermute x1, starting transfers between devices: 3.98 us -> 2.78 us  [shards(): other = lax.ppermute(own, 'c', SWAP)]
    pallas_call x6 -> x9, Pallas kernels: 5.68 us -> 6.4 us  [kernel(): pl.pallas_call(body, out_shape=pltpu.VMEM(out, dtype) if vmem_out else ja...]
  transfers between devices with their start and end apart: 6 -> 9, of which waited for: 4 -> 7; matrix products, arithmetic and copies ran while one was open for 0% -> 0% of each run, Pallas kernels for 4% -> 4%
where the time goes in v7:
time: 104 us; the launch traced here: 103 us
  starting transfers between devices  60 us (58%)
  waiting for transfers between devices  35.9 us (35%)
  Pallas kernels  6.4 us (6%)
    all_to_all x1, waiting for transfers between devices, shards(): lower = lax.all_to_all(lower.reshape(8, 128, inner), 'x', 0, 0, tiled=True)  15.7 us
    ppermute x1, starting transfers between devices, shards(): paired = lax.ppermute(lower_panels, 'zh', SWAP)  14.3 us
    all_to_all x1, starting transfers between devices, shards(): lax.all_to_all(kept.reshape(32, columns, -1), ('z1', 'z0', 'y'), 0, 0, ti...  12.6 us
    ppermute x1, waiting for transfers between devices, shards(): far = lax.ppermute(slab_cols, 'z1', SWAP)  9.3 us
    all_to_all x1, starting transfers between devices, shards(): upper = lax.all_to_all(upper, 'y', 0, 0, tiled=True).reshape(-1, inner)  8.23 us
    all_to_all x1, starting transfers between devices, shards(): lower = lax.all_to_all(lower.reshape(8, 128, inner), 'x', 0, 0, tiled=True)  6.48 us
    pallas_call x9, Pallas kernels, kernel(): pl.pallas_call(body, out_shape=pltpu.VMEM(out, dtype) if vmem_out else ja...  6.4 us
    ppermute x1, starting transfers between devices, shards(): received = lax.ppermute(partial_value(1 - core), 'c', SWAP)  4.64 us
  transfers between devices with their start and end apart: 9, of which 7 were waited for; matrix products, arithmetic and copies ran while one was open for 0% of the time, Pallas kernels for 4%

profile of v7, /device:TPU:1, one launch (start us, length us, event | category | flops | bytes accessed | tf_op | source)
XLA Modules:
  0.0 103.1 jit_solution(7341673844650701984)
XLA Ops:
  0.0 0.7 copy-done.3
  0.7 0.7 shard_map.46
  1.4 8.2 %all-to-all-start = ((bf16[8,32,256]{2,1,0:T(8,128)(2,1)}), bf16[8,32,256]{2,1,0:T(8,128)(2,1)S(1)}, u32[]{:S(2)}, u32[]{:S(2)}) async-start(bf16[8,32,256]{2,1,0:T(8,128)(2,1)} %shard_map.46), calls=%async_computation | async-start | bytes 262144 | tf_op jit(solution)/shard_map/all_to_all | solution.py:94
  9.6 14.3 %collective-permute-start = (bf16[64,256]{1,0:T(8,128)(2,1)S(1)}, bf16[64,256]{1,0:T(8,128)(2,1)S(1)}, u32[]{:S(2)}, u32[]{:S(2)}) collective-permute-start(bf16[64,256]{1,0:T(8,128)(2,1)S(1)} %copy-done.2), channel_id=1, source_target_pairs={{0,8},{8,0},{1,9},{9,1},{2,10},{10,2},{3,11},{11,3},{4,12},{12,4},... | collective-permute-start | bytes 98312 | tf_op jit(solution)/shard_map/ppermute | solution.py:95
  23.9 1.3 %collective-permute-done.other_ref = bf16[64,256]{1,0:T(8,128)(2,1)S(1)} collective-permute-done((bf16[64,256]{1,0:T(8,128)(2,1)S(1)}, bf16[64,256]{1,0:T(8,128)(2,1)S(1)}, u32[]{:S(2)}, u32[]{:S(2)}) %collective-permute-start) | collective-permute-done | bytes 32800 | tf_op jit(solution)/shard_map/ppermute | solution.py:95
  25.2 0.8 shard_map.47
  26.0 6.5 %all-to-all-start.1 = ((bf16[8,128,256]{2,1,0:T(8,128)(2,1)}), bf16[8,128,256]{2,1,0:T(8,128)(2,1)S(1)}, u32[]{:S(2)}, u32[]{:S(2)}) async-start(bf16[8,128,256]{2,1,0:T(8,128)(2,1)} %bitcast.3), calls=%async_computation.1 | async-start | bytes 1048576 | tf_op jit(solution)/shard_map/all_to_all | solution.py:97
  32.5 15.7 %all-to-all-done.1.lower_ref = bf16[8,128,256]{2,1,0:T(8,128)(2,1)S(1)} async-done(((bf16[8,128,256]{2,1,0:T(8,128)(2,1)}), bf16[8,128,256]{2,1,0:T(8,128)(2,1)S(1)}, u32[]{:S(2)}, u32[]{:S(2)}) %all-to-all-start.1) | async-done | bytes 524320 | tf_op jit(solution)/shard_map/all_to_all | solution.py:97
  48.2 0.3 shard_map.48
  48.5 4.6 %collective-permute-start.1 = (f32[4,256,128]{2,1,0:T(8,128)S(1)}, f32[4,256,128]{2,1,0:T(8,128)S(1)}, u32[]{:S(2)}, u32[]{:S(2)}) collective-permute-start(f32[4,256,128]{2,1,0:T(8,128)S(1)} %shard_map.48), channel_id=1, source_target_pairs={{0,1},{1,0},{2,3},{3,2},{4,5},{5,4},{6,7},{7,6},{8,9},{9,8},{10,11... | collective-permute-start | bytes 1572872 | tf_op jit(solution)/shard_map/ppermute | solution.py:108
  53.2 0.3 shard_map.49.right_ref
  53.5 1.2 %collective-permute-done.1.left_ref = f32[4,256,128]{2,1,0:T(8,128)S(1)} collective-permute-done((f32[4,256,128]{2,1,0:T(8,128)S(1)}, f32[4,256,128]{2,1,0:T(8,128)S(1)}, u32[]{:S(2)}, u32[]{:S(2)}) %collective-permute-start.1) | collective-permute-done | bytes 524320 | tf_op jit(solution)/shard_map/ppermute | solution.py:108
  54.7 0.8 shard_map.50
  55.5 12.6 %all-to-all-start.2 = ((f32[32,32,128]{2,1,0:T(8,128)}), f32[32,32,128]{2,1,0:T(8,128)S(1)}, u32[]{:S(2)}, u32[]{:S(2)}) async-start(f32[32,32,128]{2,1,0:T(8,128)} %bitcast.4), calls=%async_computation.2 | async-start | bytes 1048576 | tf_op jit(solution)/shard_map/all_to_all | solution.py:111
  68.2 3.1 %collective-permute-start.2 = (f32[32,1024]{1,0:T(8,128)S(1)}, f32[32,1024]{1,0:T(8,128)S(1)}, u32[]{:S(2)}, u32[]{:S(2)}) collective-permute-start(f32[32,1024]{1,0:T(8,128)S(1)} %copy-done), channel_id=1, source_target_pairs={{0,2},{2,0},{1,3},{3,1},{4,6},{6,4},{5,7},{7,5},{8,10},{10,8},{9,1... | collective-permute-start | bytes 393224 | tf_op jit(solution)/shard_map/ppermute | solution.py:99
  71.3 4.0 %collective-permute-start.3 = (f32[32,1024]{1,0:T(8,128)S(1)}, f32[32,1024]{1,0:T(8,128)S(1)}, u32[]{:S(2)}, u32[]{:S(2)}) collective-permute-start(f32[32,1024]{1,0:T(8,128)S(1)} %copy-done), channel_id=1, source_target_pairs={{0,4},{4,0},{1,5},{5,1},{2,6},{6,2},{3,7},{7,3},{8,12},{12,8},{9,1... | collective-permute-start | bytes 393224 | tf_op jit(solution)/shard_map/ppermute | solution.py:100
  75.3 4.1 %collective-permute-done.2.near_ref = f32[32,1024]{1,0:T(8,128)S(1)} collective-permute-done((f32[32,1024]{1,0:T(8,128)S(1)}, f32[32,1024]{1,0:T(8,128)S(1)}, u32[]{:S(2)}, u32[]{:S(2)}) %collective-permute-start.2) | collective-permute-done | bytes 131104 | tf_op jit(solution)/shard_map/ppermute | solution.py:99
  79.4 3.8 %collective-permute-start.4 = (f32[32,1024]{1,0:T(8,128)S(1)}, f32[32,1024]{1,0:T(8,128)S(1)}, u32[]{:S(2)}, u32[]{:S(2)}) collective-permute-start(f32[32,1024]{1,0:T(8,128)S(1)} %collective-permute-done.2.near_ref), channel_id=1, source_target_pairs={{0,4},{4,0},{1,5},{5,1},{2,6},{6,2},{3,7},{7,3},{8,12},{12,8},{9,1... | collective-permute-start | bytes 393224 | tf_op jit(solution)/shard_map/ppermute | solution.py:101
  83.2 9.3 %collective-permute-done.3.far_ref = f32[32,1024]{1,0:T(8,128)S(1)} collective-permute-done((f32[32,1024]{1,0:T(8,128)S(1)}, f32[32,1024]{1,0:T(8,128)S(1)}, u32[]{:S(2)}, u32[]{:S(2)}) %collective-permute-start.3) | collective-permute-done | bytes 131104 | tf_op jit(solution)/shard_map/ppermute | solution.py:100
  92.5 2.8 %collective-permute-done.4.far_near_ref = f32[32,1024]{1,0:T(8,128)S(1)} collective-permute-done((f32[32,1024]{1,0:T(8,128)S(1)}, f32[32,1024]{1,0:T(8,128)S(1)}, u32[]{:S(2)}, u32[]{:S(2)}) %collective-permute-start.4) | collective-permute-done | bytes 131104 | tf_op jit(solution)/shard_map/ppermute | solution.py:101
  95.3 2.8 %collective-permute-start.5 = (f32[4,32,1024]{2,1,0:T(8,128)S(1)}, f32[4,32,1024]{2,1,0:T(8,128)S(1)}, u32[]{:S(2)}, u32[]{:S(2)}) collective-permute-start(f32[4,32,1024]{2,1,0:T(8,128)S(1)} %shard_map.52.own_ref), channel_id=1, source_target_pairs={{0,1},{1,0},{2,3},{3,2},{4,5},{5,4},{6,7},{7,6},{8,9},{9,8},{10,11... | collective-permute-start | bytes 1572872 | tf_op jit(solution)/shard_map/ppermute | solution.py:103
  98.2 1.5 %collective-permute-done.5.other_ref = f32[4,32,1024]{2,1,0:T(8,128)S(1)} collective-permute-done((f32[4,32,1024]{2,1,0:T(8,128)S(1)}, f32[4,32,1024]{2,1,0:T(8,128)S(1)}, u32[]{:S(2)}, u32[]{:S(2)}) %collective-permute-start.5) | collective-permute-done | bytes 524320 | tf_op jit(solution)/shard_map/ppermute | solution.py:103
  99.6 2.8 %shard_map.53.permuted_ref = f32[32,1024]{1,0:T(8,128)S(1)} custom-call(s32[2,8,128]{2,1,0:T(8,128)S(1)} %shard_map.51.places_ref, f32[4,32,1024]{2,1,0:T(8,128)S(1)} %shard_map.52.own_ref, f32[4,32,1024]{2,1,0:T(8,128)S(1)} %collective-permute-done.5.other_ref), custom_call_target="tpu_custom_call" | custom-call | tf_op jit(solution)/shard_map/pallas_call | solution.py:19
  102.4 0.7 shard_map.54
  (11 shorter events, 0.1 us)
Async XLA Ops:
  0.0 0.7 copy-start.3
  1.4 8.2 %copy-start.2 = (bf16[64,256]{1,0:T(8,128)(2,1)S(1)}, bf16[64,256]{1,0:T(8,128)(2,1)}, u32[]{:S(2)}) copy-start(bf16[64,256]{1,0:T(8,128)(2,1)} %own_ref.2) | copy-start | bytes 98308
  1.4 24.6 %all-to-all-start = ((bf16[8,32,256]{2,1,0:T(8,128)(2,1)}), bf16[8,32,256]{2,1,0:T(8,128)(2,1)S(1)}, u32[]{:S(2)}, u32[]{:S(2)}) async-start(bf16[8,32,256]{2,1,0:T(8,128)(2,1)} %shard_map.46), calls=%async_computation | async-start | bytes 262144 | tf_op jit(solution)/shard_map/all_to_all | solution.py:94
  9.6 15.6 %collective-permute-start = (bf16[64,256]{1,0:T(8,128)(2,1)S(1)}, bf16[64,256]{1,0:T(8,128)(2,1)S(1)}, u32[]{:S(2)}, u32[]{:S(2)}) collective-permute-start(bf16[64,256]{1,0:T(8,128)(2,1)S(1)} %copy-done.2), channel_id=1, source_target_pairs={{0,8},{8,0},{1,9},{9,1},{2,10},{10,2},{3,11},{11,3},{4,12},{12,4},... | collective-permute-start | bytes 98312 | tf_op jit(solution)/shard_map/ppermute | solution.py:95
  26.0 22.2 %all-to-all-start.1 = ((bf16[8,128,256]{2,1,0:T(8,128)(2,1)}), bf16[8,128,256]{2,1,0:T(8,128)(2,1)S(1)}, u32[]{:S(2)}, u32[]{:S(2)}) async-start(bf16[8,128,256]{2,1,0:T(8,128)(2,1)} %bitcast.3), calls=%async_computation.1 | async-start | bytes 1048576 | tf_op jit(solution)/shard_map/all_to_all | solution.py:97
  48.5 6.2 %collective-permute-start.1 = (f32[4,256,128]{2,1,0:T(8,128)S(1)}, f32[4,256,128]{2,1,0:T(8,128)S(1)}, u32[]{:S(2)}, u32[]{:S(2)}) collective-permute-start(f32[4,256,128]{2,1,0:T(8,128)S(1)} %shard_map.48), channel_id=1, source_target_pairs={{0,1},{1,0},{2,3},{3,2},{4,5},{5,4},{6,7},{7,6},{8,9},{9,8},{10,11... | collective-permute-start | bytes 1572872 | tf_op jit(solution)/shard_map/ppermute | solution.py:108
  55.5 12.6 %copy-start = (f32[32,1024]{1,0:T(8,128)S(1)}, f32[32,1024]{1,0:T(8,128)}, u32[]{:S(2)}) copy-start(f32[32,1024]{1,0:T(8,128)} %own_ref.3) | copy-start | bytes 393220
  55.5 46.9 %all-to-all-start.2 = ((f32[32,32,128]{2,1,0:T(8,128)}), f32[32,32,128]{2,1,0:T(8,128)S(1)}, u32[]{:S(2)}, u32[]{:S(2)}) async-start(f32[32,32,128]{2,1,0:T(8,128)} %bitcast.4), calls=%async_computation.2 | async-start | bytes 1048576 | tf_op jit(solution)/shard_map/all_to_all | solution.py:111
  68.2 11.2 %collective-permute-start.2 = (f32[32,1024]{1,0:T(8,128)S(1)}, f32[32,1024]{1,0:T(8,128)S(1)}, u32[]{:S(2)}, u32[]{:S(2)}) collective-permute-start(f32[32,1024]{1,0:T(8,128)S(1)} %copy-done), channel_id=1, source_target_pairs={{0,2},{2,0},{1,3},{3,1},{4,6},{6,4},{5,7},{7,5},{8,10},{10,8},{9,1... | collective-permute-start | bytes 393224 | tf_op jit(solution)/shard_map/ppermute | solution.py:99
  71.3 21.2 %collective-permute-start.3 = (f32[32,1024]{1,0:T(8,128)S(1)}, f32[32,1024]{1,0:T(8,128)S(1)}, u32[]{:S(2)}, u32[]{:S(2)}) collective-permute-start(f32[32,1024]{1,0:T(8,128)S(1)} %copy-done), channel_id=1, source_target_pairs={{0,4},{4,0},{1,5},{5,1},{2,6},{6,2},{3,7},{7,3},{8,12},{12,8},{9,1... | collective-permute-start | bytes 393224 | tf_op jit(solution)/shard_map/ppermute | solution.py:100
  79.4 15.9 %collective-permute-start.4 = (f32[32,1024]{1,0:T(8,128)S(1)}, f32[32,1024]{1,0:T(8,128)S(1)}, u32[]{:S(2)}, u32[]{:S(2)}) collective-permute-start(f32[32,1024]{1,0:T(8,128)S(1)} %collective-permute-done.2.near_ref), channel_id=1, source_target_pairs={{0,4},{4,0},{1,5},{5,1},{2,6},{6,2},{3,7},{7,3},{8,12},{12,8},{9,1... | collective-permute-start | bytes 393224 | tf_op jit(solution)/shard_map/ppermute | solution.py:101
  95.3 2.8 %copy-start.1 = (s32[8192]{0:T(1024)S(1)}, s32[8192]{0:T(1024)}, u32[]{:S(2)}) copy-start(s32[8192]{0:T(1024)} %param.5) | copy-start | bytes 98308
  95.3 4.3 %collective-permute-start.5 = (f32[4,32,1024]{2,1,0:T(8,128)S(1)}, f32[4,32,1024]{2,1,0:T(8,128)S(1)}, u32[]{:S(2)}, u32[]{:S(2)}) collective-permute-start(f32[4,32,1024]{2,1,0:T(8,128)S(1)} %shard_map.52.own_ref), channel_id=1, source_target_pairs={{0,1},{1,0},{2,3},{3,2},{4,5},{5,4},{6,7},{7,6},{8,9},{9,8},{10,11... | collective-permute-start | bytes 1572872 | tf_op jit(solution)/shard_map/ppermute | solution.py:103

commit v8 on v7

--- a/solution.py
+++ b/solution.py
@@ -27,12 +27,14 @@
 def copies(zh_ref, own_ref, other_ref, out_ref):
     zh = zh_ref[0]
     for x in range(8):
-        out_ref[x, zh] = own_ref[...]
-        out_ref[x, 1 - zh] = other_ref[...]
+        for z0 in range(2):
+            rows = slice(z0 * 32, z0 * 32 + 32)
+            out_ref[x, z0, zh] = own_ref[rows]
+            out_ref[x, z0, 1 - zh] = other_ref[rows]
 
 
 def repeat(block_ref, out_ref):
-    for y in range(8):
+    for y in range(16):
         out_ref[y] = block_ref[...]
 
 
@@ -45,11 +47,20 @@
 
 
 def product(parity_ref, upper_ref, lower_ref, out_ref):
-    upper = upper_ref[...]
     for z in range(4):
-        out_ref[z] = lax.dot_general(
-            upper, lower_ref[2 * z + parity_ref[0]], (((1,), (1,)), ((), ())), preferred_element_type=jnp.float32
-        )
+        halves = []
+        for half in range(2):
+            dots = [
+                lax.dot_general(
+                    upper_ref[:, z0, half * 16 : half * 16 + 16, :].reshape(128, 256),
+                    lower_ref[2 * z + parity_ref[0], z0],
+                    (((1,), (1,)), ((), ())),
+                    preferred_element_type=jnp.float32,
+                )
+                for z0 in range(2)
+            ]
+            halves.append(dots[0] + dots[1])
+        out_ref[z] = jnp.concatenate(halves, axis=1).reshape(8, 16, 128)
 
 
 def add(left_ref, right_ref, out_ref):
@@ -79,9 +90,19 @@
 
 
 def finish(pieces_ref, permuted_ref, out_ref):
+    quarter = lax.broadcasted_iota(jnp.int32, (16, 128), 1) // 32
     for y in range(8):
         at = slice(y * 128, (y + 1) * 128)
-        out_ref[:, at] = permuted_ref[:, at] - sum(pieces_ref[zl * 8 + y] for zl in range(4))
+        sums = [pieces_ref[0, z0, y] + pieces_ref[1, z0, y] for z0 in range(2)]
+        for half in range(2):
+            rows = slice(half * 16, half * 16 + 16)
+            update = sums[0]
+            for q in range(4):
+                zh, z0 = q // 2, q % 2
+                shift = (q * 32 - half * 64 - zh * 32) % 128
+                moved = pltpu.roll(sums[z0], shift, 1) if shift else sums[z0]
+                update = jnp.where(quarter == q, moved, update)
+            out_ref[rows, at] = permuted_ref[rows, at] - update
 
 
 def shards(slab_cols, pivots, lower_panels, upper_rows):
@@ -90,11 +111,11 @@
     columns, row_block = slab_cols.shape
     inner = upper_rows.shape[1]
 
-    upper = kernel(repeat, [], [upper_rows], (8, columns, inner), dtype=jnp.bfloat16)
-    upper = lax.all_to_all(upper, "y", 0, 0, tiled=True).reshape(-1, inner)
+    upper = kernel(repeat, [], [upper_rows], (16, columns, inner), dtype=jnp.bfloat16)
+    upper = lax.all_to_all(upper, ("y", "z0"), 0, 0, tiled=True).reshape(8, 2, columns, inner)
     paired = lax.ppermute(lower_panels, "zh", SWAP)
-    lower = kernel(copies, [zh], [lower_panels, paired], (8, 2, 64, inner), dtype=jnp.bfloat16)
-    lower = lax.all_to_all(lower.reshape(8, 128, inner), "x", 0, 0, tiled=True)
+    lower = kernel(copies, [zh], [lower_panels, paired], (8, 2, 2, 32, inner), dtype=jnp.bfloat16)
+    lower = lax.all_to_all(lower.reshape(16, 64, inner), ("x", "z0"), 0, 0, tiled=True).reshape(8, 2, 64, inner)
 
     near = lax.ppermute(slab_cols, "z0", SWAP)
     far = lax.ppermute(slab_cols, "z1", SWAP)
@@ -103,12 +124,13 @@
     other = lax.ppermute(own, "c", SWAP)
 
     def partial_value(parity):
-        return kernel(product, [parity], [upper, lower], (4, 256, 128))
+        return kernel(product, [parity], [upper, lower], (4, 8, 16, 128))
 
     received = lax.ppermute(partial_value(1 - core), "c", SWAP)
-    kept = kernel(add, [], [received, partial_value(core)], (4, 256, 128))
+    kept = kernel(add, [], [received, partial_value(core)], (4, 8, 16, 128))
 
-    pieces = lax.all_to_all(kept.reshape(32, columns, -1), ("z1", "z0", "y"), 0, 0, tiled=True)
+    pieces = lax.all_to_all(kept.reshape(32, 16, 128), ("z1", "z0", "y"), 0, 0, tiled=True)
+    pieces = pieces.reshape(2, 2, 8, 16, 128)
 
     at = kernel(places, [owner, core], [pivots.reshape(-1, 128)], (2, 8, 128), dtype=jnp.int32)
     permuted = kernel(permute, [], [at, own, other], (columns, row_block))

time: 104 us -> 101 us (0.971)
  the two profiles are of different devices: /device:TPU:1 before, /device:TPU:16 now
where the time goes in v8:
time: 101 us; the launch traced here: 100 us
  starting transfers between devices  58 us (57%)
  waiting for transfers between devices  34.4 us (34%)
  Pallas kernels  6.85 us (7%)
    all_to_all x1, starting transfers between devices, shards(): lax.all_to_all(upper, ('y', 'z0'), 0, 0, tiled=True)  16.4 us
    all_to_all x1, waiting for transfers between devices, shards(): lax.all_to_all(lower.reshape(16, 64, inner), ('x', 'z0'), 0, 0, tiled=True)  12.3 us
    all_to_all x1, waiting for transfers between devices, shards(): lax.all_to_all(kept.reshape(32, 16, 128), ('z1', 'z0', 'y'), 0, 0, tiled=...  10.2 us
    all_to_all x1, starting transfers between devices, shards(): lax.all_to_all(kept.reshape(32, 16, 128), ('z1', 'z0', 'y'), 0, 0, tiled=...  9.41 us
    ppermute x1, starting transfers between devices, shards(): paired = lax.ppermute(lower_panels, 'zh', SWAP)  7.99 us
    all_to_all x1, starting transfers between devices, shards(): lax.all_to_all(lower.reshape(16, 64, inner), ('x', 'z0'), 0, 0, tiled=True)  7.87 us
    ppermute x1, waiting for transfers between devices, shards(): far = lax.ppermute(slab_cols, 'z1', SWAP)  7.24 us
    pallas_call x9, Pallas kernels, kernel(): pl.pallas_call(body, out_shape=pltpu.VMEM(out, dtype) if vmem_out else ja...  6.85 us
  transfers between devices with their start and end apart: 9, of which 5 were waited for; matrix products, arithmetic and copies ran while one was open for 0% of the time, Pallas kernels for 5%

profile of v8, /device:TPU:16, one launch (start us, length us, event | category | flops | bytes accessed | tf_op | source)
XLA Modules:
  0.0 100.1 jit_solution(11113232774529799348)
XLA Ops:
  0.0 0.7 copy-done.3
  0.7 0.7 shard_map.46
  1.5 16.4 %all-to-all-start = ((bf16[16,32,256]{2,1,0:T(8,128)(2,1)}), bf16[16,32,256]{2,1,0:T(8,128)(2,1)S(1)}, u32[]{:S(2)}, u32[]{:S(2)}) async-start(bf16[16,32,256]{2,1,0:T(8,128)(2,1)} %shard_map.46), calls=%async_computation | async-start | bytes 524288 | tf_op jit(solution)/shard_map/all_to_all | solution.py:115
  17.9 8.0 %collective-permute-start = (bf16[64,256]{1,0:T(8,128)(2,1)S(1)}, bf16[64,256]{1,0:T(8,128)(2,1)S(1)}, u32[]{:S(2)}, u32[]{:S(2)}) collective-permute-start(bf16[64,256]{1,0:T(8,128)(2,1)S(1)} %copy-done.2), channel_id=1, source_target_pairs={{0,8},{8,0},{1,9},{9,1},{2,10},{10,2},{3,11},{11,3},{4,12},{12,4},... | collective-permute-start | bytes 98312 | tf_op jit(solution)/shard_map/ppermute | solution.py:116
  25.9 1.9 %collective-permute-done.other_ref = bf16[64,256]{1,0:T(8,128)(2,1)S(1)} collective-permute-done((bf16[64,256]{1,0:T(8,128)(2,1)S(1)}, bf16[64,256]{1,0:T(8,128)(2,1)S(1)}, u32[]{:S(2)}, u32[]{:S(2)}) %collective-permute-start) | collective-permute-done | bytes 32800 | tf_op jit(solution)/shard_map/ppermute | solution.py:116
  27.8 0.8 shard_map.47
  28.6 0.0 all-to-all-done
  28.6 7.9 %all-to-all-start.1 = ((bf16[16,64,256]{2,1,0:T(8,128)(2,1)}), bf16[16,64,256]{2,1,0:T(8,128)(2,1)S(1)}, u32[]{:S(2)}, u32[]{:S(2)}) async-start(bf16[16,64,256]{2,1,0:T(8,128)(2,1)} %bitcast.3), calls=%async_computation.1 | async-start | bytes 1048576 | tf_op jit(solution)/shard_map/all_to_all | solution.py:118
  36.5 3.8 %collective-permute-start.2 = (f32[32,1024]{1,0:T(8,128)S(1)}, f32[32,1024]{1,0:T(8,128)S(1)}, u32[]{:S(2)}, u32[]{:S(2)}) collective-permute-start(f32[32,1024]{1,0:T(8,128)S(1)} %copy-done), channel_id=1, source_target_pairs={{0,2},{2,0},{1,3},{3,1},{4,6},{6,4},{5,7},{7,5},{8,10},{10,8},{9,1... | collective-permute-start | bytes 393224 | tf_op jit(solution)/shard_map/ppermute | solution.py:120
  40.3 12.3 %all-to-all-done.1 = bf16[16,64,256]{2,1,0:T(8,128)(2,1)S(1)} async-done(((bf16[16,64,256]{2,1,0:T(8,128)(2,1)}), bf16[16,64,256]{2,1,0:T(8,128)(2,1)S(1)}, u32[]{:S(2)}, u32[]{:S(2)}) %all-to-all-start.1) | async-done | bytes 524320 | tf_op jit(solution)/shard_map/all_to_all | solution.py:118
  52.7 0.5 shard_map.48
  53.1 1.9 %collective-permute-start.1 = (f32[4,8,16,128]{3,2,1,0:T(8,128)S(1)}, f32[4,8,16,128]{3,2,1,0:T(8,128)S(1)}, u32[]{:S(2)}, u32[]{:S(2)}) collective-permute-start(f32[4,8,16,128]{3,2,1,0:T(8,128)S(1)} %shard_map.48), channel_id=1, source_target_pairs={{0,1},{1,0},{2,3},{3,2},{4,5},{5,4},{6,7},{7,6},{8,9},{9,8},{10,11... | collective-permute-start | bytes 786440 | tf_op jit(solution)/shard_map/ppermute | solution.py:129
  55.1 6.6 %collective-permute-start.3 = (f32[32,1024]{1,0:T(8,128)S(1)}, f32[32,1024]{1,0:T(8,128)S(1)}, u32[]{:S(2)}, u32[]{:S(2)}) collective-permute-start(f32[32,1024]{1,0:T(8,128)S(1)} %copy-done), channel_id=1, source_target_pairs={{0,4},{4,0},{1,5},{5,1},{2,6},{6,2},{3,7},{7,3},{8,12},{12,8},{9,1... | collective-permute-start | bytes 393224 | tf_op jit(solution)/shard_map/ppermute | solution.py:121
  61.7 0.0 collective-permute-done.2.near_ref
  61.7 1.9 %collective-permute-start.4 = (f32[32,1024]{1,0:T(8,128)S(1)}, f32[32,1024]{1,0:T(8,128)S(1)}, u32[]{:S(2)}, u32[]{:S(2)}) collective-permute-start(f32[32,1024]{1,0:T(8,128)S(1)} %collective-permute-done.2.near_ref), channel_id=1, source_target_pairs={{0,4},{4,0},{1,5},{5,1},{2,6},{6,2},{3,7},{7,3},{8,12},{12,8},{9,1... | collective-permute-start | bytes 393224 | tf_op jit(solution)/shard_map/ppermute | solution.py:122
  63.6 7.2 %collective-permute-done.3.far_ref = f32[32,1024]{1,0:T(8,128)S(1)} collective-permute-done((f32[32,1024]{1,0:T(8,128)S(1)}, f32[32,1024]{1,0:T(8,128)S(1)}, u32[]{:S(2)}, u32[]{:S(2)}) %collective-permute-start.3) | collective-permute-done | bytes 131104 | tf_op jit(solution)/shard_map/ppermute | solution.py:121
  70.8 2.8 %collective-permute-done.4.far_near_ref = f32[32,1024]{1,0:T(8,128)S(1)} collective-permute-done((f32[32,1024]{1,0:T(8,128)S(1)}, f32[32,1024]{1,0:T(8,128)S(1)}, u32[]{:S(2)}, u32[]{:S(2)}) %collective-permute-start.4) | collective-permute-done | bytes 131104 | tf_op jit(solution)/shard_map/ppermute | solution.py:122
  73.7 2.0 %collective-permute-start.5 = (f32[4,32,1024]{2,1,0:T(8,128)S(1)}, f32[4,32,1024]{2,1,0:T(8,128)S(1)}, u32[]{:S(2)}, u32[]{:S(2)}) collective-permute-start(f32[4,32,1024]{2,1,0:T(8,128)S(1)} %shard_map.52.own_ref), channel_id=1, source_target_pairs={{0,1},{1,0},{2,3},{3,2},{4,5},{5,4},{6,7},{7,6},{8,9},{9,8},{10,11... | collective-permute-start | bytes 1572872 | tf_op jit(solution)/shard_map/ppermute | solution.py:124
  75.7 0.5 shard_map.49.right_ref
  76.2 0.7 shard_map.50
  76.9 9.4 %all-to-all-start.2 = ((f32[32,16,128]{2,1,0:T(8,128)}), f32[32,16,128]{2,1,0:T(8,128)S(1)}, u32[]{:S(2)}, u32[]{:S(2)}) async-start(f32[32,16,128]{2,1,0:T(8,128)} %bitcast.5), calls=%async_computation.2 | async-start | bytes 524288 | tf_op jit(solution)/shard_map/all_to_all | solution.py:132
  86.4 2.7 %shard_map.53.permuted_ref = f32[32,1024]{1,0:T(8,128)S(1)} custom-call(s32[2,8,128]{2,1,0:T(8,128)S(1)} %shard_map.51.places_ref, f32[4,32,1024]{2,1,0:T(8,128)S(1)} %shard_map.52.own_ref, f32[4,32,1024]{2,1,0:T(8,128)S(1)} %collective-permute-done.5.other_ref), custom_call_target="tpu_custom_call" | custom-call | tf_op jit(solution)/shard_map/pallas_call | solution.py:19
  89.1 10.2 %all-to-all-done.2 = f32[32,16,128]{2,1,0:T(8,128)S(1)} async-done(((f32[32,16,128]{2,1,0:T(8,128)}), f32[32,16,128]{2,1,0:T(8,128)S(1)}, u32[]{:S(2)}, u32[]{:S(2)}) %all-to-all-start.2) | async-done | bytes 262176 | tf_op jit(solution)/shard_map/all_to_all | solution.py:132
  99.3 0.8 shard_map.54
  (11 shorter events, 0.1 us)
Async XLA Ops:
  0.0 0.7 copy-start.3
  1.4 16.4 %copy-start.2 = (bf16[64,256]{1,0:T(8,128)(2,1)S(1)}, bf16[64,256]{1,0:T(8,128)(2,1)}, u32[]{:S(2)}) copy-start(bf16[64,256]{1,0:T(8,128)(2,1)} %own_ref.2) | copy-start | bytes 98308
  1.5 27.1 %all-to-all-start = ((bf16[16,32,256]{2,1,0:T(8,128)(2,1)}), bf16[16,32,256]{2,1,0:T(8,128)(2,1)S(1)}, u32[]{:S(2)}, u32[]{:S(2)}) async-start(bf16[16,32,256]{2,1,0:T(8,128)(2,1)} %shard_map.46), calls=%async_computation | async-start | bytes 524288 | tf_op jit(solution)/shard_map/all_to_all | solution.py:115
  17.9 9.9 %collective-permute-start = (bf16[64,256]{1,0:T(8,128)(2,1)S(1)}, bf16[64,256]{1,0:T(8,128)(2,1)S(1)}, u32[]{:S(2)}, u32[]{:S(2)}) collective-permute-start(bf16[64,256]{1,0:T(8,128)(2,1)S(1)} %copy-done.2), channel_id=1, source_target_pairs={{0,8},{8,0},{1,9},{9,1},{2,10},{10,2},{3,11},{11,3},{4,12},{12,4},... | collective-permute-start | bytes 98312 | tf_op jit(solution)/shard_map/ppermute | solution.py:116
  28.6 7.9 %copy-start = (f32[32,1024]{1,0:T(8,128)S(1)}, f32[32,1024]{1,0:T(8,128)}, u32[]{:S(2)}) copy-start(f32[32,1024]{1,0:T(8,128)} %own_ref.3) | copy-start | bytes 393220
  28.6 24.0 %all-to-all-start.1 = ((bf16[16,64,256]{2,1,0:T(8,128)(2,1)}), bf16[16,64,256]{2,1,0:T(8,128)(2,1)S(1)}, u32[]{:S(2)}, u32[]{:S(2)}) async-start(bf16[16,64,256]{2,1,0:T(8,128)(2,1)} %bitcast.3), calls=%async_computation.1 | async-start | bytes 1048576 | tf_op jit(solution)/shard_map/all_to_all | solution.py:118
  36.5 25.2 %collective-permute-start.2 = (f32[32,1024]{1,0:T(8,128)S(1)}, f32[32,1024]{1,0:T(8,128)S(1)}, u32[]{:S(2)}, u32[]{:S(2)}) collective-permute-start(f32[32,1024]{1,0:T(8,128)S(1)} %copy-done), channel_id=1, source_target_pairs={{0,2},{2,0},{1,3},{3,1},{4,6},{6,4},{5,7},{7,5},{8,10},{10,8},{9,1... | collective-permute-start | bytes 393224 | tf_op jit(solution)/shard_map/ppermute | solution.py:120
  53.1 23.1 %collective-permute-start.1 = (f32[4,8,16,128]{3,2,1,0:T(8,128)S(1)}, f32[4,8,16,128]{3,2,1,0:T(8,128)S(1)}, u32[]{:S(2)}, u32[]{:S(2)}) collective-permute-start(f32[4,8,16,128]{3,2,1,0:T(8,128)S(1)} %shard_map.48), channel_id=1, source_target_pairs={{0,1},{1,0},{2,3},{3,2},{4,5},{5,4},{6,7},{7,6},{8,9},{9,8},{10,11... | collective-permute-start | bytes 786440 | tf_op jit(solution)/shard_map/ppermute | solution.py:129
  55.1 15.8 %collective-permute-start.3 = (f32[32,1024]{1,0:T(8,128)S(1)}, f32[32,1024]{1,0:T(8,128)S(1)}, u32[]{:S(2)}, u32[]{:S(2)}) collective-permute-start(f32[32,1024]{1,0:T(8,128)S(1)} %copy-done), channel_id=1, source_target_pairs={{0,4},{4,0},{1,5},{5,1},{2,6},{6,2},{3,7},{7,3},{8,12},{12,8},{9,1... | collective-permute-start | bytes 393224 | tf_op jit(solution)/shard_map/ppermute | solution.py:121
  61.7 12.0 %collective-permute-start.4 = (f32[32,1024]{1,0:T(8,128)S(1)}, f32[32,1024]{1,0:T(8,128)S(1)}, u32[]{:S(2)}, u32[]{:S(2)}) collective-permute-start(f32[32,1024]{1,0:T(8,128)S(1)} %collective-permute-done.2.near_ref), channel_id=1, source_target_pairs={{0,4},{4,0},{1,5},{5,1},{2,6},{6,2},{3,7},{7,3},{8,12},{12,8},{9,1... | collective-permute-start | bytes 393224 | tf_op jit(solution)/shard_map/ppermute | solution.py:122
  73.7 12.7 %collective-permute-start.5 = (f32[4,32,1024]{2,1,0:T(8,128)S(1)}, f32[4,32,1024]{2,1,0:T(8,128)S(1)}, u32[]{:S(2)}, u32[]{:S(2)}) collective-permute-start(f32[4,32,1024]{2,1,0:T(8,128)S(1)} %shard_map.52.own_ref), channel_id=1, source_target_pairs={{0,1},{1,0},{2,3},{3,2},{4,5},{5,4},{6,7},{7,6},{8,9},{9,8},{10,11... | collective-permute-start | bytes 1572872 | tf_op jit(solution)/shard_map/ppermute | solution.py:124
  76.9 9.4 %copy-start.1 = (s32[8192]{0:T(1024)S(1)}, s32[8192]{0:T(1024)}, u32[]{:S(2)}) copy-start(s32[8192]{0:T(1024)} %param.5) | copy-start | bytes 98308
  76.9 22.4 %all-to-all-start.2 = ((f32[32,16,128]{2,1,0:T(8,128)}), f32[32,16,128]{2,1,0:T(8,128)S(1)}, u32[]{:S(2)}, u32[]{:S(2)}) async-start(f32[32,16,128]{2,1,0:T(8,128)} %bitcast.5), calls=%async_computation.2 | async-start | bytes 524288 | tf_op jit(solution)/shard_map/all_to_all | solution.py:132

commit v9 on v8

--- a/solution.py
+++ b/solution.py
@@ -34,7 +34,7 @@
 
 
 def repeat(block_ref, out_ref):
-    for y in range(16):
+    for y in range(8):
         out_ref[y] = block_ref[...]
 
 
@@ -46,18 +46,19 @@
     out_ref[2 * (1 - z1) + 1 - z0] = far_near_ref[...]
 
 
-def product(parity_ref, upper_ref, lower_ref, out_ref):
+def product(parity_ref, z0_ref, upper_ref, swapped_ref, lower_ref, out_ref):
+    parity, z0 = parity_ref[0], z0_ref[0]
     for z in range(4):
         halves = []
         for half in range(2):
             dots = [
                 lax.dot_general(
-                    upper_ref[:, z0, half * 16 : half * 16 + 16, :].reshape(128, 256),
-                    lower_ref[2 * z + parity_ref[0], z0],
+                    ref[:, half * 16 : half * 16 + 16, :].reshape(128, 256),
+                    lower_ref[2 * z + parity, index],
                     (((1,), (1,)), ((), ())),
                     preferred_element_type=jnp.float32,
                 )
-                for z0 in range(2)
+                for ref, index in ((upper_ref, z0), (swapped_ref, 1 - z0))
             ]
             halves.append(dots[0] + dots[1])
         out_ref[z] = jnp.concatenate(halves, axis=1).reshape(8, 16, 128)
@@ -111,8 +112,9 @@
     columns, row_block = slab_cols.shape
     inner = upper_rows.shape[1]
 
-    upper = kernel(repeat, [], [upper_rows], (16, columns, inner), dtype=jnp.bfloat16)
-    upper = lax.all_to_all(upper, ("y", "z0"), 0, 0, tiled=True).reshape(8, 2, columns, inner)
+    upper = kernel(repeat, [], [upper_rows], (8, columns, inner), dtype=jnp.bfloat16)
+    upper = lax.all_to_all(upper, "y", 0, 0, tiled=True)
+    swapped = lax.ppermute(upper, "z0", SWAP)
     paired = lax.ppermute(lower_panels, "zh", SWAP)
     lower = kernel(copies, [zh], [lower_panels, paired], (8, 2, 2, 32, inner), dtype=jnp.bfloat16)
     lower = lax.all_to_all(lower.reshape(16, 64, inner), ("x", "z0"), 0, 0, tiled=True).reshape(8, 2, 64, inner)
@@ -124,7 +126,7 @@
     other = lax.ppermute(own, "c", SWAP)
 
     def partial_value(parity):
-        return kernel(product, [parity], [upper, lower], (4, 8, 16, 128))
+        return kernel(product, [parity, z0], [upper, swapped, lower], (4, 8, 16, 128))
 
     received = lax.ppermute(partial_value(1 - core), "c", SWAP)
     kept = kernel(add, [], [received, partial_value(core)], (4, 8, 16, 128))

time: 101 us -> 99.7 us (0.987)
  starting transfers between devices: 58 us -> 56.8 us
    all_to_all x1, waiting for transfers between devices: 12.3 us -> 6.78 us  [shards(): lax.all_to_all(lower.reshape(16, 64, inner), ('x', 'z0'), 0, 0, tiled=True)]
    ppermute x0 -> x1, starting transfers between devices: none -> 3.82 us  [shards(): swapped = lax.ppermute(upper, 'z0', SWAP)]
    ppermute x0 -> x1, waiting for transfers between devices: none -> 3.45 us  [shards(): swapped = lax.ppermute(upper, 'z0', SWAP)]
    ppermute x1, starting transfers between devices: 3.83 us -> 2.02 us  [shards(): near = lax.ppermute(slab_cols, 'z0', SWAP)]
    ppermute x1, starting transfers between devices: 7.99 us -> 6.2 us  [shards(): paired = lax.ppermute(lower_panels, 'zh', SWAP)]
    ppermute x1, waiting for transfers between devices: 1.89 us -> 3.49 us  [shards(): paired = lax.ppermute(lower_panels, 'zh', SWAP)]
  transfers between devices with their start and end apart: 9 -> 10, of which waited for: 5 -> 6; matrix products, arithmetic and copies ran while one was open for 0% -> 0% of each run, Pallas kernels for 5% -> 5%
where the time goes in v9:
time: 99.7 us; the launch traced here: 99 us
  starting transfers between devices  56.8 us (57%)
  waiting for transfers between devices  34.5 us (35%)
  Pallas kernels  6.79 us (7%)
    all_to_all x1, starting transfers between devices, shards(): upper = lax.all_to_all(upper, 'y', 0, 0, tiled=True)  16.4 us
    all_to_all x1, waiting for transfers between devices, shards(): lax.all_to_all(kept.reshape(32, 16, 128), ('z1', 'z0', 'y'), 0, 0, tiled=...  10.2 us
    all_to_all x1, starting transfers between devices, shards(): lax.all_to_all(kept.reshape(32, 16, 128), ('z1', 'z0', 'y'), 0, 0, tiled=...  9.48 us
    ppermute x1, waiting for transfers between devices, shards(): far = lax.ppermute(slab_cols, 'z1', SWAP)  7.78 us
    all_to_all x1, starting transfers between devices, shards(): lax.all_to_all(lower.reshape(16, 64, inner), ('x', 'z0'), 0, 0, tiled=True)  7.2 us
    pallas_call x9, Pallas kernels, kernel(): pl.pallas_call(body, out_shape=pltpu.VMEM(out, dtype) if vmem_out else ja...  6.79 us
    all_to_all x1, waiting for transfers between devices, shards(): lax.all_to_all(lower.reshape(16, 64, inner), ('x', 'z0'), 0, 0, tiled=True)  6.78 us
    ppermute x1, starting transfers between devices, shards(): paired = lax.ppermute(lower_panels, 'zh', SWAP)  6.2 us
  transfers between devices with their start and end apart: 10, of which 6 were waited for; matrix products, arithmetic and copies ran while one was open for 0% of the time, Pallas kernels for 5%

profile of v9, /device:TPU:16, one launch (start us, length us, event | category | flops | bytes accessed | tf_op | source)
XLA Modules:
  0.0 99.0 jit_solution(7479500592267115911)
XLA Ops:
  0.0 0.7 copy-done.3
  0.7 0.7 shard_map.46
  1.4 16.4 %all-to-all-start = ((bf16[8,32,256]{2,1,0:T(8,128)(2,1)}), bf16[8,32,256]{2,1,0:T(8,128)(2,1)S(1)}, u32[]{:S(2)}, u32[]{:S(2)}) async-start(bf16[8,32,256]{2,1,0:T(8,128)(2,1)} %shard_map.46), calls=%async_computation | async-start | bytes 262144 | tf_op jit(solution)/shard_map/all_to_all | solution.py:116
  17.8 6.2 %collective-permute-start.1 = (bf16[64,256]{1,0:T(8,128)(2,1)S(1)}, bf16[64,256]{1,0:T(8,128)(2,1)S(1)}, u32[]{:S(2)}, u32[]{:S(2)}) collective-permute-start(bf16[64,256]{1,0:T(8,128)(2,1)S(1)} %copy-done.2), channel_id=1, source_target_pairs={{0,8},{8,0},{1,9},{9,1},{2,10},{10,2},{3,11},{11,3},{4,12},{12,4},... | collective-permute-start | bytes 98312 | tf_op jit(solution)/shard_map/ppermute | solution.py:118
  24.0 3.5 %collective-permute-done.1.other_ref = bf16[64,256]{1,0:T(8,128)(2,1)S(1)} collective-permute-done((bf16[64,256]{1,0:T(8,128)(2,1)S(1)}, bf16[64,256]{1,0:T(8,128)(2,1)S(1)}, u32[]{:S(2)}, u32[]{:S(2)}) %collective-permute-start.1) | collective-permute-done | bytes 32800 | tf_op jit(solution)/shard_map/ppermute | solution.py:118
  27.5 0.8 shard_map.47
  28.3 7.2 %all-to-all-start.1 = ((bf16[16,64,256]{2,1,0:T(8,128)(2,1)}), bf16[16,64,256]{2,1,0:T(8,128)(2,1)S(1)}, u32[]{:S(2)}, u32[]{:S(2)}) async-start(bf16[16,64,256]{2,1,0:T(8,128)(2,1)} %bitcast.3), calls=%async_computation.1 | async-start | bytes 1048576 | tf_op jit(solution)/shard_map/all_to_all | solution.py:120
  35.5 3.8 %collective-permute-start = (bf16[8,32,256]{2,1,0:T(8,128)(2,1)S(1)}, bf16[8,32,256]{2,1,0:T(8,128)(2,1)S(1)}, u32[]{:S(2)}, u32[]{:S(2)}) collective-permute-start(bf16[8,32,256]{2,1,0:T(8,128)(2,1)S(1)} %all-to-all-done.upper_ref), channel_id=1, source_target_pairs={{0,2},{2,0},{1,3},{3,1},{4,6},{6,4},{5,7},{7,5},{8,10},{10,8},{9,1... | collective-permute-start | bytes 393224 | tf_op jit(solution)/shard_map/ppermute | solution.py:117
  39.3 2.0 %collective-permute-start.3 = (f32[32,1024]{1,0:T(8,128)S(1)}, f32[32,1024]{1,0:T(8,128)S(1)}, u32[]{:S(2)}, u32[]{:S(2)}) collective-permute-start(f32[32,1024]{1,0:T(8,128)S(1)} %copy-done), channel_id=1, source_target_pairs={{0,2},{2,0},{1,3},{3,1},{4,6},{6,4},{5,7},{7,5},{8,10},{10,8},{9,1... | collective-permute-start | bytes 393224 | tf_op jit(solution)/shard_map/ppermute | solution.py:122
  41.4 3.4 %collective-permute-done.swapped_ref = bf16[8,32,256]{2,1,0:T(8,128)(2,1)S(1)} collective-permute-done((bf16[8,32,256]{2,1,0:T(8,128)(2,1)S(1)}, bf16[8,32,256]{2,1,0:T(8,128)(2,1)S(1)}, u32[]{:S(2)}, u32[]{:S(2)}) %collective-permute-start) | collective-permute-done | bytes 131104 | tf_op jit(solution)/shard_map/ppermute | solution.py:117
  44.8 6.8 %all-to-all-done.1 = bf16[16,64,256]{2,1,0:T(8,128)(2,1)S(1)} async-done(((bf16[16,64,256]{2,1,0:T(8,128)(2,1)}), bf16[16,64,256]{2,1,0:T(8,128)(2,1)S(1)}, u32[]{:S(2)}, u32[]{:S(2)}) %all-to-all-start.1) | async-done | bytes 524320 | tf_op jit(solution)/shard_map/all_to_all | solution.py:120
  51.6 0.5 shard_map.48
  52.1 1.9 %collective-permute-start.2 = (f32[4,8,16,128]{3,2,1,0:T(8,128)S(1)}, f32[4,8,16,128]{3,2,1,0:T(8,128)S(1)}, u32[]{:S(2)}, u32[]{:S(2)}) collective-permute-start(f32[4,8,16,128]{3,2,1,0:T(8,128)S(1)} %shard_map.48), channel_id=1, source_target_pairs={{0,1},{1,0},{2,3},{3,2},{4,5},{5,4},{6,7},{7,6},{8,9},{9,8},{10,11... | collective-permute-start | bytes 786440 | tf_op jit(solution)/shard_map/ppermute | solution.py:131
  54.0 5.9 %collective-permute-start.4 = (f32[32,1024]{1,0:T(8,128)S(1)}, f32[32,1024]{1,0:T(8,128)S(1)}, u32[]{:S(2)}, u32[]{:S(2)}) collective-permute-start(f32[32,1024]{1,0:T(8,128)S(1)} %copy-done), channel_id=1, source_target_pairs={{0,4},{4,0},{1,5},{5,1},{2,6},{6,2},{3,7},{7,3},{8,12},{12,8},{9,1... | collective-permute-start | bytes 393224 | tf_op jit(solution)/shard_map/ppermute | solution.py:123
  59.9 1.9 %collective-permute-start.5 = (f32[32,1024]{1,0:T(8,128)S(1)}, f32[32,1024]{1,0:T(8,128)S(1)}, u32[]{:S(2)}, u32[]{:S(2)}) collective-permute-start(f32[32,1024]{1,0:T(8,128)S(1)} %collective-permute-done.3.near_ref), channel_id=1, source_target_pairs={{0,4},{4,0},{1,5},{5,1},{2,6},{6,2},{3,7},{7,3},{8,12},{12,8},{9,1... | collective-permute-start | bytes 393224 | tf_op jit(solution)/shard_map/ppermute | solution.py:124
  61.8 7.8 %collective-permute-done.4.far_ref = f32[32,1024]{1,0:T(8,128)S(1)} collective-permute-done((f32[32,1024]{1,0:T(8,128)S(1)}, f32[32,1024]{1,0:T(8,128)S(1)}, u32[]{:S(2)}, u32[]{:S(2)}) %collective-permute-start.4) | collective-permute-done | bytes 131104 | tf_op jit(solution)/shard_map/ppermute | solution.py:123
  69.6 2.8 %collective-permute-done.5.far_near_ref = f32[32,1024]{1,0:T(8,128)S(1)} collective-permute-done((f32[32,1024]{1,0:T(8,128)S(1)}, f32[32,1024]{1,0:T(8,128)S(1)}, u32[]{:S(2)}, u32[]{:S(2)}) %collective-permute-start.5) | collective-permute-done | bytes 131104 | tf_op jit(solution)/shard_map/ppermute | solution.py:124
  72.5 2.0 %collective-permute-start.6 = (f32[4,32,1024]{2,1,0:T(8,128)S(1)}, f32[4,32,1024]{2,1,0:T(8,128)S(1)}, u32[]{:S(2)}, u32[]{:S(2)}) collective-permute-start(f32[4,32,1024]{2,1,0:T(8,128)S(1)} %shard_map.52.own_ref), channel_id=1, source_target_pairs={{0,1},{1,0},{2,3},{3,2},{4,5},{5,4},{6,7},{7,6},{8,9},{9,8},{10,11... | collective-permute-start | bytes 1572872 | tf_op jit(solution)/shard_map/ppermute | solution.py:126
  74.5 0.5 shard_map.49.right_ref
  75.0 0.7 shard_map.50
  75.7 9.5 %all-to-all-start.2 = ((f32[32,16,128]{2,1,0:T(8,128)}), f32[32,16,128]{2,1,0:T(8,128)S(1)}, u32[]{:S(2)}, u32[]{:S(2)}) async-start(f32[32,16,128]{2,1,0:T(8,128)} %bitcast.5), calls=%async_computation.2 | async-start | bytes 524288 | tf_op jit(solution)/shard_map/all_to_all | solution.py:134
  85.2 2.7 %shard_map.53.permuted_ref = f32[32,1024]{1,0:T(8,128)S(1)} custom-call(s32[2,8,128]{2,1,0:T(8,128)S(1)} %shard_map.51.places_ref, f32[4,32,1024]{2,1,0:T(8,128)S(1)} %shard_map.52.own_ref, f32[4,32,1024]{2,1,0:T(8,128)S(1)} %collective-permute-done.6.other_ref), custom_call_target="tpu_custom_call" | custom-call | tf_op jit(solution)/shard_map/pallas_call | solution.py:19
  88.0 10.2 %all-to-all-done.2 = f32[32,16,128]{2,1,0:T(8,128)S(1)} async-done(((f32[32,16,128]{2,1,0:T(8,128)}), f32[32,16,128]{2,1,0:T(8,128)S(1)}, u32[]{:S(2)}, u32[]{:S(2)}) %all-to-all-start.2) | async-done | bytes 262176 | tf_op jit(solution)/shard_map/all_to_all | solution.py:134
  98.1 0.8 shard_map.54
  (13 shorter events, 0.1 us)
Async XLA Ops:
  0.0 0.7 copy-start.3
  1.4 16.4 %copy-start.2 = (bf16[64,256]{1,0:T(8,128)(2,1)S(1)}, bf16[64,256]{1,0:T(8,128)(2,1)}, u32[]{:S(2)}) copy-start(bf16[64,256]{1,0:T(8,128)(2,1)} %own_ref.2) | copy-start | bytes 98308
  1.4 26.9 %all-to-all-start = ((bf16[8,32,256]{2,1,0:T(8,128)(2,1)}), bf16[8,32,256]{2,1,0:T(8,128)(2,1)S(1)}, u32[]{:S(2)}, u32[]{:S(2)}) async-start(bf16[8,32,256]{2,1,0:T(8,128)(2,1)} %shard_map.46), calls=%async_computation | async-start | bytes 262144 | tf_op jit(solution)/shard_map/all_to_all | solution.py:116
  17.8 9.7 %collective-permute-start.1 = (bf16[64,256]{1,0:T(8,128)(2,1)S(1)}, bf16[64,256]{1,0:T(8,128)(2,1)S(1)}, u32[]{:S(2)}, u32[]{:S(2)}) collective-permute-start(bf16[64,256]{1,0:T(8,128)(2,1)S(1)} %copy-done.2), channel_id=1, source_target_pairs={{0,8},{8,0},{1,9},{9,1},{2,10},{10,2},{3,11},{11,3},{4,12},{12,4},... | collective-permute-start | bytes 98312 | tf_op jit(solution)/shard_map/ppermute | solution.py:118
  28.3 11.0 %copy-start = (f32[32,1024]{1,0:T(8,128)S(1)}, f32[32,1024]{1,0:T(8,128)}, u32[]{:S(2)}) copy-start(f32[32,1024]{1,0:T(8,128)} %own_ref.3) | copy-start | bytes 393220
  28.3 23.3 %all-to-all-start.1 = ((bf16[16,64,256]{2,1,0:T(8,128)(2,1)}), bf16[16,64,256]{2,1,0:T(8,128)(2,1)S(1)}, u32[]{:S(2)}, u32[]{:S(2)}) async-start(bf16[16,64,256]{2,1,0:T(8,128)(2,1)} %bitcast.3), calls=%async_computation.1 | async-start | bytes 1048576 | tf_op jit(solution)/shard_map/all_to_all | solution.py:120
  35.5 9.3 %collective-permute-start = (bf16[8,32,256]{2,1,0:T(8,128)(2,1)S(1)}, bf16[8,32,256]{2,1,0:T(8,128)(2,1)S(1)}, u32[]{:S(2)}, u32[]{:S(2)}) collective-permute-start(bf16[8,32,256]{2,1,0:T(8,128)(2,1)S(1)} %all-to-all-done.upper_ref), channel_id=1, source_target_pairs={{0,2},{2,0},{1,3},{3,1},{4,6},{6,4},{5,7},{7,5},{8,10},{10,8},{9,1... | collective-permute-start | bytes 393224 | tf_op jit(solution)/shard_map/ppermute | solution.py:117
  39.3 20.6 %collective-permute-start.3 = (f32[32,1024]{1,0:T(8,128)S(1)}, f32[32,1024]{1,0:T(8,128)S(1)}, u32[]{:S(2)}, u32[]{:S(2)}) collective-permute-start(f32[32,1024]{1,0:T(8,128)S(1)} %copy-done), channel_id=1, source_target_pairs={{0,2},{2,0},{1,3},{3,1},{4,6},{6,4},{5,7},{7,5},{8,10},{10,8},{9,1... | collective-permute-start | bytes 393224 | tf_op jit(solution)/shard_map/ppermute | solution.py:122
  52.1 22.9 %collective-permute-start.2 = (f32[4,8,16,128]{3,2,1,0:T(8,128)S(1)}, f32[4,8,16,128]{3,2,1,0:T(8,128)S(1)}, u32[]{:S(2)}, u32[]{:S(2)}) collective-permute-start(f32[4,8,16,128]{3,2,1,0:T(8,128)S(1)} %shard_map.48), channel_id=1, source_target_pairs={{0,1},{1,0},{2,3},{3,2},{4,5},{5,4},{6,7},{7,6},{8,9},{9,8},{10,11... | collective-permute-start | bytes 786440 | tf_op jit(solution)/shard_map/ppermute | solution.py:131
  54.0 15.6 %collective-permute-start.4 = (f32[32,1024]{1,0:T(8,128)S(1)}, f32[32,1024]{1,0:T(8,128)S(1)}, u32[]{:S(2)}, u32[]{:S(2)}) collective-permute-start(f32[32,1024]{1,0:T(8,128)S(1)} %copy-done), channel_id=1, source_target_pairs={{0,4},{4,0},{1,5},{5,1},{2,6},{6,2},{3,7},{7,3},{8,12},{12,8},{9,1... | collective-permute-start | bytes 393224 | tf_op jit(solution)/shard_map/ppermute | solution.py:123
  59.9 12.5 %collective-permute-start.5 = (f32[32,1024]{1,0:T(8,128)S(1)}, f32[32,1024]{1,0:T(8,128)S(1)}, u32[]{:S(2)}, u32[]{:S(2)}) collective-permute-start(f32[32,1024]{1,0:T(8,128)S(1)} %collective-permute-done.3.near_ref), channel_id=1, source_target_pairs={{0,4},{4,0},{1,5},{5,1},{2,6},{6,2},{3,7},{7,3},{8,12},{12,8},{9,1... | collective-permute-start | bytes 393224 | tf_op jit(solution)/shard_map/ppermute | solution.py:124
  72.5 12.8 %collective-permute-start.6 = (f32[4,32,1024]{2,1,0:T(8,128)S(1)}, f32[4,32,1024]{2,1,0:T(8,128)S(1)}, u32[]{:S(2)}, u32[]{:S(2)}) collective-permute-start(f32[4,32,1024]{2,1,0:T(8,128)S(1)} %shard_map.52.own_ref), channel_id=1, source_target_pairs={{0,1},{1,0},{2,3},{3,2},{4,5},{5,4},{6,7},{7,6},{8,9},{9,8},{10,11... | collective-permute-start | bytes 1572872 | tf_op jit(solution)/shard_map/ppermute | solution.py:126
  75.7 9.5 %copy-start.1 = (s32[8192]{0:T(1024)S(1)}, s32[8192]{0:T(1024)}, u32[]{:S(2)}) copy-start(s32[8192]{0:T(1024)} %param.5) | copy-start | bytes 98308
  75.7 22.4 %all-to-all-start.2 = ((f32[32,16,128]{2,1,0:T(8,128)}), f32[32,16,128]{2,1,0:T(8,128)S(1)}, u32[]{:S(2)}, u32[]{:S(2)}) async-start(f32[32,16,128]{2,1,0:T(8,128)} %bitcast.5), calls=%async_computation.2 | async-start | bytes 524288 | tf_op jit(solution)/shard_map/all_to_all | solution.py:134

commit v10 on v9

--- a/solution.py
+++ b/solution.py
@@ -14,8 +14,9 @@
 SMEM = pl.BlockSpec(memory_space=pltpu.SMEM)
 
 
-def kernel(body, scalars, arrays, out, dtype=jnp.float32, vmem_out=True):
-    arrays = [pltpu.with_memory_space_constraint(a, pltpu.VMEM) for a in arrays]
+def kernel(body, scalars, arrays, out, dtype=jnp.float32, vmem_in=True, vmem_out=True):
+    if vmem_in:
+        arrays = [pltpu.with_memory_space_constraint(a, pltpu.VMEM) for a in arrays]
     return pl.pallas_call(
         body,
         out_shape=pltpu.VMEM(out, dtype) if vmem_out else jax.ShapeDtypeStruct(out, dtype),
@@ -112,7 +113,7 @@
     columns, row_block = slab_cols.shape
     inner = upper_rows.shape[1]
 
-    upper = kernel(repeat, [], [upper_rows], (8, columns, inner), dtype=jnp.bfloat16)
+    upper = kernel(repeat, [], [upper_rows], (8, columns, inner), dtype=jnp.bfloat16, vmem_in=False)
     upper = lax.all_to_all(upper, "y", 0, 0, tiled=True)
     swapped = lax.ppermute(upper, "z0", SWAP)
     paired = lax.ppermute(lower_panels, "zh", SWAP)

time: 99.7 us -> 99.7 us (level)
  no operation moved by 1% of the time
where the time goes in v10:
time: 99.7 us; the launch traced here: 99 us
  starting transfers between devices  56.8 us (57%)
  waiting for transfers between devices  34.5 us (35%)
  Pallas kernels  7.5 us (8%)
    all_to_all x1, starting transfers between devices, shards(): upper = lax.all_to_all(upper, 'y', 0, 0, tiled=True)  16.4 us
    all_to_all x1, waiting for transfers between devices, shards(): lax.all_to_all(kept.reshape(32, 16, 128), ('z1', 'z0', 'y'), 0, 0, tiled=...  10.2 us
    all_to_all x1, starting transfers between devices, shards(): lax.all_to_all(kept.reshape(32, 16, 128), ('z1', 'z0', 'y'), 0, 0, tiled=...  9.47 us
    ppermute x1, waiting for transfers between devices, shards(): far = lax.ppermute(slab_cols, 'z1', SWAP)  7.79 us
    pallas_call x9, Pallas kernels, kernel(): pl.pallas_call(body, out_shape=pltpu.VMEM(out, dtype) if vmem_out else ja...  7.5 us
    all_to_all x1, starting transfers between devices, shards(): lax.all_to_all(lower.reshape(16, 64, inner), ('x', 'z0'), 0, 0, tiled=True)  7.2 us
    all_to_all x1, waiting for transfers between devices, shards(): lax.all_to_all(lower.reshape(16, 64, inner), ('x', 'z0'), 0, 0, tiled=True)  6.78 us
    ppermute x1, starting transfers between devices, shards(): paired = lax.ppermute(lower_panels, 'zh', SWAP)  6.2 us
  transfers between devices with their start and end apart: 10, of which 6 were waited for; matrix products, arithmetic and copies ran while one was open for 0% of the time, Pallas kernels for 5%

profile of v10, /device:TPU:16, one launch (start us, length us, event | category | flops | bytes accessed | tf_op | source)
XLA Modules:
  0.0 99.0 jit_solution(7392261411005773734)
XLA Ops:
  0.0 1.4 %shard_map.46 = bf16[8,32,256]{2,1,0:T(8,128)(2,1)} custom-call(bf16[32,256]{1,0:T(8,128)(2,1)} %block_ref.1), custom_call_target="tpu_custom_call" | custom-call | tf_op jit(solution)/shard_map/pallas_call | solution.py:20
  1.4 16.4 %all-to-all-start = ((bf16[8,32,256]{2,1,0:T(8,128)(2,1)}), bf16[8,32,256]{2,1,0:T(8,128)(2,1)S(1)}, u32[]{:S(2)}, u32[]{:S(2)}) async-start(bf16[8,32,256]{2,1,0:T(8,128)(2,1)} %shard_map.46), calls=%async_computation | async-start | bytes 262144 | tf_op jit(solution)/shard_map/all_to_all | solution.py:117
  17.7 6.2 %collective-permute-start.1 = (bf16[64,256]{1,0:T(8,128)(2,1)S(1)}, bf16[64,256]{1,0:T(8,128)(2,1)S(1)}, u32[]{:S(2)}, u32[]{:S(2)}) collective-permute-start(bf16[64,256]{1,0:T(8,128)(2,1)S(1)} %copy-done.2), channel_id=1, source_target_pairs={{0,8},{8,0},{1,9},{9,1},{2,10},{10,2},{3,11},{11,3},{4,12},{12,4},... | collective-permute-start | bytes 98312 | tf_op jit(solution)/shard_map/ppermute | solution.py:119
  24.0 3.5 %collective-permute-done.1.other_ref = bf16[64,256]{1,0:T(8,128)(2,1)S(1)} collective-permute-done((bf16[64,256]{1,0:T(8,128)(2,1)S(1)}, bf16[64,256]{1,0:T(8,128)(2,1)S(1)}, u32[]{:S(2)}, u32[]{:S(2)}) %collective-permute-start.1) | collective-permute-done | bytes 32800 | tf_op jit(solution)/shard_map/ppermute | solution.py:119
  27.5 0.8 shard_map.47
  28.3 0.0 all-to-all-done.upper_ref
  28.3 7.2 %all-to-all-start.1 = ((bf16[16,64,256]{2,1,0:T(8,128)(2,1)}), bf16[16,64,256]{2,1,0:T(8,128)(2,1)S(1)}, u32[]{:S(2)}, u32[]{:S(2)}) async-start(bf16[16,64,256]{2,1,0:T(8,128)(2,1)} %bitcast.3), calls=%async_computation.1 | async-start | bytes 1048576 | tf_op jit(solution)/shard_map/all_to_all | solution.py:121
  35.5 3.8 %collective-permute-start = (bf16[8,32,256]{2,1,0:T(8,128)(2,1)S(1)}, bf16[8,32,256]{2,1,0:T(8,128)(2,1)S(1)}, u32[]{:S(2)}, u32[]{:S(2)}) collective-permute-start(bf16[8,32,256]{2,1,0:T(8,128)(2,1)S(1)} %all-to-all-done.upper_ref), channel_id=1, source_target_pairs={{0,2},{2,0},{1,3},{3,1},{4,6},{6,4},{5,7},{7,5},{8,10},{10,8},{9,1... | collective-permute-start | bytes 393224 | tf_op jit(solution)/shard_map/ppermute | solution.py:118
  39.3 2.0 %collective-permute-start.3 = (f32[32,1024]{1,0:T(8,128)S(1)}, f32[32,1024]{1,0:T(8,128)S(1)}, u32[]{:S(2)}, u32[]{:S(2)}) collective-permute-start(f32[32,1024]{1,0:T(8,128)S(1)} %copy-done), channel_id=1, source_target_pairs={{0,2},{2,0},{1,3},{3,1},{4,6},{6,4},{5,7},{7,5},{8,10},{10,8},{9,1... | collective-permute-start | bytes 393224 | tf_op jit(solution)/shard_map/ppermute | solution.py:123
  41.4 3.4 %collective-permute-done.swapped_ref = bf16[8,32,256]{2,1,0:T(8,128)(2,1)S(1)} collective-permute-done((bf16[8,32,256]{2,1,0:T(8,128)(2,1)S(1)}, bf16[8,32,256]{2,1,0:T(8,128)(2,1)S(1)}, u32[]{:S(2)}, u32[]{:S(2)}) %collective-permute-start) | collective-permute-done | bytes 131104 | tf_op jit(solution)/shard_map/ppermute | solution.py:118
  44.8 6.8 %all-to-all-done.1 = bf16[16,64,256]{2,1,0:T(8,128)(2,1)S(1)} async-done(((bf16[16,64,256]{2,1,0:T(8,128)(2,1)}), bf16[16,64,256]{2,1,0:T(8,128)(2,1)S(1)}, u32[]{:S(2)}, u32[]{:S(2)}) %all-to-all-start.1) | async-done | bytes 524320 | tf_op jit(solution)/shard_map/all_to_all | solution.py:121
  51.6 0.5 shard_map.48
  52.1 1.9 %collective-permute-start.2 = (f32[4,8,16,128]{3,2,1,0:T(8,128)S(1)}, f32[4,8,16,128]{3,2,1,0:T(8,128)S(1)}, u32[]{:S(2)}, u32[]{:S(2)}) collective-permute-start(f32[4,8,16,128]{3,2,1,0:T(8,128)S(1)} %shard_map.48), channel_id=1, source_target_pairs={{0,1},{1,0},{2,3},{3,2},{4,5},{5,4},{6,7},{7,6},{8,9},{9,8},{10,11... | collective-permute-start | bytes 786440 | tf_op jit(solution)/shard_map/ppermute | solution.py:132
  54.0 5.9 %collective-permute-start.4 = (f32[32,1024]{1,0:T(8,128)S(1)}, f32[32,1024]{1,0:T(8,128)S(1)}, u32[]{:S(2)}, u32[]{:S(2)}) collective-permute-start(f32[32,1024]{1,0:T(8,128)S(1)} %copy-done), channel_id=1, source_target_pairs={{0,4},{4,0},{1,5},{5,1},{2,6},{6,2},{3,7},{7,3},{8,12},{12,8},{9,1... | collective-permute-start | bytes 393224 | tf_op jit(solution)/shard_map/ppermute | solution.py:124
  59.9 1.9 %collective-permute-start.5 = (f32[32,1024]{1,0:T(8,128)S(1)}, f32[32,1024]{1,0:T(8,128)S(1)}, u32[]{:S(2)}, u32[]{:S(2)}) collective-permute-start(f32[32,1024]{1,0:T(8,128)S(1)} %collective-permute-done.3.near_ref), channel_id=1, source_target_pairs={{0,4},{4,0},{1,5},{5,1},{2,6},{6,2},{3,7},{7,3},{8,12},{12,8},{9,1... | collective-permute-start | bytes 393224 | tf_op jit(solution)/shard_map/ppermute | solution.py:125
  61.8 7.8 %collective-permute-done.4.far_ref = f32[32,1024]{1,0:T(8,128)S(1)} collective-permute-done((f32[32,1024]{1,0:T(8,128)S(1)}, f32[32,1024]{1,0:T(8,128)S(1)}, u32[]{:S(2)}, u32[]{:S(2)}) %collective-permute-start.4) | collective-permute-done | bytes 131104 | tf_op jit(solution)/shard_map/ppermute | solution.py:124
  69.6 2.8 %collective-permute-done.5.far_near_ref = f32[32,1024]{1,0:T(8,128)S(1)} collective-permute-done((f32[32,1024]{1,0:T(8,128)S(1)}, f32[32,1024]{1,0:T(8,128)S(1)}, u32[]{:S(2)}, u32[]{:S(2)}) %collective-permute-start.5) | collective-permute-done | bytes 131104 | tf_op jit(solution)/shard_map/ppermute | solution.py:125
  72.5 2.0 %collective-permute-start.6 = (f32[4,32,1024]{2,1,0:T(8,128)S(1)}, f32[4,32,1024]{2,1,0:T(8,128)S(1)}, u32[]{:S(2)}, u32[]{:S(2)}) collective-permute-start(f32[4,32,1024]{2,1,0:T(8,128)S(1)} %shard_map.52.own_ref), channel_id=1, source_target_pairs={{0,1},{1,0},{2,3},{3,2},{4,5},{5,4},{6,7},{7,6},{8,9},{9,8},{10,11... | collective-permute-start | bytes 1572872 | tf_op jit(solution)/shard_map/ppermute | solution.py:127
  74.5 0.5 shard_map.49.right_ref
  75.0 0.7 shard_map.50
  75.7 9.5 %all-to-all-start.2 = ((f32[32,16,128]{2,1,0:T(8,128)}), f32[32,16,128]{2,1,0:T(8,128)S(1)}, u32[]{:S(2)}, u32[]{:S(2)}) async-start(f32[32,16,128]{2,1,0:T(8,128)} %bitcast.5), calls=%async_computation.2 | async-start | bytes 524288 | tf_op jit(solution)/shard_map/all_to_all | solution.py:135
  85.2 2.7 %shard_map.53.permuted_ref = f32[32,1024]{1,0:T(8,128)S(1)} custom-call(s32[2,8,128]{2,1,0:T(8,128)S(1)} %shard_map.51.places_ref, f32[4,32,1024]{2,1,0:T(8,128)S(1)} %shard_map.52.own_ref, f32[4,32,1024]{2,1,0:T(8,128)S(1)} %collective-permute-done.6.other_ref), custom_call_target="tpu_custom_call" | custom-call | tf_op jit(solution)/shard_map/pallas_call | solution.py:20
  88.0 10.2 %all-to-all-done.2 = f32[32,16,128]{2,1,0:T(8,128)S(1)} async-done(((f32[32,16,128]{2,1,0:T(8,128)}), f32[32,16,128]{2,1,0:T(8,128)S(1)}, u32[]{:S(2)}, u32[]{:S(2)}) %all-to-all-start.2) | async-done | bytes 262176 | tf_op jit(solution)/shard_map/all_to_all | solution.py:135
  98.1 0.8 shard_map.54
  (11 shorter events, 0.1 us)
Async XLA Ops:
  1.4 16.4 %copy-start.2 = (bf16[64,256]{1,0:T(8,128)(2,1)S(1)}, bf16[64,256]{1,0:T(8,128)(2,1)}, u32[]{:S(2)}) copy-start(bf16[64,256]{1,0:T(8,128)(2,1)} %own_ref.2) | copy-start | bytes 98308
  1.4 26.9 %all-to-all-start = ((bf16[8,32,256]{2,1,0:T(8,128)(2,1)}), bf16[8,32,256]{2,1,0:T(8,128)(2,1)S(1)}, u32[]{:S(2)}, u32[]{:S(2)}) async-start(bf16[8,32,256]{2,1,0:T(8,128)(2,1)} %shard_map.46), calls=%async_computation | async-start | bytes 262144 | tf_op jit(solution)/shard_map/all_to_all | solution.py:117
  17.7 9.7 %collective-permute-start.1 = (bf16[64,256]{1,0:T(8,128)(2,1)S(1)}, bf16[64,256]{1,0:T(8,128)(2,1)S(1)}, u32[]{:S(2)}, u32[]{:S(2)}) collective-permute-start(bf16[64,256]{1,0:T(8,128)(2,1)S(1)} %copy-done.2), channel_id=1, source_target_pairs={{0,8},{8,0},{1,9},{9,1},{2,10},{10,2},{3,11},{11,3},{4,12},{12,4},... | collective-permute-start | bytes 98312 | tf_op jit(solution)/shard_map/ppermute | solution.py:119
  28.3 11.0 %copy-start = (f32[32,1024]{1,0:T(8,128)S(1)}, f32[32,1024]{1,0:T(8,128)}, u32[]{:S(2)}) copy-start(f32[32,1024]{1,0:T(8,128)} %own_ref.3) | copy-start | bytes 393220
  28.3 23.3 %all-to-all-start.1 = ((bf16[16,64,256]{2,1,0:T(8,128)(2,1)}), bf16[16,64,256]{2,1,0:T(8,128)(2,1)S(1)}, u32[]{:S(2)}, u32[]{:S(2)}) async-start(bf16[16,64,256]{2,1,0:T(8,128)(2,1)} %bitcast.3), calls=%async_computation.1 | async-start | bytes 1048576 | tf_op jit(solution)/shard_map/all_to_all | solution.py:121
  35.5 9.3 %collective-permute-start = (bf16[8,32,256]{2,1,0:T(8,128)(2,1)S(1)}, bf16[8,32,256]{2,1,0:T(8,128)(2,1)S(1)}, u32[]{:S(2)}, u32[]{:S(2)}) collective-permute-start(bf16[8,32,256]{2,1,0:T(8,128)(2,1)S(1)} %all-to-all-done.upper_ref), channel_id=1, source_target_pairs={{0,2},{2,0},{1,3},{3,1},{4,6},{6,4},{5,7},{7,5},{8,10},{10,8},{9,1... | collective-permute-start | bytes 393224 | tf_op jit(solution)/shard_map/ppermute | solution.py:118
  39.3 20.6 %collective-permute-start.3 = (f32[32,1024]{1,0:T(8,128)S(1)}, f32[32,1024]{1,0:T(8,128)S(1)}, u32[]{:S(2)}, u32[]{:S(2)}) collective-permute-start(f32[32,1024]{1,0:T(8,128)S(1)} %copy-done), channel_id=1, source_target_pairs={{0,2},{2,0},{1,3},{3,1},{4,6},{6,4},{5,7},{7,5},{8,10},{10,8},{9,1... | collective-permute-start | bytes 393224 | tf_op jit(solution)/shard_map/ppermute | solution.py:123
  52.1 22.9 %collective-permute-start.2 = (f32[4,8,16,128]{3,2,1,0:T(8,128)S(1)}, f32[4,8,16,128]{3,2,1,0:T(8,128)S(1)}, u32[]{:S(2)}, u32[]{:S(2)}) collective-permute-start(f32[4,8,16,128]{3,2,1,0:T(8,128)S(1)} %shard_map.48), channel_id=1, source_target_pairs={{0,1},{1,0},{2,3},{3,2},{4,5},{5,4},{6,7},{7,6},{8,9},{9,8},{10,11... | collective-permute-start | bytes 786440 | tf_op jit(solution)/shard_map/ppermute | solution.py:132
  54.0 15.6 %collective-permute-start.4 = (f32[32,1024]{1,0:T(8,128)S(1)}, f32[32,1024]{1,0:T(8,128)S(1)}, u32[]{:S(2)}, u32[]{:S(2)}) collective-permute-start(f32[32,1024]{1,0:T(8,128)S(1)} %copy-done), channel_id=1, source_target_pairs={{0,4},{4,0},{1,5},{5,1},{2,6},{6,2},{3,7},{7,3},{8,12},{12,8},{9,1... | collective-permute-start | bytes 393224 | tf_op jit(solution)/shard_map/ppermute | solution.py:124
  59.9 12.5 %collective-permute-start.5 = (f32[32,1024]{1,0:T(8,128)S(1)}, f32[32,1024]{1,0:T(8,128)S(1)}, u32[]{:S(2)}, u32[]{:S(2)}) collective-permute-start(f32[32,1024]{1,0:T(8,128)S(1)} %collective-permute-done.3.near_ref), channel_id=1, source_target_pairs={{0,4},{4,0},{1,5},{5,1},{2,6},{6,2},{3,7},{7,3},{8,12},{12,8},{9,1... | collective-permute-start | bytes 393224 | tf_op jit(solution)/shard_map/ppermute | solution.py:125
  72.5 12.8 %collective-permute-start.6 = (f32[4,32,1024]{2,1,0:T(8,128)S(1)}, f32[4,32,1024]{2,1,0:T(8,128)S(1)}, u32[]{:S(2)}, u32[]{:S(2)}) collective-permute-start(f32[4,32,1024]{2,1,0:T(8,128)S(1)} %shard_map.52.own_ref), channel_id=1, source_target_pairs={{0,1},{1,0},{2,3},{3,2},{4,5},{5,4},{6,7},{7,6},{8,9},{9,8},{10,11... | collective-permute-start | bytes 1572872 | tf_op jit(solution)/shard_map/ppermute | solution.py:127
  75.7 9.5 %copy-start.1 = (s32[8192]{0:T(1024)S(1)}, s32[8192]{0:T(1024)}, u32[]{:S(2)}) copy-start(s32[8192]{0:T(1024)} %param.5) | copy-start | bytes 98308
  75.7 22.4 %all-to-all-start.2 = ((f32[32,16,128]{2,1,0:T(8,128)}), f32[32,16,128]{2,1,0:T(8,128)S(1)}, u32[]{:S(2)}, u32[]{:S(2)}) async-start(f32[32,16,128]{2,1,0:T(8,128)} %bitcast.5), calls=%async_computation.2 | async-start | bytes 524288 | tf_op jit(solution)/shard_map/all_to_all | solution.py:135

commit v11 on v10

--- a/solution.py
+++ b/solution.py
@@ -25,13 +25,19 @@
     )(*scalars, *arrays)
 
 
-def copies(zh_ref, own_ref, other_ref, out_ref):
-    zh = zh_ref[0]
+def halves(zh_ref, z0_ref, own_ref, other_ref, out_ref):
+    zh, rows = zh_ref[0], pl.ds(pl.multiple_of((1 - z0_ref[0]) * 32, 32), 32)
+    out_ref[zh] = own_ref[rows, :]
+    out_ref[1 - zh] = other_ref[rows, :]
+
+
+def copies(zh_ref, z0_ref, own_ref, other_ref, got_ref, out_ref):
+    zh, z0 = zh_ref[0], z0_ref[0]
+    rows = pl.ds(pl.multiple_of(z0 * 32, 32), 32)
     for x in range(8):
-        for z0 in range(2):
-            rows = slice(z0 * 32, z0 * 32 + 32)
-            out_ref[x, z0, zh] = own_ref[rows]
-            out_ref[x, z0, 1 - zh] = other_ref[rows]
+        out_ref[x, z0, zh] = own_ref[rows, :]
+        out_ref[x, z0, 1 - zh] = other_ref[rows, :]
+        out_ref[x, 1 - z0] = got_ref[...]
 
 
 def repeat(block_ref, out_ref):
@@ -117,8 +123,10 @@
     upper = lax.all_to_all(upper, "y", 0, 0, tiled=True)
     swapped = lax.ppermute(upper, "z0", SWAP)
     paired = lax.ppermute(lower_panels, "zh", SWAP)
-    lower = kernel(copies, [zh], [lower_panels, paired], (8, 2, 2, 32, inner), dtype=jnp.bfloat16)
-    lower = lax.all_to_all(lower.reshape(16, 64, inner), ("x", "z0"), 0, 0, tiled=True).reshape(8, 2, 64, inner)
+    given = kernel(halves, [zh, z0], [lower_panels, paired], (2, 32, inner), dtype=jnp.bfloat16)
+    got = lax.ppermute(given, "z0", SWAP)
+    lower = kernel(copies, [zh, z0], [lower_panels, paired, got], (8, 2, 2, 32, inner), dtype=jnp.bfloat16)
+    lower = lax.all_to_all(lower.reshape(8, 128, inner), "x", 0, 0, tiled=True).reshape(8, 2, 64, inner)
 
     near = lax.ppermute(slab_cols, "z0", SWAP)
     far = lax.ppermute(slab_cols, "z1", SWAP)

time: 99.7 us -> 104 us (1.043)
  starting transfers between devices: 56.8 us -> 59.3 us
  waiting for transfers between devices: 34.5 us -> 36.5 us
    ppermute x0 -> x1, waiting for transfers between devices: none -> 3.13 us  [shards(): got = lax.ppermute(given, 'z0', SWAP)]
    ppermute x0 -> x1, starting transfers between devices: none -> 2.66 us  [shards(): got = lax.ppermute(given, 'z0', SWAP)]
    ppermute x1, waiting for transfers between devices: 3.45 us -> 1.86 us  [shards(): swapped = lax.ppermute(upper, 'z0', SWAP)]
    all_to_all x1, starting transfers between devices: 7.2 us -> 5.84 us  [shards(): lax.all_to_all(lower.reshape(8, 128, inner), 'x', 0, 0, tiled=True)]
    all_to_all x1, starting transfers between devices: 9.47 us -> 10.5 us  [shards(): lax.all_to_all(kept.reshape(32, 16, 128), ('z1', 'z0', 'y'), 0, 0, tiled=...]
    pallas_call x9 -> x10, Pallas kernels: 7.5 us -> 7.51 us  [kernel(): pl.pallas_call(body, out_shape=pltpu.VMEM(out, dtype) if vmem_out else ja...]
  transfers between devices with their start and end apart: 10 -> 11, of which waited for: 6 -> 7; matrix products, arithmetic and copies ran while one was open for 0% -> 0% of each run, Pallas kernels for 5% -> 5%
where the time goes in v11:
time: 104 us; the launch traced here: 103 us
  starting transfers between devices  59.3 us (57%)
  waiting for transfers between devices  36.5 us (35%)
  Pallas kernels  7.51 us (7%)
    all_to_all x1, starting transfers between devices, shards(): upper = lax.all_to_all(upper, 'y', 0, 0, tiled=True)  16.4 us
    all_to_all x1, starting transfers between devices, shards(): lax.all_to_all(kept.reshape(32, 16, 128), ('z1', 'z0', 'y'), 0, 0, tiled=...  10.5 us
    all_to_all x1, waiting for transfers between devices, shards(): lax.all_to_all(kept.reshape(32, 16, 128), ('z1', 'z0', 'y'), 0, 0, tiled=...  10.1 us
    ppermute x1, waiting for transfers between devices, shards(): far = lax.ppermute(slab_cols, 'z1', SWAP)  8.01 us
    pallas_call x10, Pallas kernels, kernel(): pl.pallas_call(body, out_shape=pltpu.VMEM(out, dtype) if vmem_out else ja...  7.51 us
    all_to_all x1, waiting for transfers between devices, shards(): lax.all_to_all(lower.reshape(8, 128, inner), 'x', 0, 0, tiled=True)  7.28 us
    ppermute x1, starting transfers between devices, shards(): paired = lax.ppermute(lower_panels, 'zh', SWAP)  6.2 us
    ppermute x1, starting transfers between devices, shards(): far = lax.ppermute(slab_cols, 'z1', SWAP)  6.11 us
  transfers between devices with their start and end apart: 11, of which 7 were waited for; matrix products, arithmetic and copies ran while one was open for 0% of the time, Pallas kernels for 5%

profile of v11, /device:TPU:16, one launch (start us, length us, event | category | flops | bytes accessed | tf_op | source)
XLA Modules:
  0.0 103.5 jit_solution(7549111700130791052)
XLA Ops:
  0.0 1.4 %shard_map.46 = bf16[8,32,256]{2,1,0:T(8,128)(2,1)} custom-call(bf16[32,256]{1,0:T(8,128)(2,1)} %block_ref.1), custom_call_target="tpu_custom_call" | custom-call | tf_op jit(solution)/shard_map/pallas_call | solution.py:20
  1.4 16.4 %all-to-all-start = ((bf16[8,32,256]{2,1,0:T(8,128)(2,1)}), bf16[8,32,256]{2,1,0:T(8,128)(2,1)S(1)}, u32[]{:S(2)}, u32[]{:S(2)}) async-start(bf16[8,32,256]{2,1,0:T(8,128)(2,1)} %shard_map.46), calls=%async_computation | async-start | bytes 262144 | tf_op jit(solution)/shard_map/all_to_all | solution.py:123
  17.7 6.2 %collective-permute-start.1 = (bf16[64,256]{1,0:T(8,128)(2,1)S(1)}, bf16[64,256]{1,0:T(8,128)(2,1)S(1)}, u32[]{:S(2)}, u32[]{:S(2)}) collective-permute-start(bf16[64,256]{1,0:T(8,128)(2,1)S(1)} %copy-done.1), channel_id=1, source_target_pairs={{0,8},{8,0},{1,9},{9,1},{2,10},{10,2},{3,11},{11,3},{4,12},{12,4},... | collective-permute-start | bytes 98312 | tf_op jit(solution)/shard_map/ppermute | solution.py:125
  24.0 3.5 %collective-permute-done.1.other_ref = bf16[64,256]{1,0:T(8,128)(2,1)S(1)} collective-permute-done((bf16[64,256]{1,0:T(8,128)(2,1)S(1)}, bf16[64,256]{1,0:T(8,128)(2,1)S(1)}, u32[]{:S(2)}, u32[]{:S(2)}) %collective-permute-start.1) | collective-permute-done | bytes 32800 | tf_op jit(solution)/shard_map/ppermute | solution.py:125
  27.5 2.7 %collective-permute-start.2 = (bf16[2,32,256]{2,1,0:T(8,128)(2,1)S(1)}, bf16[2,32,256]{2,1,0:T(8,128)(2,1)S(1)}, u32[]{:S(2)}, u32[]{:S(2)}) collective-permute-start(bf16[2,32,256]{2,1,0:T(8,128)(2,1)S(1)} %shard_map.47), channel_id=1, source_target_pairs={{0,2},{2,0},{1,3},{3,1},{4,6},{6,4},{5,7},{7,5},{8,10},{10,8},{9,1... | collective-permute-start | bytes 98312 | tf_op jit(solution)/shard_map/ppermute | solution.py:127
  30.1 3.1 %collective-permute-done.2.got_ref = bf16[2,32,256]{2,1,0:T(8,128)(2,1)S(1)} collective-permute-done((bf16[2,32,256]{2,1,0:T(8,128)(2,1)S(1)}, bf16[2,32,256]{2,1,0:T(8,128)(2,1)S(1)}, u32[]{:S(2)}, u32[]{:S(2)}) %collective-permute-start.2) | collective-permute-done | bytes 32800 | tf_op jit(solution)/shard_map/ppermute | solution.py:127
  33.3 0.8 shard_map.48
  34.1 5.8 %all-to-all-start.1 = ((bf16[8,128,256]{2,1,0:T(8,128)(2,1)}), bf16[8,128,256]{2,1,0:T(8,128)(2,1)S(1)}, u32[]{:S(2)}, u32[]{:S(2)}) async-start(bf16[8,128,256]{2,1,0:T(8,128)(2,1)} %bitcast.3), calls=%async_computation.1 | async-start | bytes 1048576 | tf_op jit(solution)/shard_map/all_to_all | solution.py:129
  39.9 3.7 %collective-permute-start = (bf16[8,32,256]{2,1,0:T(8,128)(2,1)S(1)}, bf16[8,32,256]{2,1,0:T(8,128)(2,1)S(1)}, u32[]{:S(2)}, u32[]{:S(2)}) collective-permute-start(bf16[8,32,256]{2,1,0:T(8,128)(2,1)S(1)} %all-to-all-done.upper_ref), channel_id=1, source_target_pairs={{0,2},{2,0},{1,3},{3,1},{4,6},{6,4},{5,7},{7,5},{8,10},{10,8},{9,1... | collective-permute-start | bytes 393224 | tf_op jit(solution)/shard_map/ppermute | solution.py:124
  43.7 2.1 %collective-permute-start.4 = (f32[32,1024]{1,0:T(8,128)S(1)}, f32[32,1024]{1,0:T(8,128)S(1)}, u32[]{:S(2)}, u32[]{:S(2)}) collective-permute-start(f32[32,1024]{1,0:T(8,128)S(1)} %copy-done), channel_id=1, source_target_pairs={{0,2},{2,0},{1,3},{3,1},{4,6},{6,4},{5,7},{7,5},{8,10},{10,8},{9,1... | collective-permute-start | bytes 393224 | tf_op jit(solution)/shard_map/ppermute | solution.py:131
  45.8 1.9 %collective-permute-done.swapped_ref = bf16[8,32,256]{2,1,0:T(8,128)(2,1)S(1)} collective-permute-done((bf16[8,32,256]{2,1,0:T(8,128)(2,1)S(1)}, bf16[8,32,256]{2,1,0:T(8,128)(2,1)S(1)}, u32[]{:S(2)}, u32[]{:S(2)}) %collective-permute-start) | collective-permute-done | bytes 131104 | tf_op jit(solution)/shard_map/ppermute | solution.py:124
  47.7 7.3 %all-to-all-done.1 = bf16[8,128,256]{2,1,0:T(8,128)(2,1)S(1)} async-done(((bf16[8,128,256]{2,1,0:T(8,128)(2,1)}), bf16[8,128,256]{2,1,0:T(8,128)(2,1)S(1)}, u32[]{:S(2)}, u32[]{:S(2)}) %all-to-all-start.1) | async-done | bytes 524320 | tf_op jit(solution)/shard_map/all_to_all | solution.py:129
  55.4 1.9 %collective-permute-start.3 = (f32[4,8,16,128]{3,2,1,0:T(8,128)S(1)}, f32[4,8,16,128]{3,2,1,0:T(8,128)S(1)}, u32[]{:S(2)}, u32[]{:S(2)}) collective-permute-start(f32[4,8,16,128]{3,2,1,0:T(8,128)S(1)} %shard_map.49), channel_id=1, source_target_pairs={{0,1},{1,0},{2,3},{3,2},{4,5},{5,4},{6,7},{7,6},{8,9},{9,8},{10,11... | collective-permute-start | bytes 786440 | tf_op jit(solution)/shard_map/ppermute | solution.py:140
  57.3 6.1 %collective-permute-start.5 = (f32[32,1024]{1,0:T(8,128)S(1)}, f32[32,1024]{1,0:T(8,128)S(1)}, u32[]{:S(2)}, u32[]{:S(2)}) collective-permute-start(f32[32,1024]{1,0:T(8,128)S(1)} %copy-done), channel_id=1, source_target_pairs={{0,4},{4,0},{1,5},{5,1},{2,6},{6,2},{3,7},{7,3},{8,12},{12,8},{9,1... | collective-permute-start | bytes 393224 | tf_op jit(solution)/shard_map/ppermute | solution.py:132
  63.5 1.9 %collective-permute-start.6 = (f32[32,1024]{1,0:T(8,128)S(1)}, f32[32,1024]{1,0:T(8,128)S(1)}, u32[]{:S(2)}, u32[]{:S(2)}) collective-permute-start(f32[32,1024]{1,0:T(8,128)S(1)} %collective-permute-done.4.near_ref), channel_id=1, source_target_pairs={{0,4},{4,0},{1,5},{5,1},{2,6},{6,2},{3,7},{7,3},{8,12},{12,8},{9,1... | collective-permute-start | bytes 393224 | tf_op jit(solution)/shard_map/ppermute | solution.py:133
  65.4 8.0 %collective-permute-done.5.far_ref = f32[32,1024]{1,0:T(8,128)S(1)} collective-permute-done((f32[32,1024]{1,0:T(8,128)S(1)}, f32[32,1024]{1,0:T(8,128)S(1)}, u32[]{:S(2)}, u32[]{:S(2)}) %collective-permute-start.5) | collective-permute-done | bytes 131104 | tf_op jit(solution)/shard_map/ppermute | solution.py:132
  73.4 2.6 %collective-permute-done.6.far_near_ref = f32[32,1024]{1,0:T(8,128)S(1)} collective-permute-done((f32[32,1024]{1,0:T(8,128)S(1)}, f32[32,1024]{1,0:T(8,128)S(1)}, u32[]{:S(2)}, u32[]{:S(2)}) %collective-permute-start.6) | collective-permute-done | bytes 131104 | tf_op jit(solution)/shard_map/ppermute | solution.py:133
  76.1 1.9 %collective-permute-start.7 = (f32[4,32,1024]{2,1,0:T(8,128)S(1)}, f32[4,32,1024]{2,1,0:T(8,128)S(1)}, u32[]{:S(2)}, u32[]{:S(2)}) collective-permute-start(f32[4,32,1024]{2,1,0:T(8,128)S(1)} %shard_map.53.own_ref), channel_id=1, source_target_pairs={{0,1},{1,0},{2,3},{3,2},{4,5},{5,4},{6,7},{7,6},{8,9},{9,8},{10,11... | collective-permute-start | bytes 1572872 | tf_op jit(solution)/shard_map/ppermute | solution.py:135
  78.0 0.5 shard_map.50.right_ref
  78.5 0.7 shard_map.51
  79.2 10.5 %all-to-all-start.2 = ((f32[32,16,128]{2,1,0:T(8,128)}), f32[32,16,128]{2,1,0:T(8,128)S(1)}, u32[]{:S(2)}, u32[]{:S(2)}) async-start(f32[32,16,128]{2,1,0:T(8,128)} %bitcast.5), calls=%async_computation.2 | async-start | bytes 524288 | tf_op jit(solution)/shard_map/all_to_all | solution.py:143
  89.8 2.7 %shard_map.54.permuted_ref = f32[32,1024]{1,0:T(8,128)S(1)} custom-call(s32[2,8,128]{2,1,0:T(8,128)S(1)} %shard_map.52.places_ref, f32[4,32,1024]{2,1,0:T(8,128)S(1)} %shard_map.53.own_ref, f32[4,32,1024]{2,1,0:T(8,128)S(1)} %collective-permute-done.7.other_ref), custom_call_target="tpu_custom_call" | custom-call | tf_op jit(solution)/shard_map/pallas_call | solution.py:20
  92.5 10.1 %all-to-all-done.2 = f32[32,16,128]{2,1,0:T(8,128)S(1)} async-done(((f32[32,16,128]{2,1,0:T(8,128)}), f32[32,16,128]{2,1,0:T(8,128)S(1)}, u32[]{:S(2)}, u32[]{:S(2)}) %all-to-all-start.2) | async-done | bytes 262176 | tf_op jit(solution)/shard_map/all_to_all | solution.py:143
  102.7 0.8 shard_map.55
  (14 shorter events, 0.6 us)
Async XLA Ops:
  1.4 16.4 %copy-start.1 = (bf16[64,256]{1,0:T(8,128)(2,1)S(1)}, bf16[64,256]{1,0:T(8,128)(2,1)}, u32[]{:S(2)}) copy-start(bf16[64,256]{1,0:T(8,128)(2,1)} %own_ref.4) | copy-start | bytes 98308
  1.4 32.7 %all-to-all-start = ((bf16[8,32,256]{2,1,0:T(8,128)(2,1)}), bf16[8,32,256]{2,1,0:T(8,128)(2,1)S(1)}, u32[]{:S(2)}, u32[]{:S(2)}) async-start(bf16[8,32,256]{2,1,0:T(8,128)(2,1)} %shard_map.46), calls=%async_computation | async-start | bytes 262144 | tf_op jit(solution)/shard_map/all_to_all | solution.py:123
  17.7 9.7 %collective-permute-start.1 = (bf16[64,256]{1,0:T(8,128)(2,1)S(1)}, bf16[64,256]{1,0:T(8,128)(2,1)S(1)}, u32[]{:S(2)}, u32[]{:S(2)}) collective-permute-start(bf16[64,256]{1,0:T(8,128)(2,1)S(1)} %copy-done.1), channel_id=1, source_target_pairs={{0,8},{8,0},{1,9},{9,1},{2,10},{10,2},{3,11},{11,3},{4,12},{12,4},... | collective-permute-start | bytes 98312 | tf_op jit(solution)/shard_map/ppermute | solution.py:125
  27.5 5.8 %collective-permute-start.2 = (bf16[2,32,256]{2,1,0:T(8,128)(2,1)S(1)}, bf16[2,32,256]{2,1,0:T(8,128)(2,1)S(1)}, u32[]{:S(2)}, u32[]{:S(2)}) collective-permute-start(bf16[2,32,256]{2,1,0:T(8,128)(2,1)S(1)} %shard_map.47), channel_id=1, source_target_pairs={{0,2},{2,0},{1,3},{3,1},{4,6},{6,4},{5,7},{7,5},{8,10},{10,8},{9,1... | collective-permute-start | bytes 98312 | tf_op jit(solution)/shard_map/ppermute | solution.py:127
  34.1 9.6 %copy-start = (f32[32,1024]{1,0:T(8,128)S(1)}, f32[32,1024]{1,0:T(8,128)}, u32[]{:S(2)}) copy-start(f32[32,1024]{1,0:T(8,128)} %own_ref.5) | copy-start | bytes 393220
  34.1 20.8 %all-to-all-start.1 = ((bf16[8,128,256]{2,1,0:T(8,128)(2,1)}), bf16[8,128,256]{2,1,0:T(8,128)(2,1)S(1)}, u32[]{:S(2)}, u32[]{:S(2)}) async-start(bf16[8,128,256]{2,1,0:T(8,128)(2,1)} %bitcast.3), calls=%async_computation.1 | async-start | bytes 1048576 | tf_op jit(solution)/shard_map/all_to_all | solution.py:129
  39.9 7.7 %collective-permute-start = (bf16[8,32,256]{2,1,0:T(8,128)(2,1)S(1)}, bf16[8,32,256]{2,1,0:T(8,128)(2,1)S(1)}, u32[]{:S(2)}, u32[]{:S(2)}) collective-permute-start(bf16[8,32,256]{2,1,0:T(8,128)(2,1)S(1)} %all-to-all-done.upper_ref), channel_id=1, source_target_pairs={{0,2},{2,0},{1,3},{3,1},{4,6},{6,4},{5,7},{7,5},{8,10},{10,8},{9,1... | collective-permute-start | bytes 393224 | tf_op jit(solution)/shard_map/ppermute | solution.py:124
  43.7 19.8 %collective-permute-start.4 = (f32[32,1024]{1,0:T(8,128)S(1)}, f32[32,1024]{1,0:T(8,128)S(1)}, u32[]{:S(2)}, u32[]{:S(2)}) collective-permute-start(f32[32,1024]{1,0:T(8,128)S(1)} %copy-done), channel_id=1, source_target_pairs={{0,2},{2,0},{1,3},{3,1},{4,6},{6,4},{5,7},{7,5},{8,10},{10,8},{9,1... | collective-permute-start | bytes 393224 | tf_op jit(solution)/shard_map/ppermute | solution.py:131
  55.4 23.1 %collective-permute-start.3 = (f32[4,8,16,128]{3,2,1,0:T(8,128)S(1)}, f32[4,8,16,128]{3,2,1,0:T(8,128)S(1)}, u32[]{:S(2)}, u32[]{:S(2)}) collective-permute-start(f32[4,8,16,128]{3,2,1,0:T(8,128)S(1)} %shard_map.49), channel_id=1, source_target_pairs={{0,1},{1,0},{2,3},{3,2},{4,5},{5,4},{6,7},{7,6},{8,9},{9,8},{10,11... | collective-permute-start | bytes 786440 | tf_op jit(solution)/shard_map/ppermute | solution.py:140
  57.3 16.1 %collective-permute-start.5 = (f32[32,1024]{1,0:T(8,128)S(1)}, f32[32,1024]{1,0:T(8,128)S(1)}, u32[]{:S(2)}, u32[]{:S(2)}) collective-permute-start(f32[32,1024]{1,0:T(8,128)S(1)} %copy-done), channel_id=1, source_target_pairs={{0,4},{4,0},{1,5},{5,1},{2,6},{6,2},{3,7},{7,3},{8,12},{12,8},{9,1... | collective-permute-start | bytes 393224 | tf_op jit(solution)/shard_map/ppermute | solution.py:132
  63.5 12.6 %collective-permute-start.6 = (f32[32,1024]{1,0:T(8,128)S(1)}, f32[32,1024]{1,0:T(8,128)S(1)}, u32[]{:S(2)}, u32[]{:S(2)}) collective-permute-start(f32[32,1024]{1,0:T(8,128)S(1)} %collective-permute-done.4.near_ref), channel_id=1, source_target_pairs={{0,4},{4,0},{1,5},{5,1},{2,6},{6,2},{3,7},{7,3},{8,12},{12,8},{9,1... | collective-permute-start | bytes 393224 | tf_op jit(solution)/shard_map/ppermute | solution.py:133
  76.1 13.7 %collective-permute-start.7 = (f32[4,32,1024]{2,1,0:T(8,128)S(1)}, f32[4,32,1024]{2,1,0:T(8,128)S(1)}, u32[]{:S(2)}, u32[]{:S(2)}) collective-permute-start(f32[4,32,1024]{2,1,0:T(8,128)S(1)} %shard_map.53.own_ref), channel_id=1, source_target_pairs={{0,1},{1,0},{2,3},{3,2},{4,5},{5,4},{6,7},{7,6},{8,9},{9,8},{10,11... | collective-permute-start | bytes 1572872 | tf_op jit(solution)/shard_map/ppermute | solution.py:135
  79.2 10.5 %copy-start.2 = (s32[8192]{0:T(1024)S(1)}, s32[8192]{0:T(1024)}, u32[]{:S(2)}) copy-start(s32[8192]{0:T(1024)} %param.5) | copy-start | bytes 98308
  79.2 23.4 %all-to-all-start.2 = ((f32[32,16,128]{2,1,0:T(8,128)}), f32[32,16,128]{2,1,0:T(8,128)S(1)}, u32[]{:S(2)}, u32[]{:S(2)}) async-start(f32[32,16,128]{2,1,0:T(8,128)} %bitcast.5), calls=%async_computation.2 | async-start | bytes 524288 | tf_op jit(solution)/shard_map/all_to_all | solution.py:143
